TPU v7x, 32 devices: a whole 2x2x4 slice. The times are simulated.
32 devices in a mesh: dp: 8 (over y, x, core), fsdp: 4 (over z).
Axes of the slice: x: 2, y: 2, z: 4, core: 2. Of those that a mesh axis runs over, the one named last changes fastest.
Arguments:
- patches: bfloat16 [2, 2048, 1152], P(None, ('dp', 'fsdp')), may hold values from -6 to 6
- cotangent: bfloat16 [2, 2048, 1152], P(None, ('dp', 'fsdp')), may hold values from -6 to 6
- conditioning: float32 [2, 8, 1152], replicated, may hold values from -6 to 6
- frame_of_slot: int32 [2, 2048], P(None, ('dp', 'fsdp')), may hold values from 0 to 127, as said below
- clip_of_slot: int32 [2, 2048], P(None, ('dp', 'fsdp')), may hold values from 0 to 7, as said below
- w_ada: bfloat16 [1152, 6912], P('dp', 'fsdp'), may hold values from -0.1875 to 0.1875
- b_ada: bfloat16 [6912], P('fsdp'), may hold values from -3 to 3
- w_qkv: bfloat16 [1152, 3456], P('dp', 'fsdp'), may hold values from -0.1875 to 0.1875
- b_qv: bfloat16 [2304], P('fsdp'), may hold values from -2 to 2
- w_proj: bfloat16 [1152, 1152], P('dp', 'fsdp'), may hold values from -1 to 1
- b_proj: bfloat16 [1152], P('fsdp'), may hold values from -2 to 2
- w_fc1: bfloat16 [1152, 4608], P('dp', 'fsdp'), may hold values from -0.1875 to 0.1875
- b_fc1: bfloat16 [4608], P('fsdp'), may hold values from -3 to 3
- w_fc2: bfloat16 [4608, 1152], P('dp', 'fsdp'), may hold values from -0.09375 to 0.09375
- b_fc2: bfloat16 [1152], P('fsdp'), may hold values from -2 to 2
Outputs:
- output: bfloat16 [2, 2048, 1152], P(None, ('dp', 'fsdp'))
- input_grad: bfloat16 [2, 2048, 1152], P(None, ('dp', 'fsdp'))
- cond_grad: float32 [2, 8, 1152], P(None, None, 'fsdp')
- grad_w_ada: float32 [1152, 6912], P('dp', 'fsdp')
- grad_b_ada: float32 [6912], P('fsdp')
- grad_w_qkv: float32 [1152, 3456], P('dp', 'fsdp')
- grad_b_qv: float32 [2304], P('fsdp')
- grad_w_proj: float32 [1152, 1152], P('dp', 'fsdp')
- grad_b_proj: float32 [1152], P('fsdp')
- grad_w_fc1: float32 [1152, 4608], P('dp', 'fsdp')
- grad_b_fc1: float32 [4608], P('fsdp')
- grad_w_fc2: float32 [4608, 1152], P('dp', 'fsdp')
- grad_b_fc2: float32 [1152], P('fsdp')
Inputs may be any that keep to these rules, and one draw needn't show every extreme that they name: `frame_of_slot`: in each micro-batch, each aligned block of 64 slots holds either one frame of 64 patches or four frames of 16 patches one after another; no frame number appears in two blocks. `clip_of_slot`: all slots of one frame name the same clip.
All inputs are finite; a program needn't handle non-finite values.
Results may differ from a plain program's by a relative error of at most 0.018.
Values may be sent and summed in bfloat16 or wider, within the bound.
A program may use at most 256 MiB of HBM per device.

v0:
```python
import math

import jax
import jax.numpy as jnp
from jax import lax
from jax.sharding import PartitionSpec as P

HEAD_DIM = 72


EPS = 1e-06
GELU_C = math.sqrt(2.0 / math.pi)
PRECISE = lax.Precision.HIGHEST
NEG_FILL = -1e30


def layer_norm(values):
    centre = values - jnp.mean(values, axis=-1, keepdims=True)
    return centre * lax.rsqrt(jnp.mean(centre * centre, axis=-1, keepdims=True) + EPS)


def gelu_tanh(hidden):
    return 0.5 * hidden * (1.0 + jnp.tanh(GELU_C * (hidden + 0.044715 * hidden * hidden * hidden)))


def modulate(values, shift_part, scale_part):
    return layer_norm(values) * (1.0 + scale_part) + shift_part


def matmul_plain(left, right):
    return jnp.dot(left, right, preferred_element_type=jnp.float32)


def matmul_right_t(left, right):
    return lax.dot_general(
        left, right, (((1,), (1,)), ((), ())), preferred_element_type=jnp.float32
    )


def matmul_left_t(left, right):
    return lax.dot_general(
        left, right, (((0,), (0,)), ((), ())), preferred_element_type=jnp.float32
    )


def precise_left_t(left, right):
    return lax.dot_general(
        left, right, (((0,), (0,)), ((), ())), precision=PRECISE, preferred_element_type=jnp.float32
    )


def precise_right_t(left, right):
    return lax.dot_general(
        left, right, (((1,), (1,)), ((), ())), precision=PRECISE, preferred_element_type=jnp.float32
    )


def gather_weights(w_qkv, w_proj, w_fc1, w_fc2, b_qv, b_proj, b_fc1, b_fc2):
    inner_parts = (
        lax.all_gather(w_qkv, "fsdp", axis=1, tiled=True),
        lax.all_gather(w_proj, "fsdp", axis=1, tiled=True),
        lax.all_gather(w_fc1, "fsdp", axis=1, tiled=True),
        lax.all_gather(w_fc2, "fsdp", axis=1, tiled=True),
        lax.all_gather(b_qv, "fsdp", axis=0, tiled=True),
        lax.all_gather(b_proj, "fsdp", axis=0, tiled=True),
        lax.all_gather(b_fc1, "fsdp", axis=0, tiled=True),
        lax.all_gather(b_fc2, "fsdp", axis=0, tiled=True),
    )
    whole_rows = (
        lax.all_gather(inner_parts[0], "dp", axis=0, tiled=True),
        lax.all_gather(inner_parts[1], "dp", axis=0, tiled=True),
        lax.all_gather(inner_parts[2], "dp", axis=0, tiled=True),
        lax.all_gather(inner_parts[3], "dp", axis=0, tiled=True),
    )
    return (
        whole_rows[0],
        whole_rows[1],
        whole_rows[2],
        whole_rows[3],
        inner_parts[4],
        inner_parts[5],
        inner_parts[6],
        inner_parts[7],
    )


def reduce_grads(full_w, full_b):
    inner_sums = (
        lax.psum_scatter(
            full_w[0].astype(jnp.bfloat16), "fsdp", scatter_dimension=1, tiled=True
        ).astype(jnp.float32),
        lax.psum_scatter(
            full_w[1].astype(jnp.bfloat16), "fsdp", scatter_dimension=1, tiled=True
        ).astype(jnp.float32),
        lax.psum_scatter(
            full_w[2].astype(jnp.bfloat16), "fsdp", scatter_dimension=1, tiled=True
        ).astype(jnp.float32),
        lax.psum_scatter(
            full_w[3].astype(jnp.bfloat16), "fsdp", scatter_dimension=1, tiled=True
        ).astype(jnp.float32),
        lax.psum_scatter(
            full_b[0].astype(jnp.bfloat16), "fsdp", scatter_dimension=0, tiled=True
        ).astype(jnp.float32),
        lax.psum_scatter(
            full_b[1].astype(jnp.bfloat16), "fsdp", scatter_dimension=0, tiled=True
        ).astype(jnp.float32),
        lax.psum_scatter(
            full_b[2].astype(jnp.bfloat16), "fsdp", scatter_dimension=0, tiled=True
        ).astype(jnp.float32),
        lax.psum_scatter(
            full_b[3].astype(jnp.bfloat16), "fsdp", scatter_dimension=0, tiled=True
        ).astype(jnp.float32),
    )
    outer_sums = (
        lax.psum_scatter(
            inner_sums[0].astype(jnp.bfloat16), "dp", scatter_dimension=0, tiled=True
        ).astype(jnp.float32),
        lax.psum_scatter(
            inner_sums[1].astype(jnp.bfloat16), "dp", scatter_dimension=0, tiled=True
        ).astype(jnp.float32),
        lax.psum_scatter(
            inner_sums[2].astype(jnp.bfloat16), "dp", scatter_dimension=0, tiled=True
        ).astype(jnp.float32),
        lax.psum_scatter(
            inner_sums[3].astype(jnp.bfloat16), "dp", scatter_dimension=0, tiled=True
        ).astype(jnp.float32),
    )
    small_sums = lax.psum((inner_sums[4], inner_sums[5], inner_sums[6], inner_sums[7]), "dp")
    return (tuple(outer_sums), tuple(small_sums))


def modulation_sharded(silu_low, w_ada, b_ada):
    row_width, col_width = w_ada.shape
    row_start = lax.axis_index("dp") * row_width
    col_start = lax.axis_index("fsdp") * col_width
    silu_part = lax.dynamic_slice_in_dim(silu_low, row_start, row_width, 1)
    partial_value = matmul_plain(silu_part, w_ada)
    bias_term = jnp.where(
        lax.axis_index("dp") == 0, b_ada.astype(jnp.float32), jnp.zeros((col_width,), jnp.float32)
    )
    partial_value = partial_value + bias_term[None, :]
    padded = jnp.zeros((silu_low.shape[0], col_width * lax.axis_size("fsdp")), jnp.float32)
    padded = lax.dynamic_update_slice_in_dim(padded, partial_value, col_start, 1)
    return lax.psum(padded, ("dp", "fsdp"))


def ada_grads_sharded(silu_low, cond_rows, d_modulation, w_ada):
    row_width, col_width = w_ada.shape
    row_start = lax.axis_index("dp") * row_width
    col_start = lax.axis_index("fsdp") * col_width
    d_total = lax.psum(d_modulation, ("dp", "fsdp"))
    d_cols = lax.dynamic_slice_in_dim(d_total, col_start, col_width, 1)
    silu_part = lax.dynamic_slice_in_dim(silu_low, row_start, row_width, 1).astype(jnp.float32)
    grad_weight = precise_left_t(silu_part, d_cols)
    grad_bias = jnp.sum(d_cols, axis=0)
    d_silu_part = precise_right_t(d_cols, w_ada.astype(jnp.float32))
    model_width = cond_rows.shape[1]
    padded = jnp.zeros((cond_rows.shape[0], model_width), jnp.float32)
    padded = lax.dynamic_update_slice_in_dim(padded, d_silu_part, row_start, 1)
    d_silu = lax.psum(padded, ("dp", "fsdp"))
    own_width = model_width // lax.axis_size("fsdp")
    own_start = lax.axis_index("fsdp") * own_width
    d_silu_own = lax.dynamic_slice_in_dim(d_silu, own_start, own_width, 1)
    cond_own = lax.dynamic_slice_in_dim(cond_rows, own_start, own_width, 1)
    silu_own, silu_own_back = jax.vjp(jax.nn.silu, cond_own)
    cond_grad = silu_own_back(d_silu_own)[0]
    return (grad_weight, grad_bias, cond_grad)


def head_scores(queries, key_rows, same_frame):
    scores = jnp.einsum(
        "qhd,khd->hqk", queries, key_rows, preferred_element_type=jnp.float32
    ) * HEAD_DIM ** (-0.5)
    return jnp.where(same_frame[None, :, :], scores, NEG_FILL)


def micro_forward(patch_rows, modulation, frame_ids, clip_ids, weights):
    w_qkv, w_proj, w_fc1, w_fc2, b_qv, b_proj, b_fc1, b_fc2 = weights
    row_count, model_width = patch_rows.shape
    head_count = model_width // HEAD_DIM
    clip_hot = (
        clip_ids[:, None] == jnp.arange(modulation.shape[0], dtype=jnp.int32)[None, :]
    ).astype(jnp.float32)
    token_mod = jnp.dot(clip_hot, modulation, precision=PRECISE)
    shift_one, scale_one, gate_one, shift_two, scale_two, gate_two = jnp.split(token_mod, 6, axis=1)
    inputs_float = patch_rows.astype(jnp.float32)
    attn_in, norm_one_back = jax.vjp(modulate, inputs_float, shift_one, scale_one)
    attn_low = attn_in.astype(jnp.bfloat16)
    qkv_bias = jnp.concatenate(
        [b_qv[:model_width], jnp.zeros((model_width,), jnp.bfloat16), b_qv[model_width:]]
    ).astype(jnp.float32)
    qkv_low = (matmul_plain(attn_low, w_qkv) + qkv_bias).astype(jnp.bfloat16)
    queries = qkv_low[:, :model_width].reshape(row_count, head_count, HEAD_DIM)
    key_rows = qkv_low[:, model_width : 2 * model_width].reshape(row_count, head_count, HEAD_DIM)
    value_rows = qkv_low[:, 2 * model_width :].reshape(row_count, head_count, HEAD_DIM)
    same_frame = frame_ids[:, None] == frame_ids[None, :]
    scores = head_scores(queries, key_rows, same_frame)
    row_max = jnp.max(scores, axis=-1, keepdims=True)
    exp_scores = jnp.exp(scores - row_max)
    exp_total = jnp.sum(exp_scores, axis=-1, keepdims=True)
    shares = exp_scores / exp_total
    log_total = row_max + jnp.log(exp_total)
    mixed_low = (
        jnp.einsum(
            "hqk,khd->qhd",
            shares.astype(jnp.bfloat16),
            value_rows,
            preferred_element_type=jnp.float32,
        )
        .reshape(row_count, model_width)
        .astype(jnp.bfloat16)
    )
    attn_out = matmul_plain(mixed_low, w_proj) + b_proj.astype(jnp.float32)
    after_attn = inputs_float + gate_one * attn_out
    mlp_in, norm_two_back = jax.vjp(modulate, after_attn, shift_two, scale_two)
    mlp_low = mlp_in.astype(jnp.bfloat16)
    hidden = matmul_plain(mlp_low, w_fc1) + b_fc1.astype(jnp.float32)
    act_value, gelu_back = jax.vjp(gelu_tanh, hidden)
    act_low = act_value.astype(jnp.bfloat16)
    branch = matmul_plain(act_low, w_fc2) + b_fc2.astype(jnp.float32)
    output = (after_attn + gate_two * branch).astype(jnp.bfloat16)
    saved = (
        clip_hot,
        gate_one,
        gate_two,
        norm_one_back,
        attn_low,
        queries,
        key_rows,
        value_rows,
        same_frame,
        log_total,
        mixed_low,
        attn_out,
        norm_two_back,
        mlp_low,
        gelu_back,
        act_low,
        branch,
    )
    return (output, saved)


def micro_backward(saved, cot_rows, weights):
    w_qkv, w_proj, w_fc1, w_fc2 = (weights[0], weights[1], weights[2], weights[3])
    (
        clip_hot,
        gate_one,
        gate_two,
        norm_one_back,
        attn_low,
        queries,
        key_rows,
        value_rows,
        same_frame,
        log_total,
        mixed_low,
        attn_out,
        norm_two_back,
        mlp_low,
        gelu_back,
        act_low,
        branch,
    ) = saved
    row_count = cot_rows.shape[0]
    model_width = cot_rows.shape[1]
    head_count = model_width // HEAD_DIM
    cot_float = cot_rows.astype(jnp.float32)
    d_branch = (gate_two * cot_float).astype(jnp.bfloat16)
    grad_gate_two = cot_float * branch
    grad_w_fc2 = matmul_left_t(act_low, d_branch)
    grad_b_fc2 = jnp.sum(d_branch.astype(jnp.float32), axis=0)
    d_act = matmul_right_t(d_branch, w_fc2)
    d_hidden = gelu_back(d_act)[0].astype(jnp.bfloat16)
    grad_w_fc1 = matmul_left_t(mlp_low, d_hidden)
    grad_b_fc1 = jnp.sum(d_hidden.astype(jnp.float32), axis=0)
    d_mlp = matmul_right_t(d_hidden, w_fc1)
    d_after, d_shift_two, d_scale_two = norm_two_back(d_mlp)
    d_after = cot_float + d_after
    grad_gate_one = d_after * attn_out
    d_attn = (gate_one * d_after).astype(jnp.bfloat16)
    grad_w_proj = matmul_left_t(mixed_low, d_attn)
    grad_b_proj = jnp.sum(d_attn.astype(jnp.float32), axis=0)
    d_mix = (
        matmul_right_t(d_attn, w_proj).astype(jnp.bfloat16).reshape(row_count, head_count, HEAD_DIM)
    )
    shares_again = jnp.exp(head_scores(queries, key_rows, same_frame) - log_total)
    d_shares = jnp.einsum("qhd,khd->hqk", d_mix, value_rows, preferred_element_type=jnp.float32)
    row_delta = jnp.sum(shares_again * d_shares, axis=-1, keepdims=True)
    d_scores = (shares_again * (d_shares - row_delta)).astype(jnp.bfloat16)
    d_queries = jnp.einsum(
        "hqk,khd->qhd", d_scores, key_rows, preferred_element_type=jnp.float32
    ) * HEAD_DIM ** (-0.5)
    d_keys = jnp.einsum(
        "hqk,qhd->khd", d_scores, queries, preferred_element_type=jnp.float32
    ) * HEAD_DIM ** (-0.5)
    d_values = jnp.einsum(
        "hqk,qhd->khd", shares_again.astype(jnp.bfloat16), d_mix, preferred_element_type=jnp.float32
    )
    d_qkv = jnp.concatenate(
        [
            d_queries.reshape(row_count, model_width),
            d_keys.reshape(row_count, model_width),
            d_values.reshape(row_count, model_width),
        ],
        axis=1,
    ).astype(jnp.bfloat16)
    grad_w_qkv = matmul_left_t(attn_low, d_qkv)
    column_sums = jnp.sum(d_qkv.astype(jnp.float32), axis=0)
    grad_b_qv = jnp.concatenate([column_sums[:model_width], column_sums[2 * model_width :]])
    d_attn_in = matmul_right_t(d_qkv, w_qkv)
    d_inputs, d_shift_one, d_scale_one = norm_one_back(d_attn_in)
    input_grad = (d_after + d_inputs).astype(jnp.bfloat16)
    d_token_mod = jnp.concatenate(
        [d_shift_one, d_scale_one, grad_gate_one, d_shift_two, d_scale_two, grad_gate_two], axis=1
    )
    d_modulation = lax.dot_general(
        clip_hot,
        d_token_mod,
        (((0,), (0,)), ((), ())),
        precision=PRECISE,
        preferred_element_type=jnp.float32,
    )
    grads_w = (grad_w_qkv, grad_w_proj, grad_w_fc1, grad_w_fc2)
    grads_b = (grad_b_qv, grad_b_proj, grad_b_fc1, grad_b_fc2)
    return (input_grad, d_modulation, grads_w, grads_b)


def add_terms(first_terms, second_terms):
    if first_terms is None:
        return tuple(second_terms)
    return tuple(
        (first_item + second_item for first_item, second_item in zip(first_terms, second_terms))
    )


def per_device(
    patches,
    cotangent,
    conditioning,
    frame_of_slot,
    clip_of_slot,
    w_ada,
    b_ada,
    w_qkv,
    b_qv,
    w_proj,
    b_proj,
    w_fc1,
    b_fc1,
    w_fc2,
    b_fc2,
):
    micro_count = patches.shape[0]
    outputs = []
    input_grads = []
    cond_parts = []
    summed_w = None
    summed_b = None
    ada_terms = None
    for micro_index in range(micro_count):
        cond_rows = conditioning[micro_index]
        silu_value, silu_back = jax.vjp(jax.nn.silu, cond_rows)
        silu_low = silu_value.astype(jnp.bfloat16)
        weights = gather_weights(w_qkv, w_proj, w_fc1, w_fc2, b_qv, b_proj, b_fc1, b_fc2)
        modulation = modulation_sharded(silu_low, w_ada, b_ada)
        output, saved = micro_forward(
            patches[micro_index],
            modulation,
            frame_of_slot[micro_index],
            clip_of_slot[micro_index],
            weights,
        )
        input_grad, d_modulation, grads_w, grads_b = micro_backward(
            saved, cotangent[micro_index], weights
        )
        outputs.append(output)
        input_grads.append(input_grad)
        grad_w_ada, grad_b_ada, cond_grad = ada_grads_sharded(
            silu_low, cond_rows, d_modulation, w_ada
        )
        cond_parts.append(cond_grad[None])
        ada_terms = add_terms(ada_terms, (grad_w_ada, grad_b_ada))
        part_w, part_b = reduce_grads(grads_w, grads_b)
        summed_w = add_terms(summed_w, part_w)
        summed_b = add_terms(summed_b, part_b)
    cond_all = jnp.concatenate(cond_parts, axis=0)
    return (
        jnp.stack(outputs),
        jnp.stack(input_grads),
        cond_all,
        ada_terms[0],
        ada_terms[1],
        summed_w[0],
        summed_b[0],
        summed_w[1],
        summed_b[1],
        summed_w[2],
        summed_b[2],
        summed_w[3],
        summed_b[3],
    )


def solution(mesh):
    in_specs = (
        P(None, ("dp", "fsdp"), None),
        P(None, ("dp", "fsdp"), None),
        P(),
        P(None, ("dp", "fsdp")),
        P(None, ("dp", "fsdp")),
        P("dp", "fsdp"),
        P("fsdp"),
        P("dp", "fsdp"),
        P("fsdp"),
        P("dp", "fsdp"),
        P("fsdp"),
        P("dp", "fsdp"),
        P("fsdp"),
        P("dp", "fsdp"),
        P("fsdp"),
    )
    out_specs = (
        P(None, ("dp", "fsdp"), None),
        P(None, ("dp", "fsdp"), None),
        P(None, None, "fsdp"),
        P("dp", "fsdp"),
        P("fsdp"),
        P("dp", "fsdp"),
        P("fsdp"),
        P("dp", "fsdp"),
        P("fsdp"),
        P("dp", "fsdp"),
        P("fsdp"),
        P("dp", "fsdp"),
        P("fsdp"),
    )
    return jax.shard_map(
        per_device, mesh=mesh, in_specs=in_specs, out_specs=out_specs, check_vma=False
    )
```

profile of v0, /device:TPU:0, one launch (start us, length us, event | category | flops | bytes accessed | tf_op | source)
XLA Modules:
  0.0 1921.0 jit_solution(4469489425580298956)
XLA Ops:
  14.6 38.8 %all-gather = bf16[4,864,144]{1,2,0:T(8,128)(2,1)S(1)} all-gather(bf16[1,864,144]{1,2,0:T(8,128)(2,1)S(1)} %bitcast.245), channel_id=1, replica_groups=mesh['dp'=8,'fsdp'=4] {'fsdp'}, dimensions={0}, use_global_device_ids=true | all-gather | bytes 1244160 | tf_op jit(solution)/shard_map/all_gather | solution.py:60
  55.6 15.8 all-gather.1
  73.3 24.5 %all-gather.18.cloned.1.call-done = bf16[576,1152]{0,1:T(8,128)(2,1)} async-done(((bf16[576,288]{0,1:T(8,128)(2,1)}), bf16[576,1152]{0,1:T(8,128)(2,1)}) %all-gather.18.cloned.1.call-update) | async-done | bytes 1327120 | tf_op jit(solution)/shard_map/all_gather | solution.py:63
  102.9 16.8 all-reduce.16
  119.7 13.1 all-gather.2
  135.2 69.7 %all-reduce.25.cloned.1.call-done = (f32[8,6912]{1,0:T(8,128)}, f32[8,6912]{1,0:T(8,128)}) async-done(((f32[8,6912]{1,0:T(8,128)}, f32[8,6912]{1,0:T(8,128)}), (f32[8,6912]{1,0:T(8,128)}, f32[8,6912]{1,0:T(8,128)})) %all-reduce.25.cloned.1.call-update) | async-done | bytes 442384 | tf_op jit(solution)/shard_map/psum | solution.py:144
  217.8 6.2 fusion
  238.5 12.5 all-gather.16.cloned.1.call-done
  251.0 7.1 convolution_add_fusion.1
  258.2 58.6 %all-gather.20.cloned.1.call-done = bf16[4608,1152]{1,0:T(8,128)(2,1)} async-done(((bf16[576,1152]{1,0:T(8,128)(2,1)}), bf16[4608,1152]{1,0:T(8,128)(2,1)}) %all-gather.20.cloned.1.call-update) | async-done | bytes 10616848 | tf_op jit(solution)/shard_map/all_gather | solution.py:73
  316.8 8.8 fusion.139
  331.1 8.6 fusion.141
  363.6 6.0 fusion.160
  369.7 7.6 fusion.55
  378.1 20.2 %all-reduce.15 = (bf16[1152]{0:T(1024)(128)(2,1)S(1)}, bf16[2304]{0:T(1024)(128)(2,1)}, bf16[2304]{0:T(1024)(128)(2,1)}, bf16[1152]{0:T(1024)(128)(2,1)}, bf16[1...) all-reduce(bf16[1152]{0:T(1024)(128)(2,1)S(1)} %copy-done.101, ...), channel_id=1, replica_groups=mesh['dp'=8,'fsdp'=4] {'fsdp'}, use_global_device_ids=true, to_apply=%add.2 | all-reduce | flops 19584 | bytes 78336
  399.2 6.5 convolution_add_fusion.7
  437.4 5.6 convolution_convert_fusion
  456.2 14.8 copy.162
  477.7 15.3 copy.160
  493.1 315.4 %all-reduce.23.cloned.1.call-done = (f32[8,6912]{1,0:T(8,128)}, f32[8,6912]{1,0:T(8,128)}) async-done(((f32[8,6912]{1,0:T(8,128)}, f32[8,6912]{1,0:T(8,128)}), (f32[8,6912]{1,0:T(8,128)}, f32[8,6912]{1,0:T(8,128)})) %all-reduce.23.cloned.1.call-update) | async-done | bytes 442384 | tf_op jit(solution)/shard_map/psum | solution.py:151
  825.8 168.8 %reduce-scatter.47.cloned.1.call-done = bf16[4608,288]{0,1:T(8,128)(2,1)} async-done(((bf16[4608,1152]{0,1:T(8,128)(2,1)}), bf16[4608,288]{0,1:T(8,128)(2,1)}) %reduce-scatter.47.cloned.1.call-update) | async-done | bytes 2654224 | tf_op jit(solution)/shard_map/reduce_scatter | solution.py:98
  999.5 179.6 %reduce-scatter.45.cloned.1.call-done = bf16[4608,288]{0,1:T(8,128)(2,1)} async-done(((bf16[4608,1152]{0,1:T(8,128)(2,1)}), bf16[4608,288]{0,1:T(8,128)(2,1)}) %reduce-scatter.45.cloned.1.call-update) | async-done | bytes 2654224 | tf_op jit(solution)/shard_map/reduce_scatter | solution.py:98
  1183.8 179.3 %reduce-scatter.59.cloned.1.call-done = bf16[1152,1152]{1,0:T(8,128)(2,1)} async-done(((bf16[4608,1152]{1,0:T(8,128)(2,1)}), bf16[1152,1152]{1,0:T(8,128)(2,1)}) %reduce-scatter.59.cloned.1.call-update) | async-done | bytes 2654224
  1368.5 178.4 %reduce-scatter.57.cloned.1.call-done = bf16[1152,1152]{1,0:T(8,128)(2,1)} async-done(((bf16[4608,1152]{1,0:T(8,128)(2,1)}), bf16[1152,1152]{1,0:T(8,128)(2,1)}) %reduce-scatter.57.cloned.1.call-update) | async-done | bytes 2654224
  1557.3 24.7 %all-reduce.14 = (f32[576]{0:T(1024)}, f32[288]{0:T(512)}, f32[1152]{0:T(1024)}, f32[288]{0:T(512)}) all-reduce(f32[576]{0:T(1024)S(1)} %convert_add_fusion.7, f32[288]{0:T(512)S(1)} %convert_add_fusion.9, f32[1152]{0:T(1024)S(1)} %convert_add_fusion.6, f32[288]{0:T(512)S(1)} %convert_add_fusion.8), channel_id=1, replica_groups=mesh['dp'=8,'fsdp'=4] {'dp'}, use_global_device_ids=true, to_apply=%region_36.37 | all-reduce | flops 2304 | bytes 18432 | tf_op jit(solution)/shard_map/psum | solution.py:128
  1590.9 33.9 %reduce-scatter.53.cloned.1.call-done = bf16[144,288]{1,0:T(8,128)(2,1)} async-done(((bf16[1152,288]{1,0:T(8,128)(2,1)}), bf16[144,288]{1,0:T(8,128)(2,1)}) %reduce-scatter.53.cloned.1.call-update) | async-done | bytes 82960
  1626.6 42.2 %reduce-scatter.51.cloned.1.call-done = bf16[144,864]{1,0:T(8,128)(2,1)} async-done(((bf16[1152,864]{1,0:T(8,128)(2,1)}), bf16[144,864]{1,0:T(8,128)(2,1)}) %reduce-scatter.51.cloned.1.call-update) | async-done | bytes 248848
  1669.9 43.3 %reduce-scatter.49.cloned.1.call-done = bf16[144,864]{1,0:T(8,128)(2,1)} async-done(((bf16[1152,864]{1,0:T(8,128)(2,1)}), bf16[144,864]{1,0:T(8,128)(2,1)}) %reduce-scatter.49.cloned.1.call-update) | async-done | bytes 248848
  1715.6 49.3 %reduce-scatter.63.cloned.1.call-done = bf16[576,288]{1,0:T(8,128)(2,1)} async-done(((bf16[4608,288]{1,0:T(8,128)(2,1)}), bf16[576,288]{1,0:T(8,128)(2,1)}) %reduce-scatter.63.cloned.1.call-update) | async-done | bytes 331792
  1766.1 50.2 %reduce-scatter.61.cloned.1.call-done = bf16[576,288]{1,0:T(8,128)(2,1)} async-done(((bf16[4608,288]{1,0:T(8,128)(2,1)}), bf16[576,288]{1,0:T(8,128)(2,1)}) %reduce-scatter.61.cloned.1.call-update) | async-done | bytes 331792
  1818.5 45.1 %reduce-scatter.43.cloned.1.call-done = bf16[144,1152]{1,0:T(8,128)(2,1)} async-done(((bf16[1152,1152]{1,0:T(8,128)(2,1)}), bf16[144,1152]{1,0:T(8,128)(2,1)}) %reduce-scatter.43.cloned.1.call-update) | async-done | bytes 331792 | tf_op jit(solution)/shard_map/reduce_scatter | solution.py:121
  1863.5 47.7 %reduce-scatter.41.cloned.1.call-done = bf16[144,1152]{1,0:T(8,128)(2,1)} async-done(((bf16[1152,1152]{1,0:T(8,128)(2,1)}), bf16[144,1152]{1,0:T(8,128)(2,1)}) %reduce-scatter.41.cloned.1.call-update) | async-done | bytes 331792 | tf_op jit(solution)/shard_map/reduce_scatter | solution.py:121
  (539 shorter events, 184.6 us)
Async XLA Ops:
  8.0 64.7 %all-gather.14.cloned.1.call-start = ((), (), s32[]{:S(2)}) async-start(), calls=%async_computation.18 | async-start | bytes 1658880 | tf_op jit(solution)/shard_map/all_gather | solution.py:62
  8.8 89.0 %all-gather.18.cloned.1.call-start = ((), (), s32[]{:S(2)}) async-start(), calls=%async_computation.20 | async-start | bytes 1843200 | tf_op jit(solution)/shard_map/all_gather | solution.py:63
  9.5 195.4 %all-reduce.25.cloned.1.call-start = ((), (), s32[]{:S(2)}) async-start(), calls=%async_computation.40 | async-start | bytes 884736 | tf_op jit(solution)/shard_map/psum | solution.py:144
  14.6 195.0 %all-gather.10.cloned.1.call-start = ((), (), s32[]{:S(2)}) async-start(), calls=%async_computation.16 | async-start | bytes 8957952 | tf_op jit(solution)/shard_map/all_gather | solution.py:70
  55.6 172.4 %all-gather.12.cloned.1.call-start = ((), (), s32[]{:S(2)}) async-start(), calls=%async_computation.17 | async-start | bytes 2985984 | tf_op jit(solution)/shard_map/all_gather | solution.py:71
  72.6 178.4 %all-gather.16.cloned.1.call-start = ((), (), s32[]{:S(2)}) async-start(), calls=%async_computation.19 | async-start | bytes 11943936 | tf_op jit(solution)/shard_map/all_gather | solution.py:72
  73.3 60.7 %copy-start.17 = (bf16[2,64,1152]{2,1,0:T(8,128)(2,1)S(1)}, bf16[2,64,1152]{2,1,0:T(8,128)(2,1)}, u32[]{:S(2)}) copy-start(bf16[2,64,1152]{2,1,0:T(8,128)(2,1)} %param.15) | copy-start | bytes 884740
  73.3 243.5 %all-gather.20.cloned.1.call-start = ((), (), s32[]{:S(2)}) async-start(), calls=%async_computation.21 | async-start | bytes 11943936 | tf_op jit(solution)/shard_map/all_gather | solution.py:73
  100.4 708.0 %all-reduce.23.cloned.1.call-start = ((), (), s32[]{:S(2)}) async-start(), calls=%async_computation.39 | async-start | bytes 884736 | tf_op jit(solution)/shard_map/psum | solution.py:151
  134.1 75.1 %copy-start.106 = (f32[64]{0:T(128)}, f32[64]{0:T(128)S(1)}, u32[]{:S(2)}) copy-start(f32[64]{0:T(128)S(1)} %broadcast_multiply_fusion.3) | copy-start | bytes 772
  134.1 75.1 %copy-start.109 = (f32[64]{0:T(128)}, f32[64]{0:T(128)S(1)}, u32[]{:S(2)}) copy-start(f32[64]{0:T(128)S(1)} %broadcast_multiply_fusion.1) | copy-start | bytes 772
  134.9 74.3 %copy-start.129 = (f32[64]{0:T(128)}, f32[64]{0:T(128)S(1)}, u32[]{:S(2)}) copy-start(f32[64]{0:T(128)S(1)} %fusion.129) | copy-start | bytes 772
  135.0 74.3 %copy-start.131 = (f32[64]{0:T(128)}, f32[64]{0:T(128)S(1)}, u32[]{:S(2)}) copy-start(f32[64]{0:T(128)S(1)} %fusion.131) | copy-start | bytes 772
  135.0 72.7 %copy-start.118 = (s32[64]{0:T(128)}, s32[64]{0:T(128)S(1)}, u32[]{:S(2)}) copy-start(s32[64]{0:T(128)S(1)} %get-tuple-element.151) | copy-start | bytes 772
  135.0 72.7 %copy-start.120 = (s32[64]{0:T(128)}, s32[64]{0:T(128)S(1)}, u32[]{:S(2)}) copy-start(s32[64]{0:T(128)S(1)} %get-tuple-element.152) | copy-start | bytes 772
  417.3 395.2 %reduce-scatter.39.cloned.1.call-start = ((), (), s32[]{:S(2)}) async-start(), calls=%async_computation.25 | async-start | bytes 3317760 | tf_op jit(solution)/shard_map/reduce_scatter | solution.py:92
  420.1 394.8 %reduce-scatter.37.cloned.1.call-start = ((), (), s32[]{:S(2)}) async-start(), calls=%async_computation.24 | async-start | bytes 3317760 | tf_op jit(solution)/shard_map/reduce_scatter | solution.py:92
  423.5 393.9 %reduce-scatter.35.cloned.1.call-start = ((), (), s32[]{:S(2)}) async-start(), calls=%async_computation.23 | async-start | bytes 9953280 | tf_op jit(solution)/shard_map/reduce_scatter | solution.py:89
  430.1 391.6 %reduce-scatter.33.cloned.1.call-start = ((), (), s32[]{:S(2)}) async-start(), calls=%async_computation.22 | async-start | bytes 9953280 | tf_op jit(solution)/shard_map/reduce_scatter | solution.py:89
  436.5 558.1 %reduce-scatter.47.cloned.1.call-start = ((), (), s32[]{:S(2)}) async-start(), calls=%async_computation.29 | async-start | bytes 13271040 | tf_op jit(solution)/shard_map/reduce_scatter | solution.py:98
  443.1 735.9 %reduce-scatter.45.cloned.1.call-start = ((), (), s32[]{:S(2)}) async-start(), calls=%async_computation.28 | async-start | bytes 13271040 | tf_op jit(solution)/shard_map/reduce_scatter | solution.py:98
  449.6 913.6 %reduce-scatter.59.cloned.1.call-start = ((), (), s32[]{:S(2)}) async-start(), calls=%async_computation.35 | async-start | bytes 13271040
  471.0 1075.9 %reduce-scatter.57.cloned.1.call-start = ((), (), s32[]{:S(2)}) async-start(), calls=%async_computation.34 | async-start | bytes 13271040
  493.0 1094.6 %all-reduce.21.cloned.1.call-start = ((), (), s32[]{:S(2)}) async-start(), calls=%async_computation.38 | async-start | bytes 147456 | tf_op jit(solution)/shard_map/psum | solution.py:160
  812.5 777.4 %reduce-scatter.55.cloned.1.call-start = ((), (), s32[]{:S(2)}) async-start(), calls=%async_computation.33 | async-start | bytes 995328
  814.9 809.8 %reduce-scatter.53.cloned.1.call-start = ((), (), s32[]{:S(2)}) async-start(), calls=%async_computation.32 | async-start | bytes 995328
  817.4 851.4 %reduce-scatter.51.cloned.1.call-start = ((), (), s32[]{:S(2)}) async-start(), calls=%async_computation.31 | async-start | bytes 2322432
  821.6 891.6 %reduce-scatter.49.cloned.1.call-start = ((), (), s32[]{:S(2)}) async-start(), calls=%async_computation.30 | async-start | bytes 2322432
  825.8 939.0 %reduce-scatter.63.cloned.1.call-start = ((), (), s32[]{:S(2)}) async-start(), calls=%async_computation.37 | async-start | bytes 3981312
  999.4 816.9 %reduce-scatter.61.cloned.1.call-start = ((), (), s32[]{:S(2)}) async-start(), calls=%async_computation.36 | async-start | bytes 3981312
  1183.8 679.8 %reduce-scatter.43.cloned.1.call-start = ((), (), s32[]{:S(2)}) async-start(), calls=%async_computation.27 | async-start | bytes 2985984 | tf_op jit(solution)/shard_map/reduce_scatter | solution.py:121
  1368.4 542.8 %reduce-scatter.41.cloned.1.call-start = ((), (), s32[]{:S(2)}) async-start(), calls=%async_computation.26 | async-start | bytes 2985984 | tf_op jit(solution)/shard_map/reduce_scatter | solution.py:121
  (141 other events, 917.9 us)
Sparse Core Ops, SparseCore 0:
  10.5 50.6 all-gather.13
  62.9 34.8 all-gather.17
  100.4 51.8 all-gather.9
  154.8 30.4 all-gather.11
  187.2 63.8 all-gather.15
  252.9 63.8 all-gather.19
  420.4 50.7 reduce-scatter.38
  473.6 52.8 reduce-scatter.36
  528.8 138.6 reduce-scatter.34
  669.8 140.9 reduce-scatter.32
  813.2 181.4 reduce-scatter.46
  997.0 181.9 reduce-scatter.44
  1181.4 181.7 reduce-scatter.58
  1365.5 181.3 reduce-scatter.56
  1550.0 36.2 reduce-scatter.54
  1589.7 35.0 reduce-scatter.52
  1627.9 40.8 reduce-scatter.50
  1672.4 40.8 reduce-scatter.48
  1716.7 48.0 reduce-scatter.62
  1768.2 48.0 reduce-scatter.60
  1819.8 43.7 reduce-scatter.42
  1867.4 43.7 reduce-scatter.40
Sparse Core Ops, SparseCore 1:
  16.0 188.9 all-reduce.24
  417.4 391.0 all-reduce.22
  814.5 555.3 all-reduce.20
where the time goes:
time: 1930 us; the launch traced here: 1920 us
  waiting for transfers between devices  1500 us (78%)
  matrix products  134 us (7%)
  blocking collectives  129 us (7%)
  local copies, waits for them, and re-layouts  106 us (5%)
  other arithmetic  27.3 us (1%)
  between operations  21.9 us (1%)
    unnamed x33, waiting for transfers between devices  579 us
    reduce_scatter x2, waiting for transfers between devices, reduce_grads(): lax.psum_scatter(full_w[3].astype(jnp.bfloat16), 'fsdp', scatter_dimensio...  348 us
    psum x1, waiting for transfers between devices, ada_grads_sharded(): d_total = lax.psum(d_modulation, ('dp', 'fsdp'))  315 us
    reduce_scatter x2, waiting for transfers between devices, reduce_grads(): lax.psum_scatter(inner_sums[2].astype(jnp.bfloat16), 'dp', scatter_dimens...  92.7 us
    unnamed x328, local copies, waits for them, and re-layouts  89.1 us
    psum x1, waiting for transfers between devices, modulation_sharded(): return lax.psum(padded, ('dp', 'fsdp'))  69.7 us
    all_gather x1, waiting for transfers between devices, gather_weights(): lax.all_gather(inner_parts[3], 'dp', axis=0, tiled=True)  58.6 us
    dot_general x8, matrix products, matmul_right_t(): lax.dot_general(left, right, (((1,), (1,)), ((), ())), preferred_element_...  41 us
  transfers between devices with their start and end apart: 25, of which 16 were waited for; matrix products, arithmetic and copies ran while one was open for 9% of the time, Pallas kernels for 0%

commit v1 on v0

v1 whole, which is shorter than its diff:
```python
import functools
import math

import jax
import jax.numpy as jnp
from jax import lax
from jax.experimental import pallas as pl
from jax.experimental.pallas import tpu as pltpu
from jax.sharding import PartitionSpec as P

HEAD_DIM = 72
EPS = 1e-06
GELU_C = math.sqrt(2.0 / math.pi)
PRECISE = lax.Precision.HIGHEST
NEG_FILL = -1e30
MESH_ID = pl.DeviceIdType.MESH
F32 = jnp.float32
BF16 = jnp.bfloat16


def xor_of(index, step, size):
    result, bit = 0, 1
    while bit < size:
        mine = (index // bit) % 2
        result = result + ((mine + (step // bit) % 2) % 2) * bit
        bit *= 2
    return result


class Place:
    def __init__(self, n_chip, n_plane):
        self.n = {"core": 2, "chip": n_chip, "plane": n_plane, "dp": 2 * n_chip}
        self.dp = lax.axis_index("dp")
        self.f = lax.axis_index("fsdp")
        self.c = self.dp // 2
        self.k = self.dp % 2

    def index(self, axis):
        return {"core": self.k, "chip": self.c, "plane": self.f, "dp": self.dp}[axis]

    def peer(self, axis, step):
        other = xor_of(self.index(axis), step, self.n[axis])
        if axis == "core":
            return other, (self.c * 2 + other, self.f)
        if axis == "chip":
            return other, (other * 2 + self.k, self.f)
        if axis == "plane":
            return other, (self.dp, other)
        return other, (other, self.f)


def greet(place, axes):
    barrier = pltpu.get_barrier_semaphore()
    count = 0
    for axis in axes:
        for step in range(1, place.n[axis]):
            pl.semaphore_signal(
                barrier, inc=1, device_id=place.peer(axis, step)[1], device_id_type=MESH_ID
            )
            count += 1
    pl.semaphore_wait(barrier, count)


class Wires:
    def __init__(self, send, recv, local):
        self.send, self.recv, self.local = send, recv, local
        self.remote_count = 0
        self.local_count = 0

    def far(self, src, dst, device):
        at = self.remote_count
        self.remote_count += 1
        copy = pltpu.make_async_remote_copy(
            src_ref=src,
            dst_ref=dst,
            send_sem=self.send.at[at],
            recv_sem=self.recv.at[at],
            device_id=device,
            device_id_type=MESH_ID,
        )
        copy.start()
        return copy

    def near(self, src, dst):
        at = self.local_count
        self.local_count += 1
        copy = pltpu.make_async_copy(src, dst, self.local.at[at])
        copy.start()
        return copy


def wait_all(copies):
    for copy in copies:
        copy.wait()


ANYWHERE = pl.BlockSpec(memory_space=pl.ANY)
ON_CHIP = pl.BlockSpec(memory_space=pltpu.VMEM)


def exchange(name, collective_id, sizes, items):
    n_chip, n_plane = sizes
    n_of = {"core": 2, "chip": n_chip, "plane": n_plane, "dp": 2 * n_chip}
    axes = sorted({item[0] for item in items})
    outs = []
    n_far = 0
    for axis, kind, array in items:
        n_far += n_of[axis] - 1
        shape = array.shape if kind == "a2a" else (n_of[axis],) + array.shape
        outs.append(jax.ShapeDtypeStruct(shape, array.dtype))

    def kernel(*refs):
        ins = refs[: len(items)]
        results = refs[len(items) : 2 * len(items)]
        place = Place(n_chip, n_plane)
        wires = Wires(*refs[2 * len(items) :])
        greet(place, axes)
        copies = []
        for (axis, kind, _), src, dst in zip(items, ins, results):
            mine = place.index(axis)
            for step in range(1, n_of[axis]):
                other, device = place.peer(axis, step)
                piece = src if kind == "ag" else src.at[other]
                copies.append(wires.far(piece, dst.at[mine], device))
        for (axis, kind, _), src, dst in zip(items, ins, results):
            mine = place.index(axis)
            copies.append(wires.near(src if kind == "ag" else src.at[mine], dst.at[mine]))
        wait_all(copies)

    return pl.pallas_call(
        kernel,
        out_shape=tuple(outs),
        in_specs=[ANYWHERE] * len(items),
        out_specs=tuple([ANYWHERE] * len(items)),
        scratch_shapes=[
            pltpu.SemaphoreType.DMA((n_far,)),
            pltpu.SemaphoreType.DMA((n_far,)),
            pltpu.SemaphoreType.DMA((len(items),)),
        ],
        compiler_params=pltpu.CompilerParams(collective_id=collective_id, has_side_effects=True),
        name=name,
    )(*[item[2] for item in items])


def start_kernel(dims, x, cot, ids, bias, mod, wq, w1, wp, w2):
    nc, nf = dims["nc"], dims["nf"]
    per_q, per_1 = dims["per_q"], dims["per_1"]
    chip_q, chip_1 = dims["chip_q"], dims["chip_1"]
    part_q = nc * chip_q
    rows, half = mod.shape[1], mod.shape[2]
    n_far = 5 * (nf - 1) + 3 * (nc - 1) + 4 * (nc - 1) + 4 + 1 + (nc - 1) + (nf - 1) + 1
    outs = (
        jax.ShapeDtypeStruct((nc,) + x.shape, x.dtype),
        jax.ShapeDtypeStruct((nc,) + cot.shape, cot.dtype),
        jax.ShapeDtypeStruct((nc,) + ids.shape, ids.dtype),
        jax.ShapeDtypeStruct((nf,) + bias.shape, bias.dtype),
        jax.ShapeDtypeStruct((nf, 2, rows, half), F32),
        jax.ShapeDtypeStruct((3, nc, 2, chip_q) + wq.shape[1:], BF16),
        jax.ShapeDtypeStruct((chip_1, nc, 2) + w1.shape[1:], BF16),
        jax.ShapeDtypeStruct((2, nf) + wp.shape, BF16),
        jax.ShapeDtypeStruct((2, nf) + w2.shape, BF16),
        jax.ShapeDtypeStruct((nf * per_q,) + wq.shape[1:], BF16),
        jax.ShapeDtypeStruct((nf * per_1,) + w1.shape[1:], BF16),
    )

    def kernel(
        x_in, c_in, i_in, b_in, m_in, q_in, f1_in, p_in, f2_in,
        x_all, c_all, i_all, b_all, m_all, q_chip, f1_chip, p_chip, f2_chip, q_rows, f1_rows,
        m_core, m_sum, m_chip, send, recv, local,
    ):
        place = Place(nc, nf)
        wires = Wires(send, recv, local)
        c, k, f = place.c, place.k, place.f
        greet(place, ("core", "chip", "plane"))
        core_other, core_peer = place.peer("core", 1)
        chip_peers = [place.peer("chip", step) for step in range(1, nc)]
        plane_peers = [place.peer("plane", step) for step in range(1, nf)]

        m_first = wires.far(m_in.at[core_other], m_core, core_peer)
        q_got, f1_got, p_got, f2_got, small = [], [], [], [], []
        for _, peer in plane_peers:
            q_got.append(wires.far(q_in, q_rows.at[pl.ds(f * per_q, per_q)], peer))
            small.append(wires.far(b_in, b_all.at[f], peer))
        q_got.append(wires.near(q_in, q_rows.at[pl.ds(f * per_q, per_q)]))
        small.append(wires.near(b_in, b_all.at[f]))
        for _, peer in chip_peers:
            small.append(wires.far(i_in, i_all.at[c], peer))
            small.append(wires.far(x_in, x_all.at[c], peer))
        m_first.wait()
        m_sum[...] = m_in[k] + m_core[...]
        m_chip[c] = m_sum[...]
        m_second = [wires.far(m_sum, m_chip.at[c], peer) for _, peer in chip_peers]
        for _, peer in plane_peers:
            p_got.append(wires.far(p_in, p_chip.at[k, f], peer))
        for _, peer in plane_peers:
            f1_got.append(wires.far(f1_in, f1_rows.at[pl.ds(f * per_1, per_1)], peer))
        for _, peer in plane_peers:
            f2_got.append(wires.far(f2_in, f2_chip.at[k, f], peer))
        p_got.append(wires.near(p_in, p_chip.at[k, f]))
        f1_got.append(wires.near(f1_in, f1_rows.at[pl.ds(f * per_1, per_1)]))
        f2_got.append(wires.near(f2_in, f2_chip.at[k, f]))
        small.append(wires.near(i_in, i_all.at[c]))
        small.append(wires.near(x_in, x_all.at[c]))
        for _, peer in chip_peers:
            small.append(wires.far(c_in, c_all.at[c], peer))
        small.append(wires.near(c_in, c_all.at[c]))
        wait_all(m_second)
        total = m_chip[0]
        for other in range(1, nc):
            total = total + m_chip[other]
        m_all[f, k] = total
        wait_all([wires.far(m_all.at[f, k], m_all.at[f, k], peer) for _, peer in plane_peers])
        m_last = wires.far(m_all.at[:, k], m_all.at[:, k], core_peer)

        wait_all(q_got)
        q_moved = []
        for kind in range(3):
            for other, peer in chip_peers:
                q_moved.append(
                    wires.far(
                        q_rows.at[pl.ds(kind * part_q + other * chip_q, chip_q)],
                        q_chip.at[kind, c, k],
                        peer,
                    )
                )
            q_moved.append(
                wires.near(
                    q_rows.at[pl.ds(kind * part_q + c * chip_q, chip_q)], q_chip.at[kind, c, k]
                )
            )
        wait_all(p_got)
        last = [m_last, wires.far(p_chip.at[k], p_chip.at[k], core_peer)]
        wait_all(q_moved)
        last.append(wires.far(q_chip.at[:, :, k], q_chip.at[:, :, k], core_peer))
        wait_all(f1_got)
        f1_moved = []
        for other, peer in chip_peers:
            f1_moved.append(
                wires.far(f1_rows.at[pl.ds(other * chip_1, chip_1)], f1_chip.at[:, c, k], peer)
            )
        f1_moved.append(
            wires.near(f1_rows.at[pl.ds(c * chip_1, chip_1)], f1_chip.at[:, c, k])
        )
        wait_all(f2_got)
        last.append(wires.far(f2_chip.at[k], f2_chip.at[k], core_peer))
        wait_all(f1_moved)
        last.append(wires.far(f1_chip.at[:, :, k], f1_chip.at[:, :, k], core_peer))
        wait_all(small)
        wait_all(last)

    return pl.pallas_call(
        kernel,
        out_shape=outs,
        in_specs=[ANYWHERE] * 4 + [ON_CHIP] + [ANYWHERE] * 4,
        out_specs=tuple([ANYWHERE] * 4 + [ON_CHIP] + [ANYWHERE] * 6),
        scratch_shapes=[
            pltpu.VMEM((rows, half), F32),
            pltpu.VMEM((rows, half), F32),
            pltpu.VMEM((nc, rows, half), F32),
            pltpu.SemaphoreType.DMA((n_far,)),
            pltpu.SemaphoreType.DMA((n_far,)),
            pltpu.SemaphoreType.DMA((12,)),
        ],
        compiler_params=pltpu.CompilerParams(collective_id=0, has_side_effects=True),
        name="start",
    )(x, cot, ids, bias, mod, wq, w1, wp, w2)


def sum_small_kernel(dims, terms):
    nc, nf = dims["nc"], dims["nf"]
    _, _, rows, half = terms.shape
    n_far = (nf - 1) + 1 + (nc - 1) + 1

    def kernel(t_in, total, z_got, both, core_got, chip_got, send, recv, local):
        place = Place(nc, nf)
        wires = Wires(send, recv, local)
        c, k, f = place.c, place.k, place.f
        greet(place, ("core", "chip", "plane"))
        core_other, core_peer = place.peer("core", 1)
        copies = []
        for step in range(1, nf):
            other, peer = place.peer("plane", step)
            copies.append(wires.far(t_in.at[other], z_got.at[f], peer))
        z_got[f] = t_in[f]
        wait_all(copies)
        value = z_got[0]
        for other in range(1, nf):
            value = value + z_got[other]
        both[...] = value
        wires.far(both.at[core_other], core_got, core_peer).wait()
        chip_got[c] = both[k] + core_got[...]
        copies = []
        for step in range(1, nc):
            _, peer = place.peer("chip", step)
            copies.append(wires.far(chip_got.at[c], chip_got.at[c], peer))
        wait_all(copies)
        value = chip_got[0]
        for other in range(1, nc):
            value = value + chip_got[other]
        total[k] = value
        wires.far(total.at[k], total.at[k], core_peer).wait()

    return pl.pallas_call(
        kernel,
        out_shape=jax.ShapeDtypeStruct((2, rows, half), F32),
        in_specs=[ON_CHIP],
        out_specs=ON_CHIP,
        scratch_shapes=[
            pltpu.VMEM((nf, 2, rows, half), F32),
            pltpu.VMEM((2, rows, half), F32),
            pltpu.VMEM((rows, half), F32),
            pltpu.VMEM((nc, rows, half), F32),
            pltpu.SemaphoreType.DMA((n_far,)),
            pltpu.SemaphoreType.DMA((n_far,)),
            pltpu.SemaphoreType.DMA((1,)),
        ],
        compiler_params=pltpu.CompilerParams(collective_id=1, has_side_effects=True),
        name="sum_small",
    )(terms)


def cond_kernel(dims, part):
    nc, nf = dims["nc"], dims["nf"]
    nd = 2 * nc
    rows, width = part.shape
    n_far = (nf - 1) + (nd - 1)

    def kernel(p_in, out, got, send, recv, local):
        place = Place(nc, nf)
        wires = Wires(send, recv, local)
        greet(place, ("plane", "dp"))
        copies = []
        for step in range(1, nf):
            copies.append(wires.far(p_in, got.at[place.f], place.peer("plane", step)[1]))
        got[place.f] = p_in[...]
        wait_all(copies)
        value = got[0]
        for other in range(1, nf):
            value = value + got[other]
        out[place.dp] = value
        copies = []
        for step in range(1, nd):
            copies.append(
                wires.far(out.at[place.dp], out.at[place.dp], place.peer("dp", step)[1])
            )
        wait_all(copies)

    return pl.pallas_call(
        kernel,
        out_shape=jax.ShapeDtypeStruct((nd, rows, width), F32),
        in_specs=[ON_CHIP],
        out_specs=ON_CHIP,
        scratch_shapes=[
            pltpu.VMEM((nf, rows, width), F32),
            pltpu.SemaphoreType.DMA((n_far,)),
            pltpu.SemaphoreType.DMA((n_far,)),
            pltpu.SemaphoreType.DMA((1,)),
        ],
        compiler_params=pltpu.CompilerParams(collective_id=2, has_side_effects=True),
        name="cond_sum",
    )(part)


def dot(left, right):
    return jnp.dot(left, right, preferred_element_type=F32)


def dot_rt(left, right):
    return lax.dot_general(left, right, (((1,), (1,)), ((), ())), preferred_element_type=F32)


def dot_lt(left, right):
    return lax.dot_general(left, right, (((0,), (0,)), ((), ())), preferred_element_type=F32)


def precise(left, right, dims):
    return lax.dot_general(
        left, right, (dims, ((), ())), precision=PRECISE, preferred_element_type=F32
    )


def ln_parts(values):
    centre = values - jnp.mean(values, axis=-1, keepdims=True)
    scale = lax.rsqrt(jnp.mean(centre * centre, axis=-1, keepdims=True) + EPS)
    return centre * scale, scale


def ln_back(normal, scale, grad):
    return scale * (
        grad
        - jnp.mean(grad, axis=-1, keepdims=True)
        - normal * jnp.mean(grad * normal, axis=-1, keepdims=True)
    )


def gelu_both(h):
    square = h * h
    t = jnp.tanh(GELU_C * (h + 0.044715 * h * square))
    value = 0.5 * h * (1.0 + t)
    slope = 0.5 * (1.0 + t) + 0.5 * h * (1.0 - t * t) * GELU_C * (1.0 + 3 * 0.044715 * square)
    return value, slope


def per_device(
    n_dp, nf, patches, cotangent, conditioning, frame_of_slot, clip_of_slot,
    w_ada, b_ada, w_qkv, b_qv, w_proj, b_proj, w_fc1, b_fc1, w_fc2, b_fc2,
):
    nc = n_dp // 2
    sizes = (nc, nf)
    micro, block, width = patches.shape
    own = micro * block
    clips = conditioning.shape[1]
    rows_d = width // n_dp
    cols_f = width // nf
    ff = w_fc1.shape[1] * nf
    ff_d = ff // n_dp
    chip_w = width // nc
    piece_q = math.gcd(3 * width // nf, chip_w)
    piece_1 = math.gcd(ff // nf, ff_d)
    dims = dict(
        nc=nc,
        nf=nf,
        per_q=3 * width // nf // piece_q,
        per_1=ff // nf // piece_1,
        chip_q=chip_w // piece_q,
        chip_1=ff // nc // piece_1,
    )
    dp = lax.axis_index("dp")
    f = lax.axis_index("fsdp")
    c, k = dp // 2, dp % 2

    q_send = w_qkv.reshape(rows_d, dims["per_q"], piece_q).transpose(1, 0, 2)
    f1_send = w_fc1.reshape(rows_d, dims["per_1"], piece_1).transpose(1, 0, 2)
    f2_send = w_fc2.T
    cond = conditioning.reshape(micro * clips, width)
    silu_cond = jax.nn.silu(cond)
    silu_low = silu_cond.astype(BF16)
    ada_w = w_ada.shape[1]
    silu_part = lax.dynamic_slice_in_dim(silu_low, dp * rows_d, rows_d, 1)
    mod_part = dot(silu_part, w_ada) + jnp.where(dp == 0, b_ada.astype(F32), 0.0)[None]
    mod_send = mod_part.reshape(-1, 2, ada_w // 2).transpose(1, 0, 2)
    ids = jnp.stack([frame_of_slot.reshape(own), clip_of_slot.reshape(own)])
    ids = jnp.concatenate([ids, jnp.zeros((6, own), jnp.int32)])
    bias_send = jnp.concatenate([b_qv, b_proj, b_fc1, b_fc2]).astype(F32)[None]

    (x_all, c_all, ids_all, bias_all, mod_all, q_chip, f1_chip, p_chip, f2_chip, _, _) = start_kernel(
        dims, patches.reshape(own, width), cotangent.reshape(own, width), ids, bias_send, mod_send,
        q_send, f1_send, w_proj, f2_send,
    )
    group = nc * own
    modulation = mod_all.transpose(2, 0, 1, 3).reshape(micro * clips, 6 * width)
    q_parts = [
        q_chip[i].reshape(nc, 2, dims["chip_q"], rows_d, piece_q).transpose(0, 1, 3, 2, 4).reshape(width, chip_w)
        for i in range(3)
    ]
    w1 = f1_chip.transpose(1, 2, 3, 0, 4).reshape(width, ff // nc)
    wp = p_chip.transpose(0, 2, 1, 3).reshape(chip_w, width)
    w2t = f2_chip.reshape(2, width, ff_d).transpose(1, 0, 2).reshape(width, 2 * ff_d)
    cut = [0, 2 * cols_f, 3 * cols_f, 3 * cols_f + ff // nf, 4 * cols_f + ff // nf]
    b_parts = [bias_all[:, 0, a:b].reshape(-1) for a, b in zip(cut[:-1], cut[1:])]
    bq = lax.dynamic_slice_in_dim(b_parts[0], c * chip_w, chip_w, 0)
    bv = lax.dynamic_slice_in_dim(b_parts[0], width + c * chip_w, chip_w, 0)
    b1 = lax.dynamic_slice_in_dim(b_parts[2], c * (ff // nc), ff // nc, 0)

    def hot_of(clip_ids):
        count = clip_ids.shape[0]
        row = (jnp.arange(count, dtype=jnp.int32) // block) % micro * clips + clip_ids
        return (row[:, None] == jnp.arange(micro * clips, dtype=jnp.int32)[None]).astype(F32)

    hot_group = hot_of(ids_all[:, 1].reshape(group))
    hot_own = hot_of(clip_of_slot.reshape(own))
    mod_group = precise(hot_group, modulation, ((1,), (0,)))
    mod_own = precise(hot_own, modulation, ((1,), (0,)))
    shift1, scale1 = mod_group[:, :width], mod_group[:, width : 2 * width]
    gate1 = mod_own[:, 2 * width : 3 * width]
    shift2, scale2 = mod_own[:, 3 * width : 4 * width], mod_own[:, 4 * width : 5 * width]
    gate2_group, gate2 = mod_group[:, 5 * width :], mod_own[:, 5 * width :]

    x_group = x_all.reshape(group, width).astype(F32)
    norm1, rstd1 = ln_parts(x_group)
    a_in = (norm1 * (1.0 + scale1) + shift1).astype(BF16)
    zero = jnp.zeros_like(bq)
    q, kk, v = [
        (dot(a_in, w) + b[None]).astype(BF16) for w, b in zip(q_parts, (bq, zero, bv))
    ]
    heads = chip_w // HEAD_DIM
    blocks = group // block
    q4, k4, v4 = [t.reshape(blocks, block, heads, HEAD_DIM) for t in (q, kk, v)]
    frames = ids_all[:, 0].reshape(blocks, block)
    same = (frames[:, :, None] == frames[:, None, :])[:, None]
    scores = jnp.einsum("bqhd,bkhd->bhqk", q4, k4, preferred_element_type=F32) * HEAD_DIM ** (-0.5)
    scores = jnp.where(same, scores, NEG_FILL)
    top = jnp.max(scores, axis=-1, keepdims=True)
    raised = jnp.exp(scores - top)
    probs = raised / jnp.sum(raised, axis=-1, keepdims=True)
    probs_low = probs.astype(BF16)
    mixed = jnp.einsum("bhqk,bkhd->bqhd", probs_low, v4, preferred_element_type=F32)
    mixed = mixed.reshape(group, chip_w).astype(BF16)
    attn_part = dot(mixed, wp)
    (attn_got,) = exchange(
        "attn_sum", 3, sizes, [("chip", "a2a", attn_part.astype(BF16).reshape(nc, own, width))]
    )
    attn = jnp.sum(attn_got.astype(F32), axis=0) + b_parts[1][None]
    x_own = patches.reshape(own, width).astype(F32)
    after = x_own + gate1 * attn
    norm2, rstd2 = ln_parts(after)
    m_own = (norm2 * (1.0 + scale2) + shift2).astype(BF16)
    (m_all,) = exchange("m_gather", 4, sizes, [("chip", "ag", m_own)])
    m_in = m_all.reshape(group, width)

    hidden = dot(m_in, w1) + b1[None]
    act, slope = gelu_both(hidden)
    act = act.astype(BF16)
    branch_part = dot_rt(act, w2t)
    cot_group = c_all.reshape(group, width).astype(F32)
    d_branch = (gate2_group * cot_group).astype(BF16)
    grad_2t = dot_lt(d_branch, act)
    d_hidden = (dot(d_branch, w2t) * slope).astype(BF16)
    grad_1 = dot_lt(m_in, d_hidden)
    d_m_part = dot_rt(d_hidden, w1)
    branch_got, d_m_got = exchange(
        "ff_sum",
        5,
        sizes,
        [
            ("chip", "a2a", d_m_part.astype(BF16).reshape(nc, own, width)),
            ("chip", "a2a", branch_part.astype(BF16).reshape(nc, own, width)),
        ],
    )[::-1]
    branch = jnp.sum(branch_got.astype(F32), axis=0) + b_parts[3][None]
    output = (after + gate2 * branch).astype(BF16)
    d_m = jnp.sum(d_m_got.astype(F32), axis=0)
    cot_own = cotangent.reshape(own, width).astype(F32)
    d_after = cot_own + ln_back(norm2, rstd2, d_m * (1.0 + scale2))
    d_attn = (gate1 * d_after).astype(BF16)
    (d_attn_all,) = exchange("d_attn_gather", 6, sizes, [("chip", "ag", d_attn)])
    d_attn_group = d_attn_all.reshape(group, width)
    grad_p = dot_lt(mixed, d_attn_group)
    d_mix = dot_rt(d_attn_group, wp).astype(BF16).reshape(blocks, block, heads, HEAD_DIM)
    d_probs = jnp.einsum("bqhd,bkhd->bhqk", d_mix, v4, preferred_element_type=F32)
    d_scores = probs * (d_probs - jnp.sum(probs * d_probs, axis=-1, keepdims=True))
    d_scores = d_scores.astype(BF16)
    dq = jnp.einsum("bhqk,bkhd->bqhd", d_scores, k4, preferred_element_type=F32) * HEAD_DIM ** (-0.5)
    dk = jnp.einsum("bhqk,bqhd->bkhd", d_scores, q4, preferred_element_type=F32) * HEAD_DIM ** (-0.5)
    dv = jnp.einsum("bhqk,bqhd->bkhd", probs_low, d_mix, preferred_element_type=F32)
    dqkv = [t.reshape(group, chip_w).astype(BF16) for t in (dq, dk, dv)]
    d_a_part = sum(dot_rt(t, w) for t, w in zip(dqkv, q_parts))
    grad_q = jnp.stack([dot_lt(a_in, t) for t in dqkv])
    (d_a_got,) = exchange(
        "d_a_sum", 7, sizes, [("chip", "a2a", d_a_part.astype(BF16).reshape(nc, own, width))]
    )
    d_a = jnp.sum(d_a_got.astype(F32), axis=0)
    norm1_own, rstd1_own = ln_parts(x_own)
    scale1_own = mod_own[:, width : 2 * width]
    input_grad = (d_after + ln_back(norm1_own, rstd1_own, d_a * (1.0 + scale1_own))).astype(BF16)

    g_q = grad_q.reshape(3, nc, 2, rows_d, dims["chip_q"], piece_q).transpose(2, 1, 0, 4, 3, 5)
    g_1 = grad_1.reshape(nc, 2, rows_d, dims["chip_1"], piece_1).transpose(1, 0, 3, 2, 4)
    g_p = grad_p.reshape(2, rows_d, nf, cols_f).transpose(0, 2, 1, 3)
    g_2 = grad_2t.reshape(nf, cols_f, 2, ff_d).transpose(2, 0, 1, 3)
    got = exchange("grad_core", 8, sizes, [("core", "a2a", g.astype(BF16)) for g in (g_q, g_1, g_p, g_2)])
    s_q, s_1, s_p, s_2 = [jnp.sum(g.astype(F32), axis=0).astype(BF16) for g in got]
    r_q, r_1 = exchange("grad_chip", 9, sizes, [("chip", "a2a", s_q), ("chip", "a2a", s_1)])
    z_q = r_q.transpose(1, 0, 2, 3, 4).reshape(nf, dims["per_q"], rows_d, piece_q)
    z_1 = r_1.reshape(nf, dims["per_1"], rows_d, piece_1)
    got = exchange("grad_plane", 10, sizes, [("plane", "a2a", g) for g in (z_q, z_1, s_p, s_2)])
    o_q, o_1, o_p, o_2 = [jnp.sum(g.astype(F32), axis=0) for g in got]
    grad_w_qkv = o_q.transpose(1, 0, 2).reshape(rows_d, 3 * width // nf)
    grad_w_fc1 = o_1.transpose(1, 0, 2).reshape(rows_d, ff // nf)
    grad_w_fc2 = o_2.T

    d_token = jnp.concatenate(
        [d_a, d_a * norm1_own, d_after * attn, d_m, d_m * norm2, cot_own * branch], axis=1
    )
    d_mod = precise(hot_own, d_token, ((0,), (0,)))
    d_branch_own = (gate2 * cot_own).astype(BF16).astype(F32)

    def columns(value):
        return jnp.sum(value.astype(F32), axis=0)

    def spread(value, count):
        return lax.dynamic_update_slice_in_dim(
            jnp.zeros((count,), F32), value, c * value.shape[0], 0
        )

    g_bqv = jnp.concatenate([spread(columns(dqkv[0]), width), spread(columns(dqkv[2]), width)])
    g_b1 = spread(columns(d_hidden), ff)
    bias_terms = jnp.concatenate(
        [
            g_bqv.reshape(nf, -1),
            columns(d_attn).reshape(nf, -1),
            g_b1.reshape(nf, -1),
            columns(d_branch_own).reshape(nf, -1),
        ],
        axis=1,
    )
    n_bias = bias_terms.shape[1]
    bias_rows = -(-n_bias // ada_w)
    bias_terms = jnp.pad(bias_terms, ((0, 0), (0, bias_rows * ada_w - n_bias)))
    terms = jnp.concatenate(
        [d_mod.reshape(micro * clips, nf, ada_w).transpose(1, 0, 2), bias_terms.reshape(nf, bias_rows, ada_w)],
        axis=1,
    )
    pad_rows = -terms.shape[1] % 8
    terms = jnp.pad(terms, ((0, 0), (0, pad_rows), (0, 0)))
    terms = terms.reshape(nf, -1, 2, ada_w // 2).transpose(0, 2, 1, 3)
    total = sum_small_kernel(dims, terms).transpose(1, 0, 2).reshape(-1, ada_w)
    d_cols = total[: micro * clips]
    bias_sums = total[micro * clips : micro * clips + bias_rows].reshape(-1)[:n_bias]
    g_parts = [bias_sums[a:b] for a, b in zip(cut[:-1], cut[1:])]
    grad_w_ada = precise(silu_part.astype(F32), d_cols, ((0,), (0,)))
    grad_b_ada = jnp.sum(d_cols, axis=0)
    d_silu_part = precise(d_cols, w_ada.astype(F32), ((1,), (1,)))
    d_silu = cond_kernel(dims, d_silu_part).transpose(1, 0, 2).reshape(micro * clips, width)
    d_silu_own = lax.dynamic_slice_in_dim(d_silu, f * cols_f, cols_f, 1)
    cond_own = lax.dynamic_slice_in_dim(cond, f * cols_f, cols_f, 1)
    _, silu_back = jax.vjp(jax.nn.silu, cond_own)
    cond_grad = silu_back(d_silu_own)[0].reshape(micro, clips, cols_f)
    return (
        output.reshape(patches.shape),
        input_grad.reshape(patches.shape),
        cond_grad,
        grad_w_ada,
        grad_b_ada,
        grad_w_qkv,
        g_parts[0],
        o_p,
        g_parts[1],
        grad_w_fc1,
        g_parts[2],
        grad_w_fc2,
        g_parts[3],
    )


def solution(mesh):
    tokens = P(None, ("dp", "fsdp"), None)
    ids = P(None, ("dp", "fsdp"))
    both, cols = P("dp", "fsdp"), P("fsdp")
    in_specs = (tokens, tokens, P(), ids, ids) + (both, cols) * 5
    out_specs = (tokens, tokens, P(None, None, "fsdp")) + (both, cols) * 5
    return jax.shard_map(
        functools.partial(per_device, mesh.shape["dp"], mesh.shape["fsdp"]),
        mesh=mesh,
        in_specs=in_specs,
        out_specs=out_specs,
        check_vma=False,
    )
```

time: 1930 us -> 802 us (0.42)
  waiting for transfers between devices: 1500 us -> 0 us
  Pallas kernels: 0 us -> 563 us
  blocking collectives: 129 us -> 0 us
  matrix products: 134 us -> 73.6 us
  other arithmetic: 27.3 us -> 54.3 us
  between operations: 21.9 us -> 1.85 us
    unnamed x33 -> x0, waiting for transfers between devices: 579 us -> none
    pallas_call x0 -> x11, Pallas kernels: none -> 563 us  [the longest x8 367 us: exchange(): pl.pallas_call(kernel, out_shape=tuple(outs), in_specs=[ANYWHERE] * len(i...]
    reduce_scatter x8 -> x0, waiting for transfers between devices: 441 us -> none  [the longest x2 348 us: reduce_grads(): lax.psum_scatter(full_w[3].astype(jnp.bfloat16), 'fsdp', scatter_dimensio...]
    psum x3 -> x0, waiting for transfers between devices: 385 us -> none  [the longest x1 315 us: ada_grads_sharded(): d_total = lax.psum(d_modulation, ('dp', 'fsdp'))]
    all_gather x6 -> x0, waiting for transfers between devices: 95.6 us -> none  [the longest x1 58.6 us: gather_weights(): lax.all_gather(inner_parts[3], 'dp', axis=0, tiled=True)]
    unnamed x328 -> x113, local copies, waits for them, and re-layouts: 89.1 us -> 4.45 us
    all_gather x3 -> x0, blocking collectives: 67.7 us -> none  [the longest x1 38.8 us: gather_weights(): lax.all_gather(w_qkv, 'fsdp', axis=1, tiled=True)]
    dot_general x46 -> x30, matrix products: 134 us -> 73.6 us  [the longest x6 19.9 us: dot_lt(): lax.dot_general(left, right, (((0,), (0,)), ((), ())), preferred_element_...]
  transfers between devices with their start and end apart: 25 -> 0, of which waited for: 16 -> 0; matrix products, arithmetic and copies ran while one was open for 9% -> 0% of each run, Pallas kernels for 0% -> 0%
where the time goes in v1:
time: 802 us; the launch traced here: 791 us
  Pallas kernels  563 us (70%)
  local copies, waits for them, and re-layouts  98.1 us (12%)
  matrix products  73.6 us (9%)
  other arithmetic  54.3 us (7%)
    pallas_call x8, Pallas kernels, exchange(): pl.pallas_call(kernel, out_shape=tuple(outs), in_specs=[ANYWHERE] * len(i...  367 us
    pallas_call x1, Pallas kernels, start_kernel(): pl.pallas_call(kernel, out_shape=outs, in_specs=[ANYWHERE] * 4 + [ON_CHIP...  150 us
    pallas_call x1, Pallas kernels, sum_small_kernel(): pl.pallas_call(kernel, out_shape=jax.ShapeDtypeStruct((2, rows, half), F3...  32.7 us
    dot_general x6, matrix products, dot_lt(): lax.dot_general(left, right, (((0,), (0,)), ((), ())), preferred_element_...  19.9 us
    dot_general x7, matrix products, dot(): return jnp.dot(left, right, preferred_element_type=F32)  17.6 us

profile of v1, /device:TPU:0, one launch (start us, length us, event | category | flops | bytes accessed | tf_op | source)
XLA Modules:
  0.0 790.7 jit_solution(10956920166998435606)
XLA Ops:
  8.7 150.3 %start.1 = (bf16[4,128,1152]{2,1,0:T(8,128)(2,1)}, bf16[4,128,1152]{2,1,0:T(8,128)(2,1)}, s32[4,8,128]{2,1,0:T(8,128)}, f32[4,1,2304]{2,1,0:T(1,128)}, f32[4,2,1...) custom-call(bf16[128,1152]{1,0:T(8,128)(2,1)} %bitcast.230, ...), custom_call_target="tpu_custom_call" | custom-call | tf_op jit(solution)/shard_map/start/pallas_call | solution.py:251
  164.9 5.8 fusion.53
  195.8 16.9 %attn_sum.1 = bf16[4,128,1152]{2,1,0:T(8,128)(2,1)} custom-call(bf16[4,128,1152]{2,1,0:T(8,128)(2,1)} %bitcast.268), custom_call_target="tpu_custom_call" | custom-call | tf_op jit(solution)/shard_map/attn_sum/pallas_call | solution.py:130
  214.3 3.3 fusion.56
  221.5 16.1 %m_gather.1 = bf16[4,128,1152]{2,1,0:T(8,128)(2,1)} custom-call(bf16[128,1152]{1,0:T(8,128)(2,1)} %fusion.49.refs_0_), custom_call_target="tpu_custom_call" | custom-call | tf_op jit(solution)/shard_map/m_gather/pallas_call | solution.py:130
  237.9 6.4 copy.133
  244.3 6.9 reshape.441
  251.2 5.5 convolution_add_fusion.2
  256.7 4.6 copy.132
  261.3 6.4 convert_reduce_fusion.3
  275.0 5.1 convert_bitcast_fusion.refs_1_
  280.1 3.2 convolution_convert_fusion.1
  283.3 3.0 convolution_convert_fusion.2
  286.3 27.9 %ff_sum.1 = (bf16[4,128,1152]{2,1,0:T(8,128)(2,1)}, bf16[4,128,1152]{2,1,0:T(8,128)(2,1)}) custom-call(bf16[4,128,1152]{2,1,0:T(8,128)(2,1)} %bitcast.264, bf16[4,128,1152]{2,1,0:T(8,128)(2,1)} %bitcast.263), custom_call_target="tpu_custom_call" | custom-call | tf_op jit(solution)/shard_map/ff_sum/pallas_call | solution.py:130
  314.2 3.0 convert_reduce_fusion.5
  318.7 3.0 convert_reduce_fusion.14
  321.7 14.2 %d_attn_gather.1 = bf16[4,128,1152]{2,1,0:T(8,128)(2,1)} custom-call(bf16[128,1152]{1,0:T(8,128)(2,1)} %get-tuple-element.65.refs_0_), custom_call_target="tpu_custom_call" | custom-call | tf_op jit(solution)/shard_map/d_attn_gather/pallas_call | solution.py:130
  338.6 3.1 fusion.21.refs_2_
  357.4 3.1 fusion.19
  364.2 3.1 fusion.18
  377.0 3.3 convolution_convert_fusion
  380.3 7.7 convert_element_type.280
  388.1 3.8 copy.183
  391.8 144.1 %grad_core.1 = (bf16[2,4,3,1,144,288]{5,4,3,2,1,0:T(8,128)(2,1)}, bf16[2,4,2,144,576]{4,3,2,1,0:T(8,128)(2,1)}, bf16[2,4,144,288]{3,2,1,0:T(8,128)(2,1)}, bf16[2,4,288,576]{3,2,1,0:T(8,128)(2,1)}) custom-call(bf16[2,4,3,1,144,288]{5,4,3,2,1,0:T(8,128)(2,1)} %maximum_bitcast_fusion.refs_0_, bf16[2,4,2,144,576]{4,3,2,1,0:T(8,128)(2,1)} %convert_bitcast_fusion.refs_1_, ...), custom_call_target="tpu_custom_call" | custom-call | tf_op jit(solution)/shard_map/grad_core/pallas_call | solution.py:130
  536.0 3.9 reduce_sum.317.refs_1_
  539.9 3.7 reduce_sum.315
  543.6 34.5 %grad_chip.1 = (bf16[4,3,1,144,288]{4,3,2,1,0:T(8,128)(2,1)}, bf16[4,2,144,576]{3,2,1,0:T(8,128)(2,1)}) custom-call(bf16[4,3,1,144,288]{4,3,2,1,0:T(8,128)(2,1)} %bitcast.237, bf16[4,2,144,576]{3,2,1,0:T(8,128)(2,1)} %reduce_sum.317.refs_1_), custom_call_target="tpu_custom_call" | custom-call | tf_op jit(solution)/shard_map/grad_chip/pallas_call | solution.py:130
  580.6 4.0 reduce_sum.319.refs_3_
  586.8 99.3 %grad_plane.1 = (bf16[4,3,144,288]{3,2,1,0:T(8,128)(2,1)}, bf16[4,2,144,576]{3,2,1,0:T(8,128)(2,1)}, bf16[4,144,288]{2,1,0:T(8,128)(2,1)}, bf16[4,288,576]{2,1,0:T(8,128)(2,1)}) custom-call(bf16[4,3,144,288]{3,2,1,0:T(8,128)(2,1)} %bitcast.236, bf16[4,2,144,576]{3,2,1,0:T(8,128)(2,1)} %get-tuple-element.48.refs_1_, ...), custom_call_target="tpu_custom_call" | custom-call | tf_op jit(solution)/shard_map/grad_plane/pallas_call | solution.py:130
  709.2 14.2 %d_a_sum.1 = bf16[4,128,1152]{2,1,0:T(8,128)(2,1)} custom-call(bf16[4,128,1152]{2,1,0:T(8,128)(2,1)} %bitcast.244), custom_call_target="tpu_custom_call" | custom-call | tf_op jit(solution)/shard_map/d_a_sum/pallas_call | solution.py:130
  735.8 32.7 %sum_small.1 = f32[2,24,864]{2,1,0:T(8,128)} custom-call(f32[4,2,24,864]{3,2,1,0:T(8,128)} %bitcast.252), custom_call_target="tpu_custom_call" | custom-call | tf_op jit(solution)/shard_map/sum_small/pallas_call | solution.py:303
  772.5 12.6 %cond_sum.1 = f32[8,16,144]{2,1,0:T(8,128)} custom-call(f32[16,144]{1,0:T(8,128)} %fusion.81.p_in), custom_call_target="tpu_custom_call" | custom-call | tf_op jit(solution)/shard_map/cond_sum/pallas_call | solution.py:348
  (270 shorter events, 133.9 us)
Async XLA Ops:
  0.7 5.2 copy-start.45
  0.7 6.3 copy-start.49
  0.7 6.3 copy-start.50
  0.7 6.3 copy-start.51
  0.7 6.3 copy-start.52
  0.7 7.2 copy-start.53
  0.7 7.2 copy-start.54
  159.0 4.2 copy-start.43
  164.0 6.6 copy-start.23
  164.9 5.8 copy-start.2
  164.9 5.8 copy-start.37
  173.9 4.8 copy-start.3
  178.0 4.3 copy-start.15
  189.8 6.0 copy-start.46
  195.8 18.5 %copy-start.24 = (f32[16,6912]{1,0:T(8,128)S(1)}, f32[16,6912]{1,0:T(8,128)}, u32[]{:S(2)}) copy-start(f32[16,6912]{1,0:T(8,128)} %copy-done.23) | copy-start | bytes 1327108
  214.2 4.9 copy-start.5
  214.2 3.5 copy-start.47
  214.2 3.6 copy-start.1
  261.3 6.4 copy-start.31
  275.0 5.1 copy-start.30
  275.0 5.1 copy-start.32
  280.1 3.2 copy-start.29
  280.1 3.2 copy-start.55
  314.2 4.4 copy-start.13
  357.4 3.1 copy-start.18
  357.4 3.1 copy-start.20
  361.7 5.6 copy-start.42
  363.2 6.9 copy-start.12
  694.4 6.9 copy-start.11
  702.4 3.6 copy-start.4
  723.4 4.0 copy-start.8
  734.4 35.3 %copy-start.48 = (f32[2,8,1152]{2,1,0:T(8,128)S(1)}, f32[2,8,1152]{2,1,0:T(8,128)}, u32[]{:S(2)}) copy-start(f32[2,8,1152]{2,1,0:T(8,128)} %param.17) | copy-start | bytes 221188
  (24 other events, 46.2 us)

commit v2 on v1

--- a/solution.py
+++ b/solution.py
@@ -1,5 +1,6 @@
 import functools
 import math
+import types
 
 import jax
 import jax.numpy as jnp
@@ -13,6 +14,9 @@
 GELU_C = math.sqrt(2.0 / math.pi)
 PRECISE = lax.Precision.HIGHEST
 NEG_FILL = -1e30
+SUB = 16
+CORE, CHIP, PLANE, ALL = range(4)
+GATHER, SPREAD = range(2)
 MESH_ID = pl.DeviceIdType.MESH
 F32 = jnp.float32
 BF16 = jnp.bfloat16
@@ -29,22 +33,22 @@
 
 class Place:
     def __init__(self, n_chip, n_plane):
-        self.n = {"core": 2, "chip": n_chip, "plane": n_plane, "dp": 2 * n_chip}
+        self.n = {CORE: 2, CHIP: n_chip, PLANE: n_plane, ALL: 2 * n_chip}
         self.dp = lax.axis_index("dp")
         self.f = lax.axis_index("fsdp")
         self.c = self.dp // 2
         self.k = self.dp % 2
 
     def index(self, axis):
-        return {"core": self.k, "chip": self.c, "plane": self.f, "dp": self.dp}[axis]
+        return {CORE: self.k, CHIP: self.c, PLANE: self.f, ALL: self.dp}[axis]
 
     def peer(self, axis, step):
         other = xor_of(self.index(axis), step, self.n[axis])
-        if axis == "core":
+        if axis == CORE:
             return other, (self.c * 2 + other, self.f)
-        if axis == "chip":
+        if axis == CHIP:
             return other, (other * 2 + self.k, self.f)
-        if axis == "plane":
+        if axis == PLANE:
             return other, (self.dp, other)
         return other, (other, self.f)
 
@@ -100,13 +104,13 @@
 
 def exchange(name, collective_id, sizes, items):
     n_chip, n_plane = sizes
-    n_of = {"core": 2, "chip": n_chip, "plane": n_plane, "dp": 2 * n_chip}
+    n_of = {CORE: 2, CHIP: n_chip, PLANE: n_plane, ALL: 2 * n_chip}
     axes = sorted({item[0] for item in items})
     outs = []
     n_far = 0
     for axis, kind, array in items:
         n_far += n_of[axis] - 1
-        shape = array.shape if kind == "a2a" else (n_of[axis],) + array.shape
+        shape = array.shape if kind == SPREAD else (n_of[axis],) + array.shape
         outs.append(jax.ShapeDtypeStruct(shape, array.dtype))
 
     def kernel(*refs):
@@ -120,11 +124,11 @@
             mine = place.index(axis)
             for step in range(1, n_of[axis]):
                 other, device = place.peer(axis, step)
-                piece = src if kind == "ag" else src.at[other]
+                piece = src if kind == GATHER else src.at[other]
                 copies.append(wires.far(piece, dst.at[mine], device))
         for (axis, kind, _), src, dst in zip(items, ins, results):
             mine = place.index(axis)
-            copies.append(wires.near(src if kind == "ag" else src.at[mine], dst.at[mine]))
+            copies.append(wires.near(src if kind == GATHER else src.at[mine], dst.at[mine]))
         wait_all(copies)
 
     return pl.pallas_call(
@@ -143,9 +147,9 @@
 
 
 def start_kernel(dims, x, cot, ids, bias, mod, wq, w1, wp, w2):
-    nc, nf = dims["nc"], dims["nf"]
-    per_q, per_1 = dims["per_q"], dims["per_1"]
-    chip_q, chip_1 = dims["chip_q"], dims["chip_1"]
+    nc, nf = dims.nc, dims.nf
+    per_q, per_1 = dims.per_q, dims.per_1
+    chip_q, chip_1 = dims.chip_q, dims.chip_1
     part_q = nc * chip_q
     rows, half = mod.shape[1], mod.shape[2]
     n_far = 5 * (nf - 1) + 3 * (nc - 1) + 4 * (nc - 1) + 4 + 1 + (nc - 1) + (nf - 1) + 1
@@ -171,10 +175,10 @@
         place = Place(nc, nf)
         wires = Wires(send, recv, local)
         c, k, f = place.c, place.k, place.f
-        greet(place, ("core", "chip", "plane"))
-        core_other, core_peer = place.peer("core", 1)
-        chip_peers = [place.peer("chip", step) for step in range(1, nc)]
-        plane_peers = [place.peer("plane", step) for step in range(1, nf)]
+        greet(place, (CORE, CHIP, PLANE))
+        core_other, core_peer = place.peer(CORE, 1)
+        chip_peers = [place.peer(CHIP, step) for step in range(1, nc)]
+        plane_peers = [place.peer(PLANE, step) for step in range(1, nf)]
 
         m_first = wires.far(m_in.at[core_other], m_core, core_peer)
         q_got, f1_got, p_got, f2_got, small = [], [], [], [], []
@@ -267,7 +271,7 @@
 
 
 def sum_small_kernel(dims, terms):
-    nc, nf = dims["nc"], dims["nf"]
+    nc, nf = dims.nc, dims.nf
     _, _, rows, half = terms.shape
     n_far = (nf - 1) + 1 + (nc - 1) + 1
 
@@ -275,11 +279,11 @@
         place = Place(nc, nf)
         wires = Wires(send, recv, local)
         c, k, f = place.c, place.k, place.f
-        greet(place, ("core", "chip", "plane"))
-        core_other, core_peer = place.peer("core", 1)
+        greet(place, (CORE, CHIP, PLANE))
+        core_other, core_peer = place.peer(CORE, 1)
         copies = []
         for step in range(1, nf):
-            other, peer = place.peer("plane", step)
+            other, peer = place.peer(PLANE, step)
             copies.append(wires.far(t_in.at[other], z_got.at[f], peer))
         z_got[f] = t_in[f]
         wait_all(copies)
@@ -291,7 +295,7 @@
         chip_got[c] = both[k] + core_got[...]
         copies = []
         for step in range(1, nc):
-            _, peer = place.peer("chip", step)
+            _, peer = place.peer(CHIP, step)
             copies.append(wires.far(chip_got.at[c], chip_got.at[c], peer))
         wait_all(copies)
         value = chip_got[0]
@@ -320,7 +324,7 @@
 
 
 def cond_kernel(dims, part):
-    nc, nf = dims["nc"], dims["nf"]
+    nc, nf = dims.nc, dims.nf
     nd = 2 * nc
     rows, width = part.shape
     n_far = (nf - 1) + (nd - 1)
@@ -328,10 +332,10 @@
     def kernel(p_in, out, got, send, recv, local):
         place = Place(nc, nf)
         wires = Wires(send, recv, local)
-        greet(place, ("plane", "dp"))
+        greet(place, (PLANE, ALL))
         copies = []
         for step in range(1, nf):
-            copies.append(wires.far(p_in, got.at[place.f], place.peer("plane", step)[1]))
+            copies.append(wires.far(p_in, got.at[place.f], place.peer(PLANE, step)[1]))
         got[place.f] = p_in[...]
         wait_all(copies)
         value = got[0]
@@ -341,7 +345,7 @@
         copies = []
         for step in range(1, nd):
             copies.append(
-                wires.far(out.at[place.dp], out.at[place.dp], place.peer("dp", step)[1])
+                wires.far(out.at[place.dp], out.at[place.dp], place.peer(ALL, step)[1])
             )
         wait_all(copies)
 
@@ -399,6 +403,741 @@
     value = 0.5 * h * (1.0 + t)
     slope = 0.5 * (1.0 + t) + 0.5 * h * (1.0 - t * t) * GELU_C * (1.0 + 3 * 0.044715 * square)
     return value, slope
+
+
+def block_kernel(dims, x, cot, mask, hot, bias, mod, wq, w1, wp, w2):
+    nc, nf = dims.nc, dims.nf
+    own, width = x.shape
+    group = nc * own
+    per_q, rows_d, chip_w = wq.shape
+    per_1, _, ff_d = w1.shape
+    cols_f = w2.shape[0]
+    pad_p = wp.shape[1]
+    step_p = dims.step_p
+    heads = chip_w // HEAD_DIM
+    n_rows = mod.shape[1]
+    n_sub = own // SUB
+    head_scale = HEAD_DIM ** (-0.5)
+
+    outs = (
+        jax.ShapeDtypeStruct((own, width), BF16),
+        jax.ShapeDtypeStruct((own, width), BF16),
+        jax.ShapeDtypeStruct((per_q, rows_d, chip_w), F32),
+        jax.ShapeDtypeStruct((per_1, rows_d, ff_d), F32),
+        jax.ShapeDtypeStruct((rows_d, pad_p), F32),
+        jax.ShapeDtypeStruct((cols_f, ff_d), F32),
+        jax.ShapeDtypeStruct((2, n_rows, width), F32),
+        jax.ShapeDtypeStruct((nc, 8, width), F32),
+    )
+    tokens = (nc, own, width)
+    n_sem = 160
+    scratch = dict(
+        xg=pltpu.VMEM(tokens, BF16),
+        cg=pltpu.VMEM(tokens, BF16),
+        maskg=pltpu.VMEM((nc, own, own), BF16),
+        hotg=pltpu.VMEM((nc, n_sub, 128), F32),
+        biasg=pltpu.VMEM((nf, 8, width), F32),
+        m_core=pltpu.VMEM((n_rows, width), F32),
+        m_chip=pltpu.VMEM((nc, n_rows, width), F32),
+        m_win=pltpu.VMEM((nf, 2, n_rows, width), F32),
+        tab=pltpu.VMEM((3, nc * n_sub, width), F32),
+        own_tab=pltpu.VMEM((6, n_sub, width), F32),
+        q_rows=pltpu.VMEM((nf * per_q, rows_d, chip_w), BF16),
+        f1_rows=pltpu.VMEM((nf * per_1, rows_d, ff_d), BF16),
+        w_q=pltpu.VMEM((3, nc, 2, rows_d, chip_w), BF16),
+        w_1=pltpu.VMEM((2, nc, 2, rows_d, ff_d), BF16),
+        p_got=pltpu.VMEM((2, nf, rows_d, pad_p), BF16),
+        w_p=pltpu.VMEM((chip_w, width), BF16),
+        w_2=pltpu.VMEM((2, nf, cols_f, ff_d), BF16),
+        a_in=pltpu.VMEM(tokens, BF16),
+        qkv=pltpu.VMEM((3, nc, own, chip_w), BF16),
+        probs=pltpu.VMEM((nc * heads, own, own), F32),
+        mixed=pltpu.VMEM((nc, own, chip_w), BF16),
+        sum_s=pltpu.VMEM(tokens, BF16),
+        sum_r=pltpu.VMEM(tokens, BF16),
+        br_s=pltpu.VMEM(tokens, BF16),
+        br_r=pltpu.VMEM(tokens, BF16),
+        m_all=pltpu.VMEM(tokens, BF16),
+        da_all=pltpu.VMEM(tokens, BF16),
+        attn=pltpu.VMEM((own, width), F32),
+        after=pltpu.VMEM((own, width), F32),
+        d_after=pltpu.VMEM((own, width), F32),
+        hid=pltpu.VMEM((2, own, ff_d), F32),
+        slope=pltpu.VMEM((2, own, ff_d), F32),
+        act=pltpu.VMEM((2, nc, own, ff_d), BF16),
+        d_hid=pltpu.VMEM((2, nc, own, ff_d), BF16),
+        dbr=pltpu.VMEM(tokens, BF16),
+        d_qkv=pltpu.VMEM((3, nc, own, chip_w), BF16),
+        g_2=pltpu.VMEM((2, nf, cols_f, ff_d), BF16),
+        g_2r=pltpu.VMEM((nf, cols_f, ff_d), BF16),
+        g_1=pltpu.VMEM((2, nc, 2, rows_d, ff_d), BF16),
+        g_1r=pltpu.VMEM((2, nc, rows_d, ff_d), BF16),
+        g_q=pltpu.VMEM((3, nc, 2, rows_d, chip_w), BF16),
+        g_qr=pltpu.VMEM((3, nc, rows_d, chip_w), BF16),
+        g_p=pltpu.VMEM((2, rows_d, width), BF16),
+        g_pr=pltpu.VMEM((rows_d, width), BF16),
+        z_q=pltpu.VMEM((nf, per_q, rows_d, chip_w), BF16),
+        z_1=pltpu.VMEM((nf, per_1, rows_d, ff_d), BF16),
+        z_p=pltpu.VMEM((nf, rows_d, pad_p), BF16),
+        z_2=pltpu.VMEM((nf, cols_f, ff_d), BF16),
+        sub=pltpu.VMEM((6, n_sub, width), F32),
+        d_mod=pltpu.VMEM((6, n_rows, width), F32),
+        d_bias=pltpu.VMEM((8, width), F32),
+        dz=pltpu.VMEM((nf, 2, n_rows, width), F32),
+        dzb=pltpu.VMEM((nf, 8, width), F32),
+        d_both=pltpu.VMEM((2, n_rows, width), F32),
+        d_bsum=pltpu.VMEM((8, width), F32),
+        d_coreb=pltpu.VMEM((8, width), F32),
+        send=pltpu.SemaphoreType.DMA((n_sem,)),
+        recv=pltpu.SemaphoreType.DMA((n_sem,)),
+        local=pltpu.SemaphoreType.DMA((32,)),
+    )
+    names = list(scratch)
+
+    def kernel(
+        x_in, c_in, mask_in, hot_in, bias_in, mod_in, q_in, f1_in, p_in, f2_in,
+        out, x_grad, o_q, o_1, o_p, o_2, o_mod, o_bias, *rest,
+    ):
+        r = types.SimpleNamespace(**dict(zip(names, rest)))
+        place = Place(nc, nf)
+        wires = Wires(r.send, r.recv, r.local)
+        c, k, f = place.c, place.k, place.f
+        core_o, core_dev = place.peer(CORE, 1)
+        chip_peers = [place.peer(CHIP, step) for step in range(1, nc)]
+        plane_peers = [place.peer(PLANE, step) for step in range(1, nf)]
+
+        def loop(count, body):
+            def run(i, carry):
+                body(i)
+                return carry
+
+            lax.fori_loop(0, count, run, 0)
+
+        def sub_rows(g):
+            return pl.ds(pl.multiple_of(g * SUB, SUB), SUB)
+
+        def chip_send(src, dst, base, step):
+            other, device = place.peer(CHIP, step)
+            return pltpu.make_async_remote_copy(
+                src_ref=src(other),
+                dst_ref=dst.at[c],
+                send_sem=r.send.at[base + step - 1],
+                recv_sem=r.recv.at[base + step - 1],
+                device_id=device,
+                device_id_type=MESH_ID,
+            )
+
+        def reserve(count):
+            base = wires.remote_count
+            wires.remote_count += count
+            return base
+
+        greet(place, (CORE, CHIP, PLANE))
+
+        w_q, q_rows = r.w_q, r.q_rows
+        m_first = wires.far(mod_in.at[core_o], r.m_core, core_dev)
+        q_far = [
+            wires.far(q_in, q_rows.at[pl.ds(f * per_q, per_q)], peer) for _, peer in plane_peers
+        ]
+        first = []
+        for _, peer in chip_peers:
+            first.append(wires.far(hot_in, r.hotg.at[c], peer))
+            first.append(wires.far(x_in, r.xg.at[c], peer))
+            first.append(wires.far(mask_in, r.maskg.at[c], peer))
+        for _, peer in plane_peers:
+            first.append(wires.far(bias_in, r.biasg.at[f], peer))
+        first.append(wires.near(hot_in, r.hotg.at[c]))
+        first.append(wires.near(x_in, r.xg.at[c]))
+        first.append(wires.near(mask_in, r.maskg.at[c]))
+        first.append(wires.near(bias_in, r.biasg.at[f]))
+
+        q_base = reserve(3 * nc)
+        q_local = wires.local_count
+        wires.local_count += 3
+
+        def q_piece(plane, source, at, i):
+            piece = per_q * plane + i
+            kind, chip = piece // nc, piece % nc
+            src = source.at[at]
+            dst = w_q.at[kind, c, k]
+            far = pltpu.make_async_remote_copy(
+                src_ref=src,
+                dst_ref=dst,
+                send_sem=r.send.at[q_base + kind * nc + chip],
+                recv_sem=r.recv.at[q_base + kind * nc + c],
+                device_id=(chip * 2 + k, f),
+                device_id_type=MESH_ID,
+            )
+            near = pltpu.make_async_copy(src, dst, r.local.at[q_local + kind])
+            return chip, far, near
+
+        def q_forward(plane, source, at_of):
+            for i in range(per_q):
+                chip, far, near = q_piece(plane, source, at_of(i), i)
+
+                @pl.when(chip != c)
+                def _():
+                    far.start()
+
+                @pl.when(chip == c)
+                def _():
+                    near.start()
+
+        q_forward(f, q_in, lambda i: i)
+        m_first.wait()
+        m_chip = r.m_chip
+        m_chip[c] = mod_in[k] + r.m_core[...]
+        m_second = [wires.far(m_chip.at[c], m_chip.at[c], peer) for _, peer in chip_peers]
+        q_forward_order = []
+        for step, copy in enumerate(q_far, 1):
+            copy.wait_recv()
+            plane = xor_of(f, step, nf)
+            q_forward(plane, q_rows, lambda i: per_q * plane + i)
+            if step == 1:
+                wait_all(m_second)
+                total = m_chip[0]
+                for other in range(1, nc):
+                    total = total + m_chip[other]
+                r.m_win[f, k] = total
+                m_third = [
+                    wires.far(r.m_win.at[f, k], r.m_win.at[f, k], peer)
+                    for _, peer in plane_peers
+                ]
+        p_far = [wires.far(p_in, r.p_got.at[k, f], peer) for _, peer in plane_peers]
+        f1_rows = r.f1_rows
+        f1_far = [
+            wires.far(f1_in, f1_rows.at[pl.ds(f * per_1, per_1)], peer) for _, peer in plane_peers
+        ]
+        f2_far = [wires.far(f2_in, r.w_2.at[k, f], peer) for _, peer in plane_peers]
+        p_far.append(wires.near(p_in, r.p_got.at[k, f]))
+        f1_far.append(wires.near(f1_in, f1_rows.at[pl.ds(f * per_1, per_1)]))
+        f2_far.append(wires.near(f2_in, r.w_2.at[k, f]))
+        wait_all(m_third)
+        m_last = wires.far(r.m_win.at[:, k], r.m_win.at[:, k], core_dev)
+        for copy in q_far:
+            copy.wait_send()
+        q_core = []
+        for kind in range(3):
+            for other, _ in chip_peers:
+                pltpu.make_async_remote_copy(
+                    src_ref=w_q.at[kind, other, k],
+                    dst_ref=w_q.at[kind, other, k],
+                    send_sem=r.send.at[q_base + kind * nc + other],
+                    recv_sem=r.recv.at[q_base + kind * nc + other],
+                    device_id=core_dev,
+                    device_id_type=MESH_ID,
+                ).wait()
+            pltpu.make_async_copy(
+                w_q.at[kind, c, k], w_q.at[kind, c, k], r.local.at[q_local + kind]
+            ).wait()
+            q_core.append(wires.far(w_q.at[kind, :, k], w_q.at[kind, :, k], core_dev))
+
+        wait_all(first)
+        m_last.wait()
+        hot_rows = r.hotg[...].reshape(nc * n_sub, 128)[:, :n_rows]
+        places = lax.broadcasted_iota(jnp.int32, (nc * n_sub, n_rows), 1).astype(F32)
+        hot_of = jnp.where(hot_rows == places, 1.0, 0.0)
+        own_hot = r.hotg[c][:, :n_rows]
+        own_hot = jnp.where(
+            own_hot == lax.broadcasted_iota(jnp.int32, (n_sub, n_rows), 1).astype(F32), 1.0, 0.0
+        )
+        starts = [6 * plane // nf for plane in range(nf)]
+        for kind in range(6):
+            value = None
+            for plane in range(nf):
+                if 0 <= kind - starts[plane] < 2:
+                    term = r.m_win[plane, kind - starts[plane]]
+                    value = term if value is None else value + term
+            if kind in (0, 1, 5):
+                r.tab[kind % 3] = jnp.dot(hot_of, value, precision=PRECISE, preferred_element_type=F32)
+            r.own_tab[kind] = jnp.dot(own_hot, value, precision=PRECISE, preferred_element_type=F32)
+
+        def tab_row(kind, blk, g):
+            return r.tab[kind % 3, pl.ds(blk * n_sub + g, 1), :]
+
+        def own_row(kind, g):
+            return r.own_tab[kind, pl.ds(g, 1), :]
+
+        def make_a(blk):
+            def body(g):
+                rows = sub_rows(g)
+                normal, _ = ln_parts(r.xg[blk, rows, :].astype(F32))
+                value = normal * (1.0 + tab_row(1, blk, g)) + tab_row(0, blk, g)
+                r.a_in[blk, rows, :] = value.astype(BF16)
+
+            loop(n_sub, body)
+
+        loop(nc, make_a)
+        c_far = [wires.far(c_in, r.cg.at[c], peer) for _, peer in chip_peers]
+        c_far.append(wires.near(c_in, r.cg.at[c]))
+
+        wait_all(p_far)
+        p_core = wires.far(r.p_got.at[k], r.p_got.at[k], core_dev)
+        wait_all(q_core)
+        p_core.wait()
+        blocks_p = width // 128
+        for half in range(2):
+            for j in range(blocks_p):
+                value = None
+                for plane in range(nf):
+                    at = j * 128 - plane * step_p
+                    if 0 <= at < pad_p:
+                        term = r.p_got[half, plane, :, at : at + 128]
+                        value = term if value is None else value + term
+                r.w_p[half * rows_d : (half + 1) * rows_d, j * 128 : (j + 1) * 128] = value
+        lane = lax.broadcasted_iota(jnp.int32, (1, chip_w), 1)
+        head_of = [
+            jnp.where((lane >= HEAD_DIM * h) & (lane < HEAD_DIM * (h + 1)), 1.0, 0.0).astype(BF16)
+            for h in range(heads)
+        ]
+
+        def weight_q(kind):
+            return w_q[kind].reshape(width, chip_w)
+
+        b_row = pl.ds(2 + c % 2, 1)
+        bias_q = r.biasg[c // 2, b_row, pl.ds(0, chip_w)]
+        bias_v = r.biasg[nc // 2 + c // 2, b_row, pl.ds(0, chip_w)]
+        sum_base = reserve(nc - 1)
+        sum_s, sum_r = r.sum_s, r.sum_r
+
+        def attend(i):
+            step = (i + 1) % nc
+            blk = xor_of(c, step, nc)
+            a_now = r.a_in[blk]
+            r.qkv[0, blk] = (dot(a_now, weight_q(0)) + bias_q).astype(BF16)
+            r.qkv[1, blk] = dot(a_now, weight_q(1)).astype(BF16)
+            r.qkv[2, blk] = (dot(a_now, weight_q(2)) + bias_v).astype(BF16)
+            q_now, k_now, v_now = r.qkv[0, blk], r.qkv[1, blk], r.qkv[2, blk]
+            same = r.maskg[blk].astype(F32) > 0.5
+            mixed = jnp.zeros((own, chip_w), F32)
+            for h in range(heads):
+                scores = dot_rt(q_now * head_of[h], k_now) * head_scale
+                scores = jnp.where(same, scores, NEG_FILL)
+                raised = jnp.exp(scores - jnp.max(scores, axis=-1, keepdims=True))
+                share = raised / jnp.sum(raised, axis=-1, keepdims=True)
+                r.probs[blk * heads + h] = share
+                mixed = mixed + dot(share.astype(BF16), v_now * head_of[h])
+            mixed = mixed.astype(BF16)
+            r.mixed[blk] = mixed
+            part = dot(mixed, r.w_p[...]).astype(BF16)
+
+            @pl.when(step != 0)
+            def _():
+                sum_s[blk] = part
+                chip_send(lambda other: sum_s.at[other], sum_r, sum_base, step).start()
+
+            @pl.when(step == 0)
+            def _():
+                sum_r[c] = part
+
+        loop(nc, attend)
+
+        wait_all(f1_far)
+        f1_moved = [
+            wires.far(f1_rows.at[pl.ds(other * per_1, per_1)], r.w_1.at[:, c, k], peer)
+            for other, peer in chip_peers
+        ]
+        f1_moved.append(
+            wires.near(f1_rows.at[pl.ds(c * per_1, per_1)], r.w_1.at[:, c, k])
+        )
+
+        for step in range(1, nc):
+            chip_send(lambda other: sum_s.at[other], sum_r, sum_base, step).wait()
+        bias_p = r.biasg[0, 0:1, :]
+        bias_o = r.biasg[0, 1:2, :]
+        for plane in range(1, nf):
+            bias_p = bias_p + r.biasg[plane, 0:1, :]
+            bias_o = bias_o + r.biasg[plane, 1:2, :]
+
+        def after_attention(g):
+            rows = sub_rows(g)
+            value = sum_r[0, rows, :].astype(F32)
+            for other in range(1, nc):
+                value = value + sum_r[other, rows, :].astype(F32)
+            value = value + bias_p
+            r.attn[rows, :] = value
+            after = r.xg[c, rows, :].astype(F32) + own_row(2, g) * value
+            r.after[rows, :] = after
+            normal, _ = ln_parts(after)
+            r.m_all[c, rows, :] = (normal * (1.0 + own_row(4, g)) + own_row(3, g)).astype(BF16)
+
+        loop(n_sub, after_attention)
+        m_all = r.m_all
+        m_base = reserve(nc - 1)
+        for step in range(1, nc):
+            chip_send(lambda other: m_all.at[c], m_all, m_base, step).start()
+
+        wait_all(f1_moved)
+        f1_core = wires.far(r.w_1.at[:, :, k], r.w_1.at[:, :, k], core_dev)
+        wait_all(c_far)
+
+        def make_dbr(blk):
+            def body(g):
+                rows = sub_rows(g)
+                value = r.cg[blk, rows, :].astype(F32) * tab_row(5, blk, g)
+                r.dbr[blk, rows, :] = value.astype(BF16)
+
+            loop(n_sub, body)
+
+        loop(nc, make_dbr)
+        f1_core.wait()
+        wait_all(f2_far)
+        wires.far(r.w_2.at[k], r.w_2.at[k], core_dev).wait()
+
+        def weight_1(h):
+            return r.w_1[h].reshape(width, ff_d)
+
+        def weight_2(h):
+            return r.w_2[h].reshape(width, ff_d)
+
+        dm_base = reserve(nc - 1)
+        br_base = reserve(nc - 1)
+        dm_s, dm_r, br_s, br_r = sum_s, sum_r, r.br_s, r.br_r
+
+        def feed(step):
+            blk = xor_of(c, step, nc)
+
+            @pl.when(step != 0)
+            def _():
+                chip_send(lambda other: m_all.at[c], m_all, m_base, step).wait_recv()
+
+            m_now = m_all[blk]
+            for h in range(2):
+                bias_1 = r.biasg[c, 4 + h : 5 + h, pl.ds(0, ff_d)]
+                r.hid[h] = dot(m_now, weight_1(h)) + bias_1
+
+            def gelu_rows(g):
+                rows = sub_rows(g)
+                for h in range(2):
+                    value, slope = gelu_both(r.hid[h, rows, :])
+                    r.act[h, blk, rows, :] = value.astype(BF16)
+                    r.slope[h, rows, :] = slope
+
+            loop(n_sub, gelu_rows)
+            d_now = r.dbr[blk]
+            for h in range(2):
+                r.hid[h] = dot(d_now, weight_2(h))
+
+            def back_rows(g):
+                rows = sub_rows(g)
+                for h in range(2):
+                    value = r.hid[h, rows, :] * r.slope[h, rows, :]
+                    r.d_hid[h, blk, rows, :] = value.astype(BF16)
+
+            loop(n_sub, back_rows)
+            part = dot_rt(r.d_hid[0, blk], weight_1(0)) + dot_rt(r.d_hid[1, blk], weight_1(1))
+            part = part.astype(BF16)
+
+            @pl.when(step != 0)
+            def _():
+                dm_s[blk] = part
+                chip_send(lambda other: dm_s.at[other], dm_r, dm_base, step).start()
+
+            @pl.when(step == 0)
+            def _():
+                dm_r[c] = part
+
+            part2 = dot_rt(r.act[0, blk], weight_2(0)) + dot_rt(r.act[1, blk], weight_2(1))
+            part2 = part2.astype(BF16)
+
+            @pl.when(step != 0)
+            def _():
+                br_s[blk] = part2
+                chip_send(lambda other: br_s.at[other], br_r, br_base, step).start()
+
+            @pl.when(step == 0)
+            def _():
+                br_r[c] = part2
+
+        loop(nc, feed)
+        for step in range(1, nc):
+            chip_send(lambda other: m_all.at[c], m_all, m_base, step).wait_send()
+
+        dbr_all = r.dbr[...].reshape(group, width)
+
+        def column_cuts(count):
+            return [(at, min(at + 256, count)) for at in range(0, count, 256)]
+
+        for lo, hi in column_cuts(ff_d):
+            value = dot_lt(dbr_all, r.act[core_o, :, :, lo:hi].reshape(group, hi - lo))
+            r.g_2[core_o, :, :, lo:hi] = value.astype(BF16).reshape(nf, cols_f, hi - lo)
+        g2_core = wires.far(r.g_2.at[core_o], r.g_2r, core_dev)
+        g2_core.wait()
+        for lo, hi in column_cuts(ff_d):
+            value = dot_lt(dbr_all, r.act[k, :, :, lo:hi].reshape(group, hi - lo))
+            value = value.reshape(nf, cols_f, hi - lo) + r.g_2r[:, :, lo:hi].astype(F32)
+            r.g_2[k, :, :, lo:hi] = value.astype(BF16)
+        z2_far = [
+            wires.far(r.g_2.at[k, other], r.z_2.at[f], peer) for other, peer in plane_peers
+        ]
+
+        for step in range(1, nc):
+            chip_send(lambda other: dm_s.at[other], dm_r, dm_base, step).wait()
+        da_all = r.da_all
+
+        def back_norm2(g):
+            rows = sub_rows(g)
+            d_m = dm_r[0, rows, :].astype(F32)
+            for other in range(1, nc):
+                d_m = d_m + dm_r[other, rows, :].astype(F32)
+            normal, scale = ln_parts(r.after[rows, :])
+            cot_now = r.cg[c, rows, :].astype(F32)
+            d_after = cot_now + ln_back(normal, scale, d_m * (1.0 + own_row(4, g)))
+            r.d_after[rows, :] = d_after
+            da_all[c, rows, :] = (own_row(2, g) * d_after).astype(BF16)
+            at = pl.ds(g, 1)
+            r.sub[3, at, :] = jnp.sum(d_m, axis=0, keepdims=True)
+            r.sub[4, at, :] = jnp.sum(d_m * normal, axis=0, keepdims=True)
+            r.sub[2, at, :] = jnp.sum(d_after * r.attn[rows, :], axis=0, keepdims=True)
+
+        loop(n_sub, back_norm2)
+        da_base = reserve(nc - 1)
+        for step in range(1, nc):
+            chip_send(lambda other: da_all.at[c], da_all, da_base, step).start()
+
+        m_rows = m_all[...].reshape(group, width)
+        for h in range(2):
+            for lo, hi in column_cuts(ff_d):
+                value = dot_lt(m_rows, r.d_hid[h, :, :, lo:hi].reshape(group, hi - lo))
+                r.g_1[h, :, :, :, lo:hi] = value.astype(BF16).reshape(nc, 2, rows_d, hi - lo)
+        g1_core = wires.far(r.g_1.at[:, :, core_o], r.g_1r, core_dev)
+
+        for step in range(1, nc):
+            chip_send(lambda other: br_s.at[other], br_r, br_base, step).wait()
+
+        def finish_out(g):
+            rows = sub_rows(g)
+            branch = br_r[0, rows, :].astype(F32)
+            for other in range(1, nc):
+                branch = branch + br_r[other, rows, :].astype(F32)
+            branch = branch + bias_o
+            out[rows, :] = (r.after[rows, :] + own_row(5, g) * branch).astype(BF16)
+            cot_now = r.cg[c, rows, :].astype(F32)
+            r.sub[5, pl.ds(g, 1), :] = jnp.sum(cot_now * branch, axis=0, keepdims=True)
+
+        loop(n_sub, finish_out)
+        g1_core.wait()
+        for h in range(2):
+            for chip in range(nc):
+                value = r.g_1[h, chip, k].astype(F32) + r.g_1r[h, chip].astype(F32)
+                r.g_1[h, chip, k] = value.astype(BF16)
+        f1_rows[pl.ds(per_1 * c, per_1)] = r.g_1[:, c, k]
+        y1_far = [
+            wires.far(r.g_1.at[:, other, k], f1_rows.at[pl.ds(per_1 * c, per_1)], peer)
+            for other, peer in chip_peers
+        ]
+
+        back_base = reserve(nc - 1)
+
+        def attend_back(step):
+            blk = xor_of(c, step, nc)
+
+            @pl.when(step != 0)
+            def _():
+                chip_send(lambda other: da_all.at[c], da_all, da_base, step).wait_recv()
+
+            d_mix = dot_rt(da_all[blk], r.w_p[...]).astype(BF16)
+            q_now, k_now, v_now = r.qkv[0, blk], r.qkv[1, blk], r.qkv[2, blk]
+            d_q = jnp.zeros((own, chip_w), F32)
+            d_k = jnp.zeros((own, chip_w), F32)
+            d_v = jnp.zeros((own, chip_w), F32)
+            for h in range(heads):
+                d_mix_h = d_mix * head_of[h]
+                share = r.probs[blk * heads + h]
+                d_share = dot_rt(d_mix_h, v_now)
+                d_score = share * (d_share - jnp.sum(share * d_share, axis=-1, keepdims=True))
+                d_score = d_score.astype(BF16)
+                d_q = d_q + dot(d_score, k_now * head_of[h])
+                d_k = d_k + dot_lt(d_score, q_now * head_of[h])
+                d_v = d_v + dot_lt(share.astype(BF16), d_mix_h)
+            d_q = (d_q * head_scale).astype(BF16)
+            d_k = (d_k * head_scale).astype(BF16)
+            d_v = d_v.astype(BF16)
+            r.d_qkv[0, blk] = d_q
+            r.d_qkv[1, blk] = d_k
+            r.d_qkv[2, blk] = d_v
+            part = dot_rt(d_q, weight_q(0)) + dot_rt(d_k, weight_q(1)) + dot_rt(d_v, weight_q(2))
+            part = part.astype(BF16)
+
+            @pl.when(step != 0)
+            def _():
+                sum_s[blk] = part
+                chip_send(lambda other: sum_s.at[other], sum_r, back_base, step).start()
+
+            @pl.when(step == 0)
+            def _():
+                sum_r[c] = part
+
+        loop(nc, attend_back)
+        for step in range(1, nc):
+            chip_send(lambda other: da_all.at[c], da_all, da_base, step).wait_send()
+
+        wait_all(y1_far)
+        z1_far = [
+            wires.far(f1_rows.at[pl.ds(per_1 * other, per_1)], r.z_1.at[f], peer)
+            for other, peer in plane_peers
+        ]
+
+        a_rows = r.a_in[...].reshape(group, width)
+        q_core_back = []
+        for kind in range(3):
+            for lo, hi in column_cuts(chip_w):
+                value = dot_lt(a_rows, r.d_qkv[kind, :, :, lo:hi].reshape(group, hi - lo))
+                r.g_q[kind, :, :, :, lo:hi] = value.astype(BF16).reshape(nc, 2, rows_d, hi - lo)
+            q_core_back.append(wires.far(r.g_q.at[kind, :, core_o], r.g_qr.at[kind], core_dev))
+        da_rows = da_all[...].reshape(group, width)
+        value = dot_lt(r.mixed[...].reshape(group, chip_w), da_rows).astype(BF16)
+        r.g_p[...] = value.reshape(2, rows_d, width)
+        p_core_back = wires.far(r.g_p.at[core_o], r.g_pr, core_dev)
+        yq_far = []
+        for kind in range(3):
+            q_core_back[kind].wait()
+            for chip in range(nc):
+                value = r.g_q[kind, chip, k].astype(F32) + r.g_qr[kind, chip].astype(F32)
+                r.g_q[kind, chip, k] = value.astype(BF16)
+            q_rows[kind * nc + c] = r.g_q[kind, c, k]
+            for other, peer in chip_peers:
+                yq_far.append(
+                    wires.far(r.g_q.at[kind, other, k], q_rows.at[kind * nc + c], peer)
+                )
+        p_core_back.wait()
+        r.g_p[k] = (r.g_p[k].astype(F32) + r.g_pr[...].astype(F32)).astype(BF16)
+        zp_far = [
+            wires.far(
+                r.g_p.at[k, :, pl.ds(pl.multiple_of(other * step_p, 128), pad_p)],
+                r.z_p.at[f],
+                peer,
+            )
+            for other, peer in plane_peers
+        ]
+
+        for step in range(1, nc):
+            chip_send(lambda other: sum_s.at[other], sum_r, back_base, step).wait()
+
+        def back_norm1(g):
+            rows = sub_rows(g)
+            d_a = sum_r[0, rows, :].astype(F32)
+            for other in range(1, nc):
+                d_a = d_a + sum_r[other, rows, :].astype(F32)
+            normal, scale = ln_parts(r.xg[c, rows, :].astype(F32))
+            value = r.d_after[rows, :] + ln_back(normal, scale, d_a * (1.0 + own_row(1, g)))
+            x_grad[rows, :] = value.astype(BF16)
+            at = pl.ds(g, 1)
+            r.sub[0, at, :] = jnp.sum(d_a, axis=0, keepdims=True)
+            r.sub[1, at, :] = jnp.sum(d_a * normal, axis=0, keepdims=True)
+
+        loop(n_sub, back_norm1)
+        for kind in range(6):
+            r.d_mod[kind] = lax.dot_general(
+                own_hot, r.sub[kind], (((0,), (0,)), ((), ())),
+                precision=PRECISE, preferred_element_type=F32,
+            )
+        ones_own = jnp.ones((8, own), BF16)
+        ones_all = jnp.ones((8, group), BF16)
+        r.d_bias[...] = jnp.zeros((8, width), F32)
+        r.d_bias[0:1, :] = dot(ones_own, da_all[c])[0:1]
+        r.d_bias[1:2, :] = dot(ones_own, r.dbr[c])[0:1]
+        for at, kind in ((2, 0), (3, 2)):
+            sums = dot(ones_all, r.d_qkv[kind].reshape(group, chip_w))
+            r.d_bias[at : at + 1, 0:chip_w] = sums[0:1]
+        for h in range(2):
+            sums = dot(ones_all, r.d_hid[h].reshape(group, ff_d))
+            r.d_bias[4 + h : 5 + h, 0:ff_d] = sums[0:1]
+
+        small = []
+        for other, peer in plane_peers:
+            small.append(
+                wires.far(r.d_mod.at[pl.ds(6 * other // nf, 2)], r.dz.at[f], peer)
+            )
+            small.append(wires.far(r.d_bias, r.dzb.at[f], peer))
+        wait_all(yq_far)
+        zq_far = [
+            wires.far(q_rows.at[pl.ds(per_q * other, per_q)], r.z_q.at[f], peer)
+            for other, peer in plane_peers
+        ]
+        r.dz[f] = r.d_mod[pl.ds(6 * f // nf, 2)]
+        r.dzb[f] = r.d_bias[...]
+        wait_all(small)
+        value, value_b = r.dz[0], r.dzb[0]
+        for plane in range(1, nf):
+            value = value + r.dz[plane]
+            value_b = value_b + r.dzb[plane]
+        r.d_both[...] = value
+        r.d_bsum[...] = value_b
+        small = [
+            wires.far(r.d_both.at[core_o], r.m_core, core_dev),
+            wires.far(r.d_bsum, r.d_coreb, core_dev),
+        ]
+        wait_all(small)
+        m_chip[c] = r.d_both[k] + r.m_core[...]
+        o_bias[c] = r.d_bsum[...] + r.d_coreb[...]
+        small = []
+        for _, peer in chip_peers:
+            small.append(wires.far(m_chip.at[c], m_chip.at[c], peer))
+            small.append(wires.far(o_bias.at[c], o_bias.at[c], peer))
+
+        wait_all(z2_far)
+        r.z_2[f] = r.g_2[k, f]
+        total = r.z_2[0].astype(F32)
+        for plane in range(1, nf):
+            total = total + r.z_2[plane].astype(F32)
+        o_2[...] = total
+        wait_all(z1_far)
+        r.z_1[f] = f1_rows[pl.ds(per_1 * f, per_1)]
+        total = r.z_1[0].astype(F32)
+        for plane in range(1, nf):
+            total = total + r.z_1[plane].astype(F32)
+        o_1[...] = total
+        wait_all(small)
+        value = m_chip[0]
+        for chip in range(1, nc):
+            value = value + m_chip[chip]
+        o_mod[k] = value
+        m_end = wires.far(o_mod.at[k], o_mod.at[k], core_dev)
+        wait_all(zp_far)
+        for plane in range(nf):
+
+            @pl.when(f == plane)
+            def _():
+                r.z_p[plane] = r.g_p[k, :, plane * step_p : plane * step_p + pad_p]
+
+        total = r.z_p[0].astype(F32)
+        for plane in range(1, nf):
+            total = total + r.z_p[plane].astype(F32)
+        o_p[...] = total
+        wait_all(zq_far)
+        r.z_q[f] = q_rows[pl.ds(per_q * f, per_q)]
+        total = r.z_q[0].astype(F32)
+        for plane in range(1, nf):
+            total = total + r.z_q[plane].astype(F32)
+        o_q[...] = total
+        m_end.wait()
+        assert wires.remote_count <= n_sem and wires.local_count <= 32
+
+    return pl.pallas_call(
+        kernel,
+        out_shape=outs,
+        in_specs=[ANYWHERE] * 5 + [ON_CHIP] + [ANYWHERE] * 4,
+        out_specs=tuple([ON_CHIP] * len(outs)),
+        scratch_shapes=list(scratch.values()),
+        compiler_params=pltpu.CompilerParams(
+            collective_id=0, has_side_effects=True, vmem_limit_bytes=63 * 2**20
+        ),
+        name="block",
+    )(x, cot, mask, hot, bias, mod, wq, w1, wp, w2)
+
+
+def fits_block(n_dp, nf, width, ff, own, micro):
+    nc = n_dp // 2
+    return (
+        nc == nf
+        and nf == 4
+        and width % (128 * nf) == 128
+        and ff == 4 * width
+        and (width // n_dp) % 16 == 0
+        and (width // nc) % HEAD_DIM == 0
+        and own % (2 * SUB) == 0
+    )
 
 
 def per_device(
@@ -417,7 +1156,7 @@
     chip_w = width // nc
     piece_q = math.gcd(3 * width // nf, chip_w)
     piece_1 = math.gcd(ff // nf, ff_d)
-    dims = dict(
+    dims = types.SimpleNamespace(
         nc=nc,
         nf=nf,
         per_q=3 * width // nf // piece_q,
@@ -429,8 +1168,8 @@
     f = lax.axis_index("fsdp")
     c, k = dp // 2, dp % 2
 
-    q_send = w_qkv.reshape(rows_d, dims["per_q"], piece_q).transpose(1, 0, 2)
-    f1_send = w_fc1.reshape(rows_d, dims["per_1"], piece_1).transpose(1, 0, 2)
+    q_send = w_qkv.reshape(rows_d, dims.per_q, piece_q).transpose(1, 0, 2)
+    f1_send = w_fc1.reshape(rows_d, dims.per_1, piece_1).transpose(1, 0, 2)
     f2_send = w_fc2.T
     cond = conditioning.reshape(micro * clips, width)
     silu_cond = jax.nn.silu(cond)
@@ -439,6 +1178,77 @@
     silu_part = lax.dynamic_slice_in_dim(silu_low, dp * rows_d, rows_d, 1)
     mod_part = dot(silu_part, w_ada) + jnp.where(dp == 0, b_ada.astype(F32), 0.0)[None]
     mod_send = mod_part.reshape(-1, 2, ada_w // 2).transpose(1, 0, 2)
+    cut = [0, 2 * cols_f, 3 * cols_f, 3 * cols_f + ff // nf, 4 * cols_f + ff // nf]
+    cond_own = lax.dynamic_slice_in_dim(cond, f * cols_f, cols_f, 1)
+
+    def ada_outputs(d_cols):
+        grad_w_ada = precise(silu_part.astype(F32), d_cols, ((0,), (0,)))
+        d_silu_part = precise(d_cols, w_ada.astype(F32), ((1,), (1,)))
+        d_silu = cond_kernel(dims, d_silu_part).transpose(1, 0, 2).reshape(micro * clips, width)
+        d_silu_own = lax.dynamic_slice_in_dim(d_silu, f * cols_f, cols_f, 1)
+        _, silu_back = jax.vjp(jax.nn.silu, cond_own)
+        cond_grad = silu_back(d_silu_own)[0].reshape(micro, clips, cols_f)
+        return cond_grad, grad_w_ada, jnp.sum(d_cols, axis=0)
+
+    if fits_block(n_dp, nf, width, ff, own, micro):
+        n_rows = micro * clips
+        window = f * ada_w - 6 * f // nf * width
+        pad_p = width // nf // 128 * 128 + 128
+        dims.step_p = (width - pad_p) // (nf - 1)
+        shift_p = f * (cols_f - dims.step_p)
+
+        def lanes(value, start):
+            empty = jnp.zeros(value.shape[:-1] + (width,), F32)
+            return lax.dynamic_update_slice_in_dim(empty, value.astype(F32), start, value.ndim - 1)
+
+        mod_send = jnp.zeros((n_rows, 2 * width), F32)
+        mod_send = lax.dynamic_update_slice_in_dim(mod_send, mod_part, window, 1)
+        mod_send = mod_send.reshape(n_rows, 2, width).transpose(1, 0, 2)
+        p_send = jnp.zeros((rows_d, pad_p), BF16)
+        p_send = lax.dynamic_update_slice_in_dim(p_send, w_proj, shift_p, 1)
+        bias_send = jnp.concatenate(
+            [
+                lanes(b_proj[None], f * cols_f),
+                lanes(b_fc2[None], f * cols_f),
+                lanes(b_qv.reshape(2, chip_w), 0),
+                lanes(b_fc1.reshape(2, ff_d), 0),
+                jnp.zeros((2, width), F32),
+            ]
+        )
+        frames = frame_of_slot + jnp.arange(micro, dtype=jnp.int32)[:, None] * 65536
+        frames = frames.reshape(own)
+        mask = (frames[:, None] == frames[None, :]).astype(BF16)
+        row = clip_of_slot + jnp.arange(micro, dtype=jnp.int32)[:, None] * clips
+        row = row.reshape(own // SUB, SUB)[:, :1].astype(F32)
+        hot = jnp.broadcast_to(row, (own // SUB, 128))
+        output, input_grad, o_q, o_1, o_p, o_2, o_mod, o_bias = block_kernel(
+            dims, patches.reshape(own, width), cotangent.reshape(own, width), mask, hot, bias_send,
+            mod_send, q_send, f1_send, p_send, f2_send,
+        )
+        d_cols = o_mod.transpose(1, 0, 2).reshape(n_rows, 2 * width)
+        d_cols = lax.dynamic_slice_in_dim(d_cols, window, ada_w, 1)
+        cond_grad, grad_w_ada, grad_b_ada = ada_outputs(d_cols)
+        own_bias = jnp.sum(o_bias[:, :2], axis=0)
+        own_bias = lax.dynamic_slice_in_dim(own_bias, f * cols_f, cols_f, 1)
+        qv = jnp.concatenate([o_bias[:, 2, :chip_w], o_bias[:, 3, :chip_w]])
+        qv = lax.dynamic_slice_in_dim(qv, 2 * f, 2, 0).reshape(2 * chip_w)
+        fc1 = lax.dynamic_index_in_dim(o_bias[:, 4:6, :ff_d], f, 0, False).reshape(2 * ff_d)
+        return (
+            output.reshape(patches.shape),
+            input_grad.reshape(patches.shape),
+            cond_grad,
+            grad_w_ada,
+            grad_b_ada,
+            o_q.transpose(1, 0, 2).reshape(rows_d, 3 * width // nf),
+            qv,
+            lax.dynamic_slice_in_dim(o_p, shift_p, cols_f, 1),
+            own_bias[0],
+            o_1.transpose(1, 0, 2).reshape(rows_d, ff // nf),
+            fc1,
+            o_2.T,
+            own_bias[1],
+        )
+
     ids = jnp.stack([frame_of_slot.reshape(own), clip_of_slot.reshape(own)])
     ids = jnp.concatenate([ids, jnp.zeros((6, own), jnp.int32)])
     bias_send = jnp.concatenate([b_qv, b_proj, b_fc1, b_fc2]).astype(F32)[None]
@@ -450,13 +1260,12 @@
     group = nc * own
     modulation = mod_all.transpose(2, 0, 1, 3).reshape(micro * clips, 6 * width)
     q_parts = [
-        q_chip[i].reshape(nc, 2, dims["chip_q"], rows_d, piece_q).transpose(0, 1, 3, 2, 4).reshape(width, chip_w)
+        q_chip[i].reshape(nc, 2, dims.chip_q, rows_d, piece_q).transpose(0, 1, 3, 2, 4).reshape(width, chip_w)
         for i in range(3)
     ]
     w1 = f1_chip.transpose(1, 2, 3, 0, 4).reshape(width, ff // nc)
     wp = p_chip.transpose(0, 2, 1, 3).reshape(chip_w, width)
     w2t = f2_chip.reshape(2, width, ff_d).transpose(1, 0, 2).reshape(width, 2 * ff_d)
-    cut = [0, 2 * cols_f, 3 * cols_f, 3 * cols_f + ff // nf, 4 * cols_f + ff // nf]
     b_parts = [bias_all[:, 0, a:b].reshape(-1) for a, b in zip(cut[:-1], cut[1:])]
     bq = lax.dynamic_slice_in_dim(b_parts[0], c * chip_w, chip_w, 0)
     bv = lax.dynamic_slice_in_dim(b_parts[0], width + c * chip_w, chip_w, 0)
@@ -498,14 +1307,14 @@
     mixed = mixed.reshape(group, chip_w).astype(BF16)
     attn_part = dot(mixed, wp)
     (attn_got,) = exchange(
-        "attn_sum", 3, sizes, [("chip", "a2a", attn_part.astype(BF16).reshape(nc, own, width))]
+        "attn_sum", 3, sizes, [(CHIP, SPREAD, attn_part.astype(BF16).reshape(nc, own, width))]
     )
     attn = jnp.sum(attn_got.astype(F32), axis=0) + b_parts[1][None]
     x_own = patches.reshape(own, width).astype(F32)
     after = x_own + gate1 * attn
     norm2, rstd2 = ln_parts(after)
     m_own = (norm2 * (1.0 + scale2) + shift2).astype(BF16)
-    (m_all,) = exchange("m_gather", 4, sizes, [("chip", "ag", m_own)])
+    (m_all,) = exchange("m_gather", 4, sizes, [(CHIP, GATHER, m_own)])
     m_in = m_all.reshape(group, width)
 
     hidden = dot(m_in, w1) + b1[None]
@@ -523,8 +1332,8 @@
         5,
         sizes,
         [
-            ("chip", "a2a", d_m_part.astype(BF16).reshape(nc, own, width)),
-            ("chip", "a2a", branch_part.astype(BF16).reshape(nc, own, width)),
+            (CHIP, SPREAD, d_m_part.astype(BF16).reshape(nc, own, width)),
+            (CHIP, SPREAD, branch_part.astype(BF16).reshape(nc, own, width)),
         ],
     )[::-1]
     branch = jnp.sum(branch_got.astype(F32), axis=0) + b_parts[3][None]
@@ -533,7 +1342,7 @@
     cot_own = cotangent.reshape(own, width).astype(F32)
     d_after = cot_own + ln_back(norm2, rstd2, d_m * (1.0 + scale2))
     d_attn = (gate1 * d_after).astype(BF16)
-    (d_attn_all,) = exchange("d_attn_gather", 6, sizes, [("chip", "ag", d_attn)])
+    (d_attn_all,) = exchange("d_attn_gather", 6, sizes, [(CHIP, GATHER, d_attn)])
     d_attn_group = d_attn_all.reshape(group, width)
     grad_p = dot_lt(mixed, d_attn_group)
     d_mix = dot_rt(d_attn_group, wp).astype(BF16).reshape(blocks, block, heads, HEAD_DIM)
@@ -547,23 +1356,23 @@
     d_a_part = sum(dot_rt(t, w) for t, w in zip(dqkv, q_parts))
     grad_q = jnp.stack([dot_lt(a_in, t) for t in dqkv])
     (d_a_got,) = exchange(
-        "d_a_sum", 7, sizes, [("chip", "a2a", d_a_part.astype(BF16).reshape(nc, own, width))]
+        "d_a_sum", 7, sizes, [(CHIP, SPREAD, d_a_part.astype(BF16).reshape(nc, own, width))]
     )
     d_a = jnp.sum(d_a_got.astype(F32), axis=0)
     norm1_own, rstd1_own = ln_parts(x_own)
     scale1_own = mod_own[:, width : 2 * width]
     input_grad = (d_after + ln_back(norm1_own, rstd1_own, d_a * (1.0 + scale1_own))).astype(BF16)
 
-    g_q = grad_q.reshape(3, nc, 2, rows_d, dims["chip_q"], piece_q).transpose(2, 1, 0, 4, 3, 5)
-    g_1 = grad_1.reshape(nc, 2, rows_d, dims["chip_1"], piece_1).transpose(1, 0, 3, 2, 4)
+    g_q = grad_q.reshape(3, nc, 2, rows_d, dims.chip_q, piece_q).transpose(2, 1, 0, 4, 3, 5)
+    g_1 = grad_1.reshape(nc, 2, rows_d, dims.chip_1, piece_1).transpose(1, 0, 3, 2, 4)
     g_p = grad_p.reshape(2, rows_d, nf, cols_f).transpose(0, 2, 1, 3)
     g_2 = grad_2t.reshape(nf, cols_f, 2, ff_d).transpose(2, 0, 1, 3)
-    got = exchange("grad_core", 8, sizes, [("core", "a2a", g.astype(BF16)) for g in (g_q, g_1, g_p, g_2)])
+    got = exchange("grad_core", 8, sizes, [(CORE, SPREAD, g.astype(BF16)) for g in (g_q, g_1, g_p, g_2)])
     s_q, s_1, s_p, s_2 = [jnp.sum(g.astype(F32), axis=0).astype(BF16) for g in got]
-    r_q, r_1 = exchange("grad_chip", 9, sizes, [("chip", "a2a", s_q), ("chip", "a2a", s_1)])
-    z_q = r_q.transpose(1, 0, 2, 3, 4).reshape(nf, dims["per_q"], rows_d, piece_q)
-    z_1 = r_1.reshape(nf, dims["per_1"], rows_d, piece_1)
-    got = exchange("grad_plane", 10, sizes, [("plane", "a2a", g) for g in (z_q, z_1, s_p, s_2)])
+    r_q, r_1 = exchange("grad_chip", 9, sizes, [(CHIP, SPREAD, s_q), (CHIP, SPREAD, s_1)])
+    z_q = r_q.transpose(1, 0, 2, 3, 4).reshape(nf, dims.per_q, rows_d, piece_q)
+    z_1 = r_1.reshape(nf, dims.per_1, rows_d, piece_1)
+    got = exchange("grad_plane", 10, sizes, [(PLANE, SPREAD, g) for g in (z_q, z_1, s_p, s_2)])
     o_q, o_1, o_p, o_2 = [jnp.sum(g.astype(F32), axis=0) for g in got]
     grad_w_qkv = o_q.transpose(1, 0, 2).reshape(rows_d, 3 * width // nf)
     grad_w_fc1 = o_1.transpose(1, 0, 2).reshape(rows_d, ff // nf)
@@ -608,14 +1417,7 @@
     d_cols = total[: micro * clips]
     bias_sums = total[micro * clips : micro * clips + bias_rows].reshape(-1)[:n_bias]
     g_parts = [bias_sums[a:b] for a, b in zip(cut[:-1], cut[1:])]
-    grad_w_ada = precise(silu_part.astype(F32), d_cols, ((0,), (0,)))
-    grad_b_ada = jnp.sum(d_cols, axis=0)
-    d_silu_part = precise(d_cols, w_ada.astype(F32), ((1,), (1,)))
-    d_silu = cond_kernel(dims, d_silu_part).transpose(1, 0, 2).reshape(micro * clips, width)
-    d_silu_own = lax.dynamic_slice_in_dim(d_silu, f * cols_f, cols_f, 1)
-    cond_own = lax.dynamic_slice_in_dim(cond, f * cols_f, cols_f, 1)
-    _, silu_back = jax.vjp(jax.nn.silu, cond_own)
-    cond_grad = silu_back(d_silu_own)[0].reshape(micro, clips, cols_f)
+    cond_grad, grad_w_ada, grad_b_ada = ada_outputs(d_cols)
     return (
         output.reshape(patches.shape),
         input_grad.reshape(patches.shape),

time: 802 us -> 329 us (0.41); the launches traced: 791 us -> 328 us
  Pallas kernels: 563 us -> 298 us
  local copies, waits for them, and re-layouts: 98.1 us -> 21.9 us
  matrix products: 73.6 us -> 3.12 us
  other arithmetic: 54.3 us -> 4.08 us
    pallas_call x10 -> x1, Pallas kernels: 550 us -> 282 us  [block_kernel(): pl.pallas_call(kernel, out_shape=outs, in_specs=[ANYWHERE] * 5 + [ON_CHIP...]
    dot_general x18 -> x0, matrix products: 42.7 us -> none  [the longest x6 19.9 us: dot_lt(): lax.dot_general(left, right, (((0,), (0,)), ((), ())), preferred_element_...]
    reduce_sum x21 -> x2, other arithmetic: 38.5 us -> 1.64 us  [the longest x1 0.93 us: per_device(): own_bias = jnp.sum(o_bias[:, :2], axis=0)]
    reshape x31 -> x12, local copies, waits for them, and re-layouts: 36 us -> 6.88 us  [the longest x1 1.33 us: per_device(): o_1.transpose(1, 0, 2).reshape(rows_d, ff // nf)]
    convert_element_type x14 -> x4, local copies, waits for them, and re-layouts: 27.9 us -> 0.18 us  [lanes(): value.astype(F32)]
    dot_general x7 -> x1, matrix products: 17.6 us -> 0.25 us  [dot(): return jnp.dot(left, right, preferred_element_type=F32)]
    transpose x7 -> x3, local copies, waits for them, and re-layouts: 14.3 us -> 2.8 us  [the longest x1 1.43 us: per_device(): o_q.transpose(1, 0, 2).reshape(rows_d, 3 * width // nf)]
    dot_general x5 -> x2, matrix products: 13.2 us -> 2.86 us  [precise(): lax.dot_general(left, right, (dims, ((), ())), precision=PRECISE, preferr...]
where the time goes in v2:
time: 329 us; the launch traced here: 328 us
  Pallas kernels  298 us (91%)
  local copies, waits for them, and re-layouts  21.9 us (7%)
  other arithmetic  4.08 us (1%)
    pallas_call x1, Pallas kernels, block_kernel(): pl.pallas_call(kernel, out_shape=outs, in_specs=[ANYWHERE] * 5 + [ON_CHIP...  282 us
    pallas_call x1, Pallas kernels, cond_kernel(): pl.pallas_call(kernel, out_shape=jax.ShapeDtypeStruct((nd, rows, width),...  16.5 us

profile of v2, /device:TPU:0, one launch (start us, length us, event | category | flops | bytes accessed | tf_op | source)
XLA Modules:
  0.0 328.2 jit_solution(5157293360164155134)
XLA Ops:
  0.7 0.7 convert_select_fusion
  2.0 0.8 dynamic_update_slice.28
  2.9 0.7 copy.46
  4.2 0.7 concatenate.6.bias_in
  4.8 0.6 dynamic_update_slice.29.p_in
  6.1 0.8 copy.45
  7.5 0.8 copy.44
  8.3 0.7 copy-done.16
  9.1 0.7 compare_convert_fusion.mask_in
  9.8 0.7 copy-done.17
  10.8 0.7 broadcast_in_dim.23.hot_in
  11.4 281.7 %block.1 = (bf16[128,1152]{1,0:T(8,128)(2,1)}, bf16[128,1152]{1,0:T(8,128)(2,1)}, f32[3,144,288]{2,1,0:T(8,128)}, f32[2,144,576]{2,1,0:T(8,128)}, f32[144,384]{1...) custom-call(bf16[128,1152]{1,0:T(8,128)(2,1)} %bitcast.49, ...), custom_call_target="tpu_custom_call" | custom-call | tf_op jit(solution)/shard_map/block/pallas_call | solution.py:1117
  293.2 0.9 copy.35
  294.1 0.8 slice.23
  295.0 0.7 reshape.111
  295.6 1.4 copy.34
  297.1 1.1 reshape.110
  298.6 1.3 reshape.112
  300.0 1.7 fusion
  301.6 1.2 fusion.2.p_in
  302.8 16.5 %cond_sum.1 = f32[8,16,144]{2,1,0:T(8,128)} custom-call(f32[16,144]{1,0:T(8,128)} %fusion.2.p_in), custom_call_target="tpu_custom_call" | custom-call | tf_op jit(solution)/shard_map/cond_sum/pallas_call | solution.py:352
  319.3 1.0 copy.33
  320.4 0.7 fusion.6
  321.1 0.7 dynamic-slice_reduce_fusion
  321.8 0.8 constant_dynamic-slice_fusion.2
  322.6 1.0 slice.26
  323.6 0.7 reshape.113
  324.3 0.9 slice_reduce_fusion
  325.2 0.7 dynamic-slice_reduce_fusion.1
  325.9 0.7 copy.55
  326.6 0.7 copy.56
  327.3 0.9 copy.57
  (63 shorter events, 3.4 us)
Async XLA Ops:
  0.6 1.1 copy-start
  0.7 1.0 copy-start.11
  2.8 0.7 copy-start.14
  2.8 0.9 copy-start.15
  2.8 1.1 copy-start.12
  2.8 1.2 copy-start.13
  2.9 2.0 copy-start.10
  3.5 1.9 copy-start.7
  5.4 0.6 copy-start.3
  6.1 1.1 copy-start.4
  8.3 0.7 copy-start.16
  9.8 0.7 copy-start.17
  297.1 1.1 copy-start.2
  298.6 1.3 copy-start.9
  320.3 1.5 copy-start.8
  321.8 4.1 %copy-start.6 = (bf16[128,1152]{1,0:T(8,128)(2,1)S(1)}, bf16[128,1152]{1,0:T(8,128)(2,1)}, u32[]{:S(2)}) copy-start(bf16[128,1152]{1,0:T(8,128)(2,1)} %get-tuple-element.21) | copy-start | bytes 884740
  321.8 4.8 %copy-start.5 = (bf16[128,1152]{1,0:T(8,128)(2,1)S(1)}, bf16[128,1152]{1,0:T(8,128)(2,1)}, u32[]{:S(2)}) copy-start(bf16[128,1152]{1,0:T(8,128)(2,1)} %get-tuple-element.22) | copy-start | bytes 884740
  322.6 4.7 %copy-start.1 = (f32[288,576]{1,0:T(8,128)S(1)}, f32[288,576]{1,0:T(8,128)}, u32[]{:S(2)}) copy-start(f32[288,576]{1,0:T(8,128)} %get-tuple-element.28) | copy-start | bytes 1990660

commit v3 on v2

--- a/solution.py
+++ b/solution.py
@@ -405,50 +405,80 @@
     return value, slope
 
 
-def block_kernel(dims, x, cot, mask, hot, bias, mod, wq, w1, wp, w2):
+def dot3(left, right):
+    wide_left = left.dtype == F32
+    value = left if wide_left else right
+    total = None
+    for _ in range(3):
+        term = value.astype(BF16)
+        value = value - term.astype(F32)
+        part = dot(term, right) if wide_left else dot(left, term)
+        total = part if total is None else total + part
+    return total
+
+
+def add_low(left, right):
+    return (left.astype(F32) + right.astype(F32)).astype(BF16)
+
+
+def block_kernel(dims, x, cot, ids, bias, silu_part, cond_own, w_ada, wq, wp, w1, w2):
     nc, nf = dims.nc, dims.nf
     own, width = x.shape
     group = nc * own
-    per_q, rows_d, chip_w = wq.shape
-    per_1, _, ff_d = w1.shape
-    cols_f = w2.shape[0]
-    pad_p = wp.shape[1]
-    step_p = dims.step_p
+    rows_d, q_w = wq.shape
+    chip_w = q_w // 3
+    ff_d, cols_f = w2.shape
+    ff_c = 2 * ff_d
+    ada_w = w_ada.shape[1]
+    n_bias = bias.shape[1]
     heads = chip_w // HEAD_DIM
-    n_rows = mod.shape[1]
+    n_rows = silu_part.shape[0]
+    half = n_rows // 2
     n_sub = own // SUB
     head_scale = HEAD_DIM ** (-0.5)
+    last = nf - 2
 
     outs = (
         jax.ShapeDtypeStruct((own, width), BF16),
         jax.ShapeDtypeStruct((own, width), BF16),
-        jax.ShapeDtypeStruct((per_q, rows_d, chip_w), F32),
-        jax.ShapeDtypeStruct((per_1, rows_d, ff_d), F32),
-        jax.ShapeDtypeStruct((rows_d, pad_p), F32),
-        jax.ShapeDtypeStruct((cols_f, ff_d), F32),
-        jax.ShapeDtypeStruct((2, n_rows, width), F32),
-        jax.ShapeDtypeStruct((nc, 8, width), F32),
+        jax.ShapeDtypeStruct((n_rows, cols_f), F32),
+        jax.ShapeDtypeStruct((rows_d, ada_w), F32),
+        jax.ShapeDtypeStruct((1, ada_w), F32),
+        jax.ShapeDtypeStruct((rows_d, q_w), F32),
+        jax.ShapeDtypeStruct((1, 2 * chip_w), F32),
+        jax.ShapeDtypeStruct((rows_d, cols_f), F32),
+        jax.ShapeDtypeStruct((1, cols_f), F32),
+        jax.ShapeDtypeStruct((rows_d, ff_c), F32),
+        jax.ShapeDtypeStruct((1, ff_c), F32),
+        jax.ShapeDtypeStruct((ff_d, cols_f), F32),
+        jax.ShapeDtypeStruct((1, cols_f), F32),
     )
     tokens = (nc, own, width)
-    n_sem = 160
+    n_sem = 240
     scratch = dict(
         xg=pltpu.VMEM(tokens, BF16),
         cg=pltpu.VMEM(tokens, BF16),
-        maskg=pltpu.VMEM((nc, own, own), BF16),
-        hotg=pltpu.VMEM((nc, n_sub, 128), F32),
-        biasg=pltpu.VMEM((nf, 8, width), F32),
-        m_core=pltpu.VMEM((n_rows, width), F32),
-        m_chip=pltpu.VMEM((nc, n_rows, width), F32),
-        m_win=pltpu.VMEM((nf, 2, n_rows, width), F32),
+        idsg=pltpu.VMEM((nc, 8, own), F32),
+        biasg=pltpu.VMEM((nf, 1, n_bias), F32),
+        ada=pltpu.VMEM(w_ada.shape, BF16),
+        m_part=pltpu.VMEM((2, half, ada_w), F32),
+        m_core=pltpu.VMEM((half, ada_w), F32),
+        m_chip=pltpu.VMEM((nc, half, ada_w), F32),
+        m_z=pltpu.VMEM((nf, 2, half, ada_w), F32),
+        m_tab=pltpu.VMEM((n_rows, 6 * width), F32),
         tab=pltpu.VMEM((3, nc * n_sub, width), F32),
         own_tab=pltpu.VMEM((6, n_sub, width), F32),
-        q_rows=pltpu.VMEM((nf * per_q, rows_d, chip_w), BF16),
-        f1_rows=pltpu.VMEM((nf * per_1, rows_d, ff_d), BF16),
+        q_z=pltpu.VMEM((nf, rows_d, q_w), BF16),
+        q_rows=pltpu.VMEM((nf * 3, rows_d, chip_w), BF16),
         w_q=pltpu.VMEM((3, nc, 2, rows_d, chip_w), BF16),
-        w_1=pltpu.VMEM((2, nc, 2, rows_d, ff_d), BF16),
-        p_got=pltpu.VMEM((2, nf, rows_d, pad_p), BF16),
+        f1_z=pltpu.VMEM((nf, rows_d, ff_c), BF16),
+        w_1=pltpu.VMEM((nc, 2, rows_d, ff_c), BF16),
+        p_got=pltpu.VMEM((2, nf, rows_d, cols_f), BF16),
         w_p=pltpu.VMEM((chip_w, width), BF16),
-        w_2=pltpu.VMEM((2, nf, cols_f, ff_d), BF16),
+        f2_nat=pltpu.VMEM((ff_d, cols_f), BF16),
+        f2_half=pltpu.VMEM((2, rows_d, ff_d), BF16),
+        f2_got=pltpu.VMEM((rows_d, ff_d), BF16),
+        w_2=pltpu.VMEM((nf, 2, rows_d, ff_c), BF16),
         a_in=pltpu.VMEM(tokens, BF16),
         qkv=pltpu.VMEM((3, nc, own, chip_w), BF16),
         probs=pltpu.VMEM((nc * heads, own, own), F32),
@@ -462,32 +492,34 @@
         attn=pltpu.VMEM((own, width), F32),
         after=pltpu.VMEM((own, width), F32),
         d_after=pltpu.VMEM((own, width), F32),
-        hid=pltpu.VMEM((2, own, ff_d), F32),
-        slope=pltpu.VMEM((2, own, ff_d), F32),
-        act=pltpu.VMEM((2, nc, own, ff_d), BF16),
-        d_hid=pltpu.VMEM((2, nc, own, ff_d), BF16),
+        hid=pltpu.VMEM((own, ff_c), F32),
+        slope=pltpu.VMEM((own, ff_c), F32),
+        act=pltpu.VMEM((nc, own, ff_c), BF16),
+        d_hid=pltpu.VMEM((nc, own, ff_c), BF16),
         dbr=pltpu.VMEM(tokens, BF16),
         d_qkv=pltpu.VMEM((3, nc, own, chip_w), BF16),
-        g_2=pltpu.VMEM((2, nf, cols_f, ff_d), BF16),
-        g_2r=pltpu.VMEM((nf, cols_f, ff_d), BF16),
-        g_1=pltpu.VMEM((2, nc, 2, rows_d, ff_d), BF16),
-        g_1r=pltpu.VMEM((2, nc, rows_d, ff_d), BF16),
-        g_q=pltpu.VMEM((3, nc, 2, rows_d, chip_w), BF16),
+        g_2=pltpu.VMEM((nf, 2, rows_d, ff_c), BF16),
+        g_2r=pltpu.VMEM((nf, rows_d, ff_c), BF16),
+        g_1r=pltpu.VMEM((nc, rows_d, ff_c), BF16),
         g_qr=pltpu.VMEM((3, nc, rows_d, chip_w), BF16),
-        g_p=pltpu.VMEM((2, rows_d, width), BF16),
         g_pr=pltpu.VMEM((rows_d, width), BF16),
-        z_q=pltpu.VMEM((nf, per_q, rows_d, chip_w), BF16),
-        z_1=pltpu.VMEM((nf, per_1, rows_d, ff_d), BF16),
-        z_p=pltpu.VMEM((nf, rows_d, pad_p), BF16),
-        z_2=pltpu.VMEM((nf, cols_f, ff_d), BF16),
+        got_q=pltpu.VMEM((2, nf - 1, rows_d, q_w), BF16),
+        got_1=pltpu.VMEM((2, nf - 1, rows_d, ff_c), BF16),
+        got_p=pltpu.VMEM((2, nf - 1, rows_d, cols_f), BF16),
+        got_2=pltpu.VMEM((2, nf - 1, rows_d, ff_c), BF16),
+        all_2=pltpu.VMEM((2, rows_d, ff_c), F32),
         sub=pltpu.VMEM((6, n_sub, width), F32),
-        d_mod=pltpu.VMEM((6, n_rows, width), F32),
+        d_cut=pltpu.VMEM((nf, n_rows, ada_w), F32),
         d_bias=pltpu.VMEM((8, width), F32),
-        dz=pltpu.VMEM((nf, 2, n_rows, width), F32),
+        dz=pltpu.VMEM((nf, n_rows, ada_w), F32),
         dzb=pltpu.VMEM((nf, 8, width), F32),
-        d_both=pltpu.VMEM((2, n_rows, width), F32),
+        d_both=pltpu.VMEM((2, half, ada_w), F32),
+        d_tot=pltpu.VMEM((2, half, ada_w), F32),
         d_bsum=pltpu.VMEM((8, width), F32),
         d_coreb=pltpu.VMEM((8, width), F32),
+        d_chipb=pltpu.VMEM((nc, 8, width), F32),
+        c_part=pltpu.VMEM((nf, n_rows, rows_d), F32),
+        c_all=pltpu.VMEM((nc, 2, n_rows, rows_d), F32),
         send=pltpu.SemaphoreType.DMA((n_sem,)),
         recv=pltpu.SemaphoreType.DMA((n_sem,)),
         local=pltpu.SemaphoreType.DMA((32,)),
@@ -495,8 +527,8 @@
     names = list(scratch)
 
     def kernel(
-        x_in, c_in, mask_in, hot_in, bias_in, mod_in, q_in, f1_in, p_in, f2_in,
-        out, x_grad, o_q, o_1, o_p, o_2, o_mod, o_bias, *rest,
+        x_in, c_in, ids_in, bias_in, silu_in, cond_in, ada_in, q_in, p_in, f1_in, f2_in,
+        out, x_grad, o_cond, o_ada, o_bada, o_q, o_bqv, o_p, o_bp, o_1, o_b1, o_2, o_b2, *rest,
     ):
         r = types.SimpleNamespace(**dict(zip(names, rest)))
         place = Place(nc, nf)
@@ -513,144 +545,245 @@
 
             lax.fori_loop(0, count, run, 0)
 
+        def when(condition, body):
+            pl.when(condition)(body)
+
         def sub_rows(g):
             return pl.ds(pl.multiple_of(g * SUB, SUB), SUB)
-
-        def chip_send(src, dst, base, step):
-            other, device = place.peer(CHIP, step)
-            return pltpu.make_async_remote_copy(
-                src_ref=src(other),
-                dst_ref=dst.at[c],
-                send_sem=r.send.at[base + step - 1],
-                recv_sem=r.recv.at[base + step - 1],
-                device_id=device,
-                device_id_type=MESH_ID,
-            )
 
         def reserve(count):
             base = wires.remote_count
             wires.remote_count += count
             return base
 
+        def pair(src, dst, device, send_at, recv_at):
+            return pltpu.make_async_remote_copy(
+                src_ref=src,
+                dst_ref=dst,
+                send_sem=r.send.at[send_at],
+                recv_sem=r.recv.at[recv_at],
+                device_id=device,
+                device_id_type=MESH_ID,
+            )
+
+        def chip_send(src, dst, base, step):
+            other, device = place.peer(CHIP, step)
+            at = base + step - 1
+            return pair(src(other), dst.at[c], device, at, at)
+
+        up, down = (place.dp, f + 1), (place.dp, f - 1)
+
+        class Gather:
+            def __init__(self, slot):
+                self.slot = slot
+                self.up, self.down = reserve(nf - 1), reserve(nf - 1)
+
+            def both(self, step, src=None):
+                above = pair(
+                    self.slot(f - step) if src is None else src,
+                    self.slot(f - step), up, self.up + step, self.up + step,
+                )
+                below = pair(
+                    self.slot(f + step) if src is None else src,
+                    self.slot(f + step), down, self.down + step, self.down + step,
+                )
+                return (
+                    ((f - step >= 0) & (f < nf - 1), above),
+                    ((f + step <= nf - 1) & (f > 0), below),
+                )
+
+            def start(self, step, src=None):
+                for condition, copy in self.both(step, src):
+                    when(condition, copy.start)
+
+            def arrive(self, step, then=None):
+                for condition, got, base in (
+                    (f - 1 - step >= 0, f - 1 - step, self.up),
+                    (f + 1 + step <= nf - 1, f + 1 + step, self.down),
+                ):
+
+                    def body(got=got, base=base):
+                        slot = self.slot(got)
+                        pair(slot, slot, core_dev, base + step, base + step).wait_recv()
+                        if then is not None:
+                            then(got)
+
+                    when(condition, body)
+
+            def sent(self, src=None):
+                for step in range(nf - 1):
+                    for condition, copy in self.both(step, src if step == 0 else None):
+                        when(condition, copy.wait_send)
+
+        class Sum:
+            def __init__(self, terms, got):
+                self.terms, self.got = terms, got
+                self.bases = (reserve(nf - 1), reserve(nf - 1))
+
+            def both(self, step):
+                for way in range(2):
+                    target = f + (nf - 1) - step if way == 0 else f - (nf - 1) + step
+                    condition = (f <= step) & (f < nf - 1) if way == 0 else (target >= 0) & (f > 0)
+                    more = condition & (f > 0 if way == 0 else f < nf - 1)
+                    at = self.bases[way] + step
+                    copy = pair(
+                        self.terms(target), self.got.at[way, step], up if way == 0 else down, at, at
+                    )
+                    yield way, target, condition, more, copy
+
+            def wait(self, way, step):
+                at = self.bases[way] + step
+                ref = self.got.at[way, step]
+                pair(ref, ref, core_dev, at, at).wait_recv()
+
+            def start(self, step):
+                for way, target, condition, more, copy in self.both(step):
+                    if step > 0:
+
+                        def body(way=way, target=target):
+                            self.wait(way, step - 1)
+                            ref = self.terms(target)
+                            ref[...] = add_low(ref[...], self.got[way, step - 1])
+
+                        when(more, body)
+                    when(condition, copy.start)
+
+            def finish(self, result):
+                result[...] = self.terms(f)[...].astype(F32)
+                for way, condition in ((0, f > 0), (1, f < nf - 1)):
+
+                    def body(way=way):
+                        self.wait(way, last)
+                        result[...] = result[...] + self.got[way, last].astype(F32)
+
+                    when(condition, body)
+                for step in range(nf - 1):
+                    for _, _, condition, _, copy in self.both(step):
+                        when(condition, copy.wait_send)
+
         greet(place, (CORE, CHIP, PLANE))
 
-        w_q, q_rows = r.w_q, r.q_rows
-        m_first = wires.far(mod_in.at[core_o], r.m_core, core_dev)
-        q_far = [
-            wires.far(q_in, q_rows.at[pl.ds(f * per_q, per_q)], peer) for _, peer in plane_peers
-        ]
+        q_line = Gather(lambda g: r.q_z.at[g])
+        p_line = Gather(lambda g: r.p_got.at[k, g])
+        f1_line = Gather(lambda g: r.f1_z.at[g])
+        f2_line = Gather(lambda g: r.w_2.at[g, k])
+        q_line.start(0, q_in)
+        ada_near = wires.near(ada_in, r.ada)
+        q_near = wires.near(q_in, r.q_z.at[f])
+        f2_near = wires.near(f2_in, r.f2_nat)
         first = []
         for _, peer in chip_peers:
-            first.append(wires.far(hot_in, r.hotg.at[c], peer))
-            first.append(wires.far(x_in, r.xg.at[c], peer))
-            first.append(wires.far(mask_in, r.maskg.at[c], peer))
+            first.append(wires.far(ids_in, r.idsg.at[c], peer))
         for _, peer in plane_peers:
             first.append(wires.far(bias_in, r.biasg.at[f], peer))
-        first.append(wires.near(hot_in, r.hotg.at[c]))
         first.append(wires.near(x_in, r.xg.at[c]))
-        first.append(wires.near(mask_in, r.maskg.at[c]))
-        first.append(wires.near(bias_in, r.biasg.at[f]))
-
+        first.append(wires.near(c_in, r.cg.at[c]))
+        p_near = wires.near(p_in, r.p_got.at[k, f])
+        f1_near = wires.near(f1_in, r.f1_z.at[f])
+        r.idsg[c] = ids_in[...]
+        r.biasg[f] = bias_in[...]
+        ada_near.wait()
+        ada_bias = jnp.where(place.dp == 0, bias_in[:, n_bias - ada_w :], 0.0)
+        value = dot(silu_in[...], r.ada[...]) + ada_bias
+        r.m_part[...] = value.reshape(2, half, ada_w)
+        m_first = wires.far(r.m_part.at[core_o], r.m_core, core_dev)
+
+        w_q, q_rows = r.w_q, r.q_rows
         q_base = reserve(3 * nc)
         q_local = wires.local_count
         wires.local_count += 3
 
-        def q_piece(plane, source, at, i):
-            piece = per_q * plane + i
+        def q_copies(plane, i):
+            piece = 3 * plane + i
             kind, chip = piece // nc, piece % nc
-            src = source.at[at]
-            dst = w_q.at[kind, c, k]
-            far = pltpu.make_async_remote_copy(
-                src_ref=src,
-                dst_ref=dst,
-                send_sem=r.send.at[q_base + kind * nc + chip],
-                recv_sem=r.recv.at[q_base + kind * nc + c],
-                device_id=(chip * 2 + k, f),
-                device_id_type=MESH_ID,
-            )
-            near = pltpu.make_async_copy(src, dst, r.local.at[q_local + kind])
-            return chip, far, near
-
-        def q_forward(plane, source, at_of):
-            for i in range(per_q):
-                chip, far, near = q_piece(plane, source, at_of(i), i)
-
-                @pl.when(chip != c)
-                def _():
-                    far.start()
-
-                @pl.when(chip == c)
-                def _():
-                    near.start()
-
-        q_forward(f, q_in, lambda i: i)
+            src, dst = q_rows.at[piece], w_q.at[kind, c, k]
+            far = pair(src, dst, (chip * 2 + k, f), q_base + kind * nc + chip, q_base + kind * nc + c)
+            return chip, far, pltpu.make_async_copy(src, dst, r.local.at[q_local + kind])
+
+        def q_forward(plane):
+            for i in range(3):
+                q_rows[3 * plane + i] = r.q_z[plane, :, chip_w * i : chip_w * (i + 1)]
+                chip, far, near = q_copies(plane, i)
+                when(chip != c, far.start)
+                when(chip == c, near.start)
+
+        f1_base = reserve(nc)
+        f1_local = wires.local_count
+        wires.local_count += 1
+
+        def f1_copies(plane):
+            src, dst = r.f1_z.at[plane], r.w_1.at[c, k]
+            far = pair(src, dst, (plane * 2 + k, f), f1_base + plane, f1_base + c)
+            return far, pltpu.make_async_copy(src, dst, r.local.at[f1_local])
+
+        def f1_forward(plane):
+            far, near = f1_copies(plane)
+            when(plane != c, far.start)
+            when(plane == c, near.start)
+
+        q_near.wait()
+        q_forward(f)
         m_first.wait()
         m_chip = r.m_chip
-        m_chip[c] = mod_in[k] + r.m_core[...]
+        m_chip[c] = r.m_part[k] + r.m_core[...]
         m_second = [wires.far(m_chip.at[c], m_chip.at[c], peer) for _, peer in chip_peers]
-        q_forward_order = []
-        for step, copy in enumerate(q_far, 1):
-            copy.wait_recv()
-            plane = xor_of(f, step, nf)
-            q_forward(plane, q_rows, lambda i: per_q * plane + i)
-            if step == 1:
-                wait_all(m_second)
-                total = m_chip[0]
-                for other in range(1, nc):
-                    total = total + m_chip[other]
-                r.m_win[f, k] = total
-                m_third = [
-                    wires.far(r.m_win.at[f, k], r.m_win.at[f, k], peer)
-                    for _, peer in plane_peers
-                ]
-        p_far = [wires.far(p_in, r.p_got.at[k, f], peer) for _, peer in plane_peers]
-        f1_rows = r.f1_rows
-        f1_far = [
-            wires.far(f1_in, f1_rows.at[pl.ds(f * per_1, per_1)], peer) for _, peer in plane_peers
-        ]
-        f2_far = [wires.far(f2_in, r.w_2.at[k, f], peer) for _, peer in plane_peers]
-        p_far.append(wires.near(p_in, r.p_got.at[k, f]))
-        f1_far.append(wires.near(f1_in, f1_rows.at[pl.ds(f * per_1, per_1)]))
-        f2_far.append(wires.near(f2_in, r.w_2.at[k, f]))
+        for _, peer in chip_peers:
+            first.append(wires.far(x_in, r.xg.at[c], peer))
+        q_line.arrive(0, q_forward)
+        q_line.start(1)
+        wait_all(m_second)
+        total = m_chip[0]
+        for other in range(1, nc):
+            total = total + m_chip[other]
+        r.m_z[f, k] = total
+        m_third = [wires.far(r.m_z.at[f, k], r.m_z.at[f, k], peer) for _, peer in plane_peers]
+        p_line.start(0, p_in)
+        f2_near.wait()
+        turned = r.f2_nat[...].T
+        r.f2_half[...] = turned.reshape(2, rows_d, ff_d)
+        f2_swap = wires.far(r.f2_half.at[core_o], r.f2_got, core_dev)
+        q_line.arrive(1, q_forward)
+        q_line.start(2)
+        p_line.arrive(0)
+        p_line.start(1)
+        f1_line.start(0, f1_in)
+        f2_swap.wait()
+
+        def join_even():
+            r.w_2[f, k] = jnp.concatenate([r.f2_half[0], r.f2_got[...]], axis=1)
+
+        def join_odd():
+            r.w_2[f, k] = jnp.concatenate([r.f2_got[...], r.f2_half[1]], axis=1)
+
+        when(k == 0, join_even)
+        when(k == 1, join_odd)
+        q_line.arrive(2, q_forward)
+        p_line.arrive(1)
+        p_line.start(2)
         wait_all(m_third)
-        m_last = wires.far(r.m_win.at[:, k], r.m_win.at[:, k], core_dev)
-        for copy in q_far:
-            copy.wait_send()
-        q_core = []
-        for kind in range(3):
-            for other, _ in chip_peers:
-                pltpu.make_async_remote_copy(
-                    src_ref=w_q.at[kind, other, k],
-                    dst_ref=w_q.at[kind, other, k],
-                    send_sem=r.send.at[q_base + kind * nc + other],
-                    recv_sem=r.recv.at[q_base + kind * nc + other],
-                    device_id=core_dev,
-                    device_id_type=MESH_ID,
-                ).wait()
-            pltpu.make_async_copy(
-                w_q.at[kind, c, k], w_q.at[kind, c, k], r.local.at[q_local + kind]
-            ).wait()
-            q_core.append(wires.far(w_q.at[kind, :, k], w_q.at[kind, :, k], core_dev))
+        m_last = wires.far(r.m_z.at[:, k], r.m_z.at[:, k], core_dev)
+        f2_line.start(0)
 
         wait_all(first)
         m_last.wait()
-        hot_rows = r.hotg[...].reshape(nc * n_sub, 128)[:, :n_rows]
-        places = lax.broadcasted_iota(jnp.int32, (nc * n_sub, n_rows), 1).astype(F32)
-        hot_of = jnp.where(hot_rows == places, 1.0, 0.0)
-        own_hot = r.hotg[c][:, :n_rows]
-        own_hot = jnp.where(
-            own_hot == lax.broadcasted_iota(jnp.int32, (n_sub, n_rows), 1).astype(F32), 1.0, 0.0
-        )
-        starts = [6 * plane // nf for plane in range(nf)]
+        m_rows = [r.m_z[plane].reshape(n_rows, ada_w) for plane in range(nf)]
+        r.m_tab[...] = jnp.concatenate(m_rows, axis=1)
+        lead = lax.broadcasted_iota(jnp.int32, (n_sub, own), 1)
+        lead = lead == SUB * lax.broadcasted_iota(jnp.int32, (n_sub, own), 0)
+        lead = jnp.where(lead, 1.0, 0.0).astype(BF16)
+        places = lax.broadcasted_iota(jnp.int32, (own, n_rows), 1).astype(F32)
+
+        def hot_rows(blk):
+            clip = r.idsg[blk].T[:, 1:2]
+            return dot(lead, jnp.where(clip == places, 1.0, 0.0).astype(BF16)).astype(BF16)
+
+        hot_all = jnp.concatenate([hot_rows(blk) for blk in range(nc)], axis=0)
+        own_hot = hot_rows(c)
         for kind in range(6):
-            value = None
-            for plane in range(nf):
-                if 0 <= kind - starts[plane] < 2:
-                    term = r.m_win[plane, kind - starts[plane]]
-                    value = term if value is None else value + term
+            value = r.m_tab[:, width * kind : width * (kind + 1)]
             if kind in (0, 1, 5):
-                r.tab[kind % 3] = jnp.dot(hot_of, value, precision=PRECISE, preferred_element_type=F32)
-            r.own_tab[kind] = jnp.dot(own_hot, value, precision=PRECISE, preferred_element_type=F32)
+                r.tab[kind % 3] = dot3(hot_all, value)
+            r.own_tab[kind] = dot3(own_hot, value)
 
         def tab_row(kind, blk, g):
             return r.tab[kind % 3, pl.ds(blk * n_sub + g, 1), :]
@@ -668,23 +801,30 @@
             loop(n_sub, body)
 
         loop(nc, make_a)
+
+        q_core = []
+        for kind in range(3):
+            for other, _ in chip_peers:
+                ref = w_q.at[kind, other, k]
+                at = q_base + kind * nc + other
+                pair(ref, ref, core_dev, at, at).wait()
+            ref = w_q.at[kind, c, k]
+            pltpu.make_async_copy(ref, ref, r.local.at[q_local + kind]).wait()
+            q_core.append(wires.far(w_q.at[kind, :, k], w_q.at[kind, :, k], core_dev))
+        p_line.arrive(2)
+        p_near.wait()
+        p_core = wires.far(r.p_got.at[k], r.p_got.at[k], core_dev)
+        f1_near.wait()
+        f1_forward(f)
+        f1_line.arrive(0, f1_forward)
+        f1_line.start(1)
         c_far = [wires.far(c_in, r.cg.at[c], peer) for _, peer in chip_peers]
-        c_far.append(wires.near(c_in, r.cg.at[c]))
-
-        wait_all(p_far)
-        p_core = wires.far(r.p_got.at[k], r.p_got.at[k], core_dev)
+        p_core.wait()
+        for side in range(2):
+            row = [r.p_got[side, plane] for plane in range(nf)]
+            r.w_p[side * rows_d : (side + 1) * rows_d, :] = jnp.concatenate(row, axis=1)
         wait_all(q_core)
-        p_core.wait()
-        blocks_p = width // 128
-        for half in range(2):
-            for j in range(blocks_p):
-                value = None
-                for plane in range(nf):
-                    at = j * 128 - plane * step_p
-                    if 0 <= at < pad_p:
-                        term = r.p_got[half, plane, :, at : at + 128]
-                        value = term if value is None else value + term
-                r.w_p[half * rows_d : (half + 1) * rows_d, j * 128 : (j + 1) * 128] = value
+
         lane = lax.broadcasted_iota(jnp.int32, (1, chip_w), 1)
         head_of = [
             jnp.where((lane >= HEAD_DIM * h) & (lane < HEAD_DIM * (h + 1)), 1.0, 0.0).astype(BF16)
@@ -694,11 +834,30 @@
         def weight_q(kind):
             return w_q[kind].reshape(width, chip_w)
 
-        b_row = pl.ds(2 + c % 2, 1)
-        bias_q = r.biasg[c // 2, b_row, pl.ds(0, chip_w)]
-        bias_v = r.biasg[nc // 2 + c // 2, b_row, pl.ds(0, chip_w)]
+        def qv_bias(plane):
+            row = r.biasg[plane]
+            return jnp.where(c % 2 == 0, row[:, :chip_w], row[:, chip_w : 2 * chip_w])
+
+        bias_q, bias_v = qv_bias(c // 2), qv_bias(nf // 2 + c // 2)
+        at_p = 2 * chip_w
+        at_1 = at_p + cols_f
+        at_2 = at_1 + ff_c
+        bias_p = jnp.concatenate([r.biasg[g][:, at_p : at_p + cols_f] for g in range(nf)], axis=1)
+        bias_o = jnp.concatenate([r.biasg[g][:, at_2 : at_2 + cols_f] for g in range(nf)], axis=1)
+        bias_1 = r.biasg[c][:, at_1 : at_1 + ff_c]
         sum_base = reserve(nc - 1)
         sum_s, sum_r = r.sum_s, r.sum_r
+
+        def hand_on(step, blk, part, s_ref, r_ref, base):
+            def away():
+                s_ref[blk] = part
+                chip_send(lambda other: s_ref.at[other], r_ref, base, step).start()
+
+            def stay():
+                r_ref[c] = part
+
+            when(step != 0, away)
+            when(step == 0, stay)
 
         def attend(i):
             step = (i + 1) % nc
@@ -708,7 +867,8 @@
             r.qkv[1, blk] = dot(a_now, weight_q(1)).astype(BF16)
             r.qkv[2, blk] = (dot(a_now, weight_q(2)) + bias_v).astype(BF16)
             q_now, k_now, v_now = r.qkv[0, blk], r.qkv[1, blk], r.qkv[2, blk]
-            same = r.maskg[blk].astype(F32) > 0.5
+            frames = r.idsg[blk]
+            same = frames.T[:, 0:1] == frames[0:1, :]
             mixed = jnp.zeros((own, chip_w), F32)
             for h in range(heads):
                 scores = dot_rt(q_now * head_of[h], k_now) * head_scale
@@ -719,35 +879,16 @@
                 mixed = mixed + dot(share.astype(BF16), v_now * head_of[h])
             mixed = mixed.astype(BF16)
             r.mixed[blk] = mixed
-            part = dot(mixed, r.w_p[...]).astype(BF16)
-
-            @pl.when(step != 0)
-            def _():
-                sum_s[blk] = part
-                chip_send(lambda other: sum_s.at[other], sum_r, sum_base, step).start()
-
-            @pl.when(step == 0)
-            def _():
-                sum_r[c] = part
+            hand_on(step, blk, dot(mixed, r.w_p[...]).astype(BF16), sum_s, sum_r, sum_base)
 
         loop(nc, attend)
-
-        wait_all(f1_far)
-        f1_moved = [
-            wires.far(f1_rows.at[pl.ds(other * per_1, per_1)], r.w_1.at[:, c, k], peer)
-            for other, peer in chip_peers
-        ]
-        f1_moved.append(
-            wires.near(f1_rows.at[pl.ds(c * per_1, per_1)], r.w_1.at[:, c, k])
-        )
+        f1_line.arrive(1, f1_forward)
+        f1_line.start(2)
+        f2_line.arrive(0)
+        f2_line.start(1)
 
         for step in range(1, nc):
             chip_send(lambda other: sum_s.at[other], sum_r, sum_base, step).wait()
-        bias_p = r.biasg[0, 0:1, :]
-        bias_o = r.biasg[0, 1:2, :]
-        for plane in range(1, nf):
-            bias_p = bias_p + r.biasg[plane, 0:1, :]
-            bias_o = bias_o + r.biasg[plane, 1:2, :]
 
         def after_attention(g):
             rows = sub_rows(g)
@@ -766,9 +907,9 @@
         m_base = reserve(nc - 1)
         for step in range(1, nc):
             chip_send(lambda other: m_all.at[c], m_all, m_base, step).start()
-
-        wait_all(f1_moved)
-        f1_core = wires.far(r.w_1.at[:, :, k], r.w_1.at[:, :, k], core_dev)
+        f1_line.arrive(2, f1_forward)
+        f2_line.arrive(1)
+        f2_line.start(2)
         wait_all(c_far)
 
         def make_dbr(blk):
@@ -780,106 +921,91 @@
             loop(n_sub, body)
 
         loop(nc, make_dbr)
+        for other, _ in chip_peers:
+            ref = r.w_1.at[other, k]
+            pair(ref, ref, core_dev, f1_base + other, f1_base + other).wait()
+        ref = r.w_1.at[c, k]
+        pltpu.make_async_copy(ref, ref, r.local.at[f1_local]).wait()
+        f1_line.sent(f1_in)
+        f1_core = wires.far(r.w_1.at[:, k], r.w_1.at[:, k], core_dev)
+        f2_line.arrive(2)
+        f2_core = wires.far(r.w_2.at[:, k], r.w_2.at[:, k], core_dev)
         f1_core.wait()
-        wait_all(f2_far)
-        wires.far(r.w_2.at[k], r.w_2.at[k], core_dev).wait()
-
-        def weight_1(h):
-            return r.w_1[h].reshape(width, ff_d)
-
-        def weight_2(h):
-            return r.w_2[h].reshape(width, ff_d)
+        f2_core.wait()
+
+        def weight_1():
+            return r.w_1[...].reshape(width, ff_c)
+
+        def weight_2():
+            return r.w_2[...].reshape(width, ff_c)
 
         dm_base = reserve(nc - 1)
         br_base = reserve(nc - 1)
-        dm_s, dm_r, br_s, br_r = sum_s, sum_r, r.br_s, r.br_r
+        br_s, br_r = r.br_s, r.br_r
 
         def feed(step):
             blk = xor_of(c, step, nc)
-
-            @pl.when(step != 0)
-            def _():
-                chip_send(lambda other: m_all.at[c], m_all, m_base, step).wait_recv()
-
-            m_now = m_all[blk]
-            for h in range(2):
-                bias_1 = r.biasg[c, 4 + h : 5 + h, pl.ds(0, ff_d)]
-                r.hid[h] = dot(m_now, weight_1(h)) + bias_1
+            when(
+                step != 0,
+                lambda: chip_send(lambda other: m_all.at[c], m_all, m_base, step).wait_recv(),
+            )
+            r.hid[...] = dot(m_all[blk], weight_1()) + bias_1
 
             def gelu_rows(g):
                 rows = sub_rows(g)
-                for h in range(2):
-                    value, slope = gelu_both(r.hid[h, rows, :])
-                    r.act[h, blk, rows, :] = value.astype(BF16)
-                    r.slope[h, rows, :] = slope
+                value, slope = gelu_both(r.hid[rows, :])
+                r.act[blk, rows, :] = value.astype(BF16)
+                r.slope[rows, :] = slope
 
             loop(n_sub, gelu_rows)
-            d_now = r.dbr[blk]
-            for h in range(2):
-                r.hid[h] = dot(d_now, weight_2(h))
+            r.hid[...] = dot(r.dbr[blk], weight_2())
 
             def back_rows(g):
                 rows = sub_rows(g)
-                for h in range(2):
-                    value = r.hid[h, rows, :] * r.slope[h, rows, :]
-                    r.d_hid[h, blk, rows, :] = value.astype(BF16)
+                r.d_hid[blk, rows, :] = (r.hid[rows, :] * r.slope[rows, :]).astype(BF16)
 
             loop(n_sub, back_rows)
-            part = dot_rt(r.d_hid[0, blk], weight_1(0)) + dot_rt(r.d_hid[1, blk], weight_1(1))
-            part = part.astype(BF16)
-
-            @pl.when(step != 0)
-            def _():
-                dm_s[blk] = part
-                chip_send(lambda other: dm_s.at[other], dm_r, dm_base, step).start()
-
-            @pl.when(step == 0)
-            def _():
-                dm_r[c] = part
-
-            part2 = dot_rt(r.act[0, blk], weight_2(0)) + dot_rt(r.act[1, blk], weight_2(1))
-            part2 = part2.astype(BF16)
-
-            @pl.when(step != 0)
-            def _():
-                br_s[blk] = part2
-                chip_send(lambda other: br_s.at[other], br_r, br_base, step).start()
-
-            @pl.when(step == 0)
-            def _():
-                br_r[c] = part2
+            part = dot_rt(r.d_hid[blk], weight_1()).astype(BF16)
+            hand_on(step, blk, part, sum_s, sum_r, dm_base)
 
         loop(nc, feed)
         for step in range(1, nc):
             chip_send(lambda other: m_all.at[c], m_all, m_base, step).wait_send()
 
-        dbr_all = r.dbr[...].reshape(group, width)
-
         def column_cuts(count):
             return [(at, min(at + 256, count)) for at in range(0, count, 256)]
 
-        for lo, hi in column_cuts(ff_d):
-            value = dot_lt(dbr_all, r.act[core_o, :, :, lo:hi].reshape(group, hi - lo))
-            r.g_2[core_o, :, :, lo:hi] = value.astype(BF16).reshape(nf, cols_f, hi - lo)
-        g2_core = wires.far(r.g_2.at[core_o], r.g_2r, core_dev)
+        def all_rows(ref):
+            return ref[...].reshape(group, ref.shape[-1])
+
+        dbr_all = all_rows(r.dbr)
+        for lo, hi in column_cuts(ff_c):
+            value = dot_lt(dbr_all, r.act[:, :, lo:hi].reshape(group, hi - lo))
+            r.g_2[:, :, :, lo:hi] = value.astype(BF16).reshape(nf, 2, rows_d, hi - lo)
+        g2_core = wires.far(r.g_2.at[:, core_o], r.g_2r, core_dev)
+
+        def branch_out(i):
+            step = (i + 1) % nc
+            blk = xor_of(c, step, nc)
+            part = dot_rt(r.act[blk], weight_2()).astype(BF16)
+            hand_on(step, blk, part, br_s, br_r, br_base)
+
+        loop(nc, branch_out)
         g2_core.wait()
-        for lo, hi in column_cuts(ff_d):
-            value = dot_lt(dbr_all, r.act[k, :, :, lo:hi].reshape(group, hi - lo))
-            value = value.reshape(nf, cols_f, hi - lo) + r.g_2r[:, :, lo:hi].astype(F32)
-            r.g_2[k, :, :, lo:hi] = value.astype(BF16)
-        z2_far = [
-            wires.far(r.g_2.at[k, other], r.z_2.at[f], peer) for other, peer in plane_peers
-        ]
+        for plane in range(nf):
+            r.g_2[plane, k] = add_low(r.g_2[plane, k], r.g_2r[plane])
+        sum_2 = Sum(lambda t: r.g_2.at[t, k], r.got_2)
+        sum_2.start(0)
 
         for step in range(1, nc):
-            chip_send(lambda other: dm_s.at[other], dm_r, dm_base, step).wait()
+            chip_send(lambda other: sum_s.at[other], sum_r, dm_base, step).wait()
         da_all = r.da_all
 
         def back_norm2(g):
             rows = sub_rows(g)
-            d_m = dm_r[0, rows, :].astype(F32)
+            d_m = sum_r[0, rows, :].astype(F32)
             for other in range(1, nc):
-                d_m = d_m + dm_r[other, rows, :].astype(F32)
+                d_m = d_m + sum_r[other, rows, :].astype(F32)
             normal, scale = ln_parts(r.after[rows, :])
             cot_now = r.cg[c, rows, :].astype(F32)
             d_after = cot_now + ln_back(normal, scale, d_m * (1.0 + own_row(4, g)))
@@ -894,13 +1020,14 @@
         da_base = reserve(nc - 1)
         for step in range(1, nc):
             chip_send(lambda other: da_all.at[c], da_all, da_base, step).start()
-
-        m_rows = m_all[...].reshape(group, width)
-        for h in range(2):
-            for lo, hi in column_cuts(ff_d):
-                value = dot_lt(m_rows, r.d_hid[h, :, :, lo:hi].reshape(group, hi - lo))
-                r.g_1[h, :, :, :, lo:hi] = value.astype(BF16).reshape(nc, 2, rows_d, hi - lo)
-        g1_core = wires.far(r.g_1.at[:, :, core_o], r.g_1r, core_dev)
+        sum_2.start(1)
+
+        g_1 = r.w_1
+        m_rows_all = all_rows(m_all)
+        for lo, hi in column_cuts(ff_c):
+            value = dot_lt(m_rows_all, r.d_hid[:, :, lo:hi].reshape(group, hi - lo))
+            g_1[:, :, :, lo:hi] = value.astype(BF16).reshape(nc, 2, rows_d, hi - lo)
+        g1_core = wires.far(g_1.at[:, core_o], r.g_1r, core_dev)
 
         for step in range(1, nc):
             chip_send(lambda other: br_s.at[other], br_r, br_base, step).wait()
@@ -917,25 +1044,21 @@
 
         loop(n_sub, finish_out)
         g1_core.wait()
-        for h in range(2):
-            for chip in range(nc):
-                value = r.g_1[h, chip, k].astype(F32) + r.g_1r[h, chip].astype(F32)
-                r.g_1[h, chip, k] = value.astype(BF16)
-        f1_rows[pl.ds(per_1 * c, per_1)] = r.g_1[:, c, k]
-        y1_far = [
-            wires.far(r.g_1.at[:, other, k], f1_rows.at[pl.ds(per_1 * c, per_1)], peer)
-            for other, peer in chip_peers
-        ]
+        for chip in range(nc):
+            g_1[chip, k] = add_low(g_1[chip, k], r.g_1r[chip])
+        y_1 = r.f1_z
+        y_1[c] = g_1[c, k]
+        y1_far = [wires.far(g_1.at[other, k], y_1.at[c], peer) for other, peer in chip_peers]
+        sum_2.start(2)
 
         back_base = reserve(nc - 1)
 
         def attend_back(step):
             blk = xor_of(c, step, nc)
-
-            @pl.when(step != 0)
-            def _():
-                chip_send(lambda other: da_all.at[c], da_all, da_base, step).wait_recv()
-
+            when(
+                step != 0,
+                lambda: chip_send(lambda other: da_all.at[c], da_all, da_base, step).wait_recv(),
+            )
             d_mix = dot_rt(da_all[blk], r.w_p[...]).astype(BF16)
             q_now, k_now, v_now = r.qkv[0, blk], r.qkv[1, blk], r.qkv[2, blk]
             d_q = jnp.zeros((own, chip_w), F32)
@@ -957,59 +1080,46 @@
             r.d_qkv[1, blk] = d_k
             r.d_qkv[2, blk] = d_v
             part = dot_rt(d_q, weight_q(0)) + dot_rt(d_k, weight_q(1)) + dot_rt(d_v, weight_q(2))
-            part = part.astype(BF16)
-
-            @pl.when(step != 0)
-            def _():
-                sum_s[blk] = part
-                chip_send(lambda other: sum_s.at[other], sum_r, back_base, step).start()
-
-            @pl.when(step == 0)
-            def _():
-                sum_r[c] = part
+            hand_on(step, blk, part.astype(BF16), sum_s, sum_r, back_base)
 
         loop(nc, attend_back)
         for step in range(1, nc):
             chip_send(lambda other: da_all.at[c], da_all, da_base, step).wait_send()
-
         wait_all(y1_far)
-        z1_far = [
-            wires.far(f1_rows.at[pl.ds(per_1 * other, per_1)], r.z_1.at[f], peer)
-            for other, peer in plane_peers
-        ]
-
-        a_rows = r.a_in[...].reshape(group, width)
+        sum_1 = Sum(lambda t: y_1.at[t], r.got_1)
+        sum_1.start(0)
+
+        g_q, g_p = w_q, r.w_p
+        a_rows = all_rows(r.a_in)
         q_core_back = []
         for kind in range(3):
             for lo, hi in column_cuts(chip_w):
                 value = dot_lt(a_rows, r.d_qkv[kind, :, :, lo:hi].reshape(group, hi - lo))
-                r.g_q[kind, :, :, :, lo:hi] = value.astype(BF16).reshape(nc, 2, rows_d, hi - lo)
-            q_core_back.append(wires.far(r.g_q.at[kind, :, core_o], r.g_qr.at[kind], core_dev))
-        da_rows = da_all[...].reshape(group, width)
-        value = dot_lt(r.mixed[...].reshape(group, chip_w), da_rows).astype(BF16)
-        r.g_p[...] = value.reshape(2, rows_d, width)
-        p_core_back = wires.far(r.g_p.at[core_o], r.g_pr, core_dev)
+                g_q[kind, :, :, :, lo:hi] = value.astype(BF16).reshape(nc, 2, rows_d, hi - lo)
+            q_core_back.append(wires.far(g_q.at[kind, :, core_o], r.g_qr.at[kind], core_dev))
+        g_p[...] = dot_lt(all_rows(r.mixed), all_rows(da_all)).astype(BF16)
+
+        def own_side(ref, side):
+            return ref.at[pl.ds(pl.multiple_of(side * rows_d, SUB), rows_d)]
+
+        p_core_back = wires.far(own_side(g_p, core_o), r.g_pr, core_dev)
         yq_far = []
         for kind in range(3):
             q_core_back[kind].wait()
             for chip in range(nc):
-                value = r.g_q[kind, chip, k].astype(F32) + r.g_qr[kind, chip].astype(F32)
-                r.g_q[kind, chip, k] = value.astype(BF16)
-            q_rows[kind * nc + c] = r.g_q[kind, c, k]
+                g_q[kind, chip, k] = add_low(g_q[kind, chip, k], r.g_qr[kind, chip])
+            q_rows[kind * nc + c] = g_q[kind, c, k]
             for other, peer in chip_peers:
-                yq_far.append(
-                    wires.far(r.g_q.at[kind, other, k], q_rows.at[kind * nc + c], peer)
-                )
+                yq_far.append(wires.far(g_q.at[kind, other, k], q_rows.at[kind * nc + c], peer))
         p_core_back.wait()
-        r.g_p[k] = (r.g_p[k].astype(F32) + r.g_pr[...].astype(F32)).astype(BF16)
-        zp_far = [
-            wires.far(
-                r.g_p.at[k, :, pl.ds(pl.multiple_of(other * step_p, 128), pad_p)],
-                r.z_p.at[f],
-                peer,
-            )
-            for other, peer in plane_peers
-        ]
+        p_line.sent(p_in)
+        y_p = r.p_got
+        total = add_low(own_side(g_p, k)[...], r.g_pr[...])
+        for plane in range(nf):
+            y_p[k, plane] = total[:, plane * cols_f : (plane + 1) * cols_f]
+        sum_p = Sum(lambda t: y_p.at[k, t], r.got_p)
+        sum_p.start(0)
+        sum_1.start(1)
 
         for step in range(1, nc):
             chip_send(lambda other: sum_s.at[other], sum_r, back_base, step).wait()
@@ -1027,104 +1137,140 @@
             r.sub[1, at, :] = jnp.sum(d_a * normal, axis=0, keepdims=True)
 
         loop(n_sub, back_norm1)
+        hot_turned = own_hot.astype(F32).T.astype(BF16)
         for kind in range(6):
-            r.d_mod[kind] = lax.dot_general(
-                own_hot, r.sub[kind], (((0,), (0,)), ((), ())),
-                precision=PRECISE, preferred_element_type=F32,
-            )
+            r.m_tab[:, width * kind : width * (kind + 1)] = dot3(hot_turned, r.sub[kind])
+        for plane in range(nf):
+            r.d_cut[plane] = r.m_tab[:, ada_w * plane : ada_w * (plane + 1)]
         ones_own = jnp.ones((8, own), BF16)
         ones_all = jnp.ones((8, group), BF16)
         r.d_bias[...] = jnp.zeros((8, width), F32)
         r.d_bias[0:1, :] = dot(ones_own, da_all[c])[0:1]
         r.d_bias[1:2, :] = dot(ones_own, r.dbr[c])[0:1]
-        for at, kind in ((2, 0), (3, 2)):
-            sums = dot(ones_all, r.d_qkv[kind].reshape(group, chip_w))
-            r.d_bias[at : at + 1, 0:chip_w] = sums[0:1]
-        for h in range(2):
-            sums = dot(ones_all, r.d_hid[h].reshape(group, ff_d))
-            r.d_bias[4 + h : 5 + h, 0:ff_d] = sums[0:1]
-
+        r.d_bias[2:3, 0:chip_w] = dot(ones_all, all_rows(r.d_qkv.at[0]))[0:1]
+        r.d_bias[3:4, 0:chip_w] = dot(ones_all, all_rows(r.d_qkv.at[2]))[0:1]
+
+        ones_ff = dot(ones_all, all_rows(r.d_hid))[0:1]
+        r.d_bias[4:5, :] = ones_ff[:, :width]
+        for part in range(1, ff_c // width):
+            r.d_bias[4 + part : 5 + part, :] = ones_ff[:, part * width : (part + 1) * width]
         small = []
         for other, peer in plane_peers:
-            small.append(
-                wires.far(r.d_mod.at[pl.ds(6 * other // nf, 2)], r.dz.at[f], peer)
-            )
+            small.append(wires.far(r.d_cut.at[other], r.dz.at[f], peer))
             small.append(wires.far(r.d_bias, r.dzb.at[f], peer))
+        r.dz[f] = r.d_cut[f]
+        r.dzb[f] = r.d_bias[...]
+        sum_1.start(2)
         wait_all(yq_far)
-        zq_far = [
-            wires.far(q_rows.at[pl.ds(per_q * other, per_q)], r.z_q.at[f], peer)
-            for other, peer in plane_peers
-        ]
-        r.dz[f] = r.d_mod[pl.ds(6 * f // nf, 2)]
-        r.dzb[f] = r.d_bias[...]
+        q_line.sent(q_in)
+        y_q = r.q_z
+        for plane in range(nf):
+            row = [q_rows[3 * plane + i] for i in range(3)]
+            y_q[plane] = jnp.concatenate(row, axis=1)
+        sum_q = Sum(lambda t: y_q.at[t], r.got_q)
+        sum_q.start(0)
+        sum_p.start(1)
         wait_all(small)
         value, value_b = r.dz[0], r.dzb[0]
         for plane in range(1, nf):
             value = value + r.dz[plane]
             value_b = value_b + r.dzb[plane]
-        r.d_both[...] = value
+        r.d_both[...] = value.reshape(2, half, ada_w)
         r.d_bsum[...] = value_b
         small = [
             wires.far(r.d_both.at[core_o], r.m_core, core_dev),
             wires.far(r.d_bsum, r.d_coreb, core_dev),
         ]
+        sum_q.start(1)
+        sum_p.start(2)
         wait_all(small)
         m_chip[c] = r.d_both[k] + r.m_core[...]
-        o_bias[c] = r.d_bsum[...] + r.d_coreb[...]
+        r.d_chipb[c] = r.d_bsum[...] + r.d_coreb[...]
         small = []
         for _, peer in chip_peers:
             small.append(wires.far(m_chip.at[c], m_chip.at[c], peer))
-            small.append(wires.far(o_bias.at[c], o_bias.at[c], peer))
-
-        wait_all(z2_far)
-        r.z_2[f] = r.g_2[k, f]
-        total = r.z_2[0].astype(F32)
-        for plane in range(1, nf):
-            total = total + r.z_2[plane].astype(F32)
-        o_2[...] = total
-        wait_all(z1_far)
-        r.z_1[f] = f1_rows[pl.ds(per_1 * f, per_1)]
-        total = r.z_1[0].astype(F32)
-        for plane in range(1, nf):
-            total = total + r.z_1[plane].astype(F32)
-        o_1[...] = total
+            small.append(wires.far(r.d_chipb.at[c], r.d_chipb.at[c], peer))
+
+        sum_2.finish(r.all_2.at[k])
+        o2_swap = wires.far(r.all_2.at[k], r.all_2.at[k], core_dev)
         wait_all(small)
         value = m_chip[0]
         for chip in range(1, nc):
             value = value + m_chip[chip]
-        o_mod[k] = value
-        m_end = wires.far(o_mod.at[k], o_mod.at[k], core_dev)
-        wait_all(zp_far)
+        r.d_tot[k] = value
+        d_swap = wires.far(r.d_tot.at[k], r.d_tot.at[k], core_dev)
+        sum_q.start(2)
+        d_swap.wait()
+        d_cols = r.d_tot[...].reshape(n_rows, ada_w)
+        silu_turned = silu_in[...].astype(F32).T.astype(BF16)
+        o_bada[...] = jnp.sum(d_cols, axis=0, keepdims=True)
+        value, total = d_cols, None
+        for _ in range(3):
+            term = value.astype(BF16)
+            value = value - term.astype(F32)
+            part = dot_rt(term, r.ada[...])
+            total = part if total is None else total + part
+        r.c_part[f] = total
+        c_far = [wires.far(r.c_part.at[f], r.c_part.at[f], peer) for _, peer in plane_peers]
+        for lo, hi in column_cuts(ada_w):
+            o_ada[:, lo:hi] = dot3(silu_turned, d_cols[:, lo:hi])
+        sum_1.finish(o_1)
+        o2_swap.wait()
+
+        def own_columns(lo):
+            def body():
+                both = r.all_2[:, :, lo : lo + ff_d].reshape(cols_f, ff_d)
+                o_2[...] = both.T
+
+            return body
+
+        when(k == 0, own_columns(0))
+        when(k == 1, own_columns(ff_d))
+        wait_all(c_far)
+        value = r.c_part[0]
+        for plane in range(1, nf):
+            value = value + r.c_part[plane]
+        r.c_all[c, k] = value
+        wait_all([wires.far(r.c_all.at[c, k], r.c_all.at[c, k], peer) for _, peer in chip_peers])
+        c_swap = wires.far(r.c_all.at[:, k], r.c_all.at[:, k], core_dev)
+        sum_p.finish(o_p)
+        own_sums = r.d_chipb[0]
+        for chip in range(1, nc):
+            own_sums = own_sums + r.d_chipb[chip]
         for plane in range(nf):
 
-            @pl.when(f == plane)
-            def _():
-                r.z_p[plane] = r.g_p[k, :, plane * step_p : plane * step_p + pad_p]
-
-        total = r.z_p[0].astype(F32)
-        for plane in range(1, nf):
-            total = total + r.z_p[plane].astype(F32)
-        o_p[...] = total
-        wait_all(zq_far)
-        r.z_q[f] = q_rows[pl.ds(per_q * f, per_q)]
-        total = r.z_q[0].astype(F32)
-        for plane in range(1, nf):
-            total = total + r.z_q[plane].astype(F32)
-        o_q[...] = total
-        m_end.wait()
+            def bias_columns(plane=plane):
+                at = plane * cols_f
+                o_bp[...] = own_sums[0:1, at : at + cols_f]
+                o_b2[...] = own_sums[1:2, at : at + cols_f]
+                kind, chip = 2 * plane // nc, 2 * plane % nc
+                o_bqv[...] = jnp.concatenate(
+                    [r.d_chipb[chip + i, 2 + kind : 3 + kind, 0:chip_w] for i in range(2)], axis=1
+                )
+                parts = [r.d_chipb[plane, 4 + i : 5 + i, :] for i in range(ff_c // width)]
+                o_b1[...] = parts[0] if len(parts) == 1 else jnp.concatenate(parts, axis=1)
+
+            when(f == plane, bias_columns)
+        c_swap.wait()
+        d_silu = jnp.concatenate([r.c_all[f, 0], r.c_all[f, 1]], axis=1)
+        cond_now = cond_in[...]
+        gate = 1.0 / (1.0 + jnp.exp(-cond_now))
+        o_cond[...] = d_silu * (gate * (1.0 + cond_now * (1.0 - gate)))
+        sum_q.finish(o_q)
+        f2_line.sent()
         assert wires.remote_count <= n_sem and wires.local_count <= 32
 
     return pl.pallas_call(
         kernel,
         out_shape=outs,
-        in_specs=[ANYWHERE] * 5 + [ON_CHIP] + [ANYWHERE] * 4,
+        in_specs=[ANYWHERE] * 2 + [ON_CHIP] * 4 + [ANYWHERE] * 5,
         out_specs=tuple([ON_CHIP] * len(outs)),
         scratch_shapes=list(scratch.values()),
         compiler_params=pltpu.CompilerParams(
             collective_id=0, has_side_effects=True, vmem_limit_bytes=63 * 2**20
         ),
         name="block",
-    )(x, cot, mask, hot, bias, mod, wq, w1, wp, w2)
+    )(x, cot, ids, bias, silu_part, cond_own, w_ada, wq, wp, w1, w2)
 
 
 def fits_block(n_dp, nf, width, ff, own, micro):
@@ -1191,62 +1337,33 @@
         return cond_grad, grad_w_ada, jnp.sum(d_cols, axis=0)
 
     if fits_block(n_dp, nf, width, ff, own, micro):
-        n_rows = micro * clips
-        window = f * ada_w - 6 * f // nf * width
-        pad_p = width // nf // 128 * 128 + 128
-        dims.step_p = (width - pad_p) // (nf - 1)
-        shift_p = f * (cols_f - dims.step_p)
-
-        def lanes(value, start):
-            empty = jnp.zeros(value.shape[:-1] + (width,), F32)
-            return lax.dynamic_update_slice_in_dim(empty, value.astype(F32), start, value.ndim - 1)
-
-        mod_send = jnp.zeros((n_rows, 2 * width), F32)
-        mod_send = lax.dynamic_update_slice_in_dim(mod_send, mod_part, window, 1)
-        mod_send = mod_send.reshape(n_rows, 2, width).transpose(1, 0, 2)
-        p_send = jnp.zeros((rows_d, pad_p), BF16)
-        p_send = lax.dynamic_update_slice_in_dim(p_send, w_proj, shift_p, 1)
-        bias_send = jnp.concatenate(
-            [
-                lanes(b_proj[None], f * cols_f),
-                lanes(b_fc2[None], f * cols_f),
-                lanes(b_qv.reshape(2, chip_w), 0),
-                lanes(b_fc1.reshape(2, ff_d), 0),
-                jnp.zeros((2, width), F32),
-            ]
+        bias_send = jnp.concatenate([b_qv, b_proj, b_fc1, b_fc2, b_ada]).astype(F32)[None]
+        order = jnp.arange(micro, dtype=jnp.int32)[:, None]
+        pair_rows = jnp.stack(
+            [(frame_of_slot + order * 65536).reshape(own), (clip_of_slot + order * clips).reshape(own)]
         )
-        frames = frame_of_slot + jnp.arange(micro, dtype=jnp.int32)[:, None] * 65536
-        frames = frames.reshape(own)
-        mask = (frames[:, None] == frames[None, :]).astype(BF16)
-        row = clip_of_slot + jnp.arange(micro, dtype=jnp.int32)[:, None] * clips
-        row = row.reshape(own // SUB, SUB)[:, :1].astype(F32)
-        hot = jnp.broadcast_to(row, (own // SUB, 128))
-        output, input_grad, o_q, o_1, o_p, o_2, o_mod, o_bias = block_kernel(
-            dims, patches.reshape(own, width), cotangent.reshape(own, width), mask, hot, bias_send,
-            mod_send, q_send, f1_send, p_send, f2_send,
+        id_rows = jnp.concatenate([pair_rows.astype(F32), jnp.zeros((6, own), F32)])
+        (
+            output, input_grad, cond_grad, grad_ada, grad_b_ada, grad_qkv, grad_b_qv,
+            grad_proj, grad_b_proj, grad_fc1, grad_b_fc1, grad_fc2, grad_b_fc2,
+        ) = block_kernel(
+            dims, patches.reshape(own, width), cotangent.reshape(own, width), id_rows, bias_send,
+            silu_part, cond_own, w_ada, w_qkv, w_proj, w_fc1, w_fc2,
         )
-        d_cols = o_mod.transpose(1, 0, 2).reshape(n_rows, 2 * width)
-        d_cols = lax.dynamic_slice_in_dim(d_cols, window, ada_w, 1)
-        cond_grad, grad_w_ada, grad_b_ada = ada_outputs(d_cols)
-        own_bias = jnp.sum(o_bias[:, :2], axis=0)
-        own_bias = lax.dynamic_slice_in_dim(own_bias, f * cols_f, cols_f, 1)
-        qv = jnp.concatenate([o_bias[:, 2, :chip_w], o_bias[:, 3, :chip_w]])
-        qv = lax.dynamic_slice_in_dim(qv, 2 * f, 2, 0).reshape(2 * chip_w)
-        fc1 = lax.dynamic_index_in_dim(o_bias[:, 4:6, :ff_d], f, 0, False).reshape(2 * ff_d)
         return (
             output.reshape(patches.shape),
             input_grad.reshape(patches.shape),
-            cond_grad,
-            grad_w_ada,
-            grad_b_ada,
-            o_q.transpose(1, 0, 2).reshape(rows_d, 3 * width // nf),
-            qv,
-            lax.dynamic_slice_in_dim(o_p, shift_p, cols_f, 1),
-            own_bias[0],
-            o_1.transpose(1, 0, 2).reshape(rows_d, ff // nf),
-            fc1,
-            o_2.T,
-            own_bias[1],
+            cond_grad.reshape(micro, clips, cols_f),
+            grad_ada,
+            grad_b_ada[0],
+            grad_qkv,
+            grad_b_qv[0],
+            grad_proj,
+            grad_b_proj[0],
+            grad_fc1,
+            grad_b_fc1[0],
+            grad_fc2,
+            grad_b_fc2[0],
         )
 
     ids = jnp.stack([frame_of_slot.reshape(own), clip_of_slot.reshape(own)])

time: 329 us -> 270 us (0.82)
  Pallas kernels: 298 us -> 251 us
  local copies, waits for them, and re-layouts: 21.9 us -> 13.8 us
    pallas_call x2 -> x1, Pallas kernels: 298 us -> 251 us  [block_kernel(): pl.pallas_call(kernel, out_shape=outs, in_specs=[ANYWHERE] * 2 + [ON_CHIP...]
    unnamed x40 -> x49, local copies, waits for them, and re-layouts: 4.62 us -> 12.2 us
    reshape x12 -> x0, local copies, waits for them, and re-layouts: 6.88 us -> none  [the longest x1 1.33 us: per_device(): o_1.transpose(1, 0, 2).reshape(rows_d, ff // nf)]
where the time goes in v3:
time: 270 us
  Pallas kernels  251 us (93%)
  local copies, waits for them, and re-layouts  13.8 us (5%)
  other arithmetic  4.51 us (2%)
    pallas_call x1, Pallas kernels, block_kernel(): pl.pallas_call(kernel, out_shape=outs, in_specs=[ANYWHERE] * 2 + [ON_CHIP...  251 us
    unnamed x49, local copies, waits for them, and re-layouts  12.2 us

profile of v3, /device:TPU:0, one launch (start us, length us, event | category | flops | bytes accessed | tf_op | source)
XLA Modules:
  0.0 269.7 jit_solution(4359077653587147859)
XLA Ops:
  0.7 0.0 copy-start.7
  0.7 0.6 copy-done.16
  1.3 0.1 broadcast_add_fusion.1
  1.4 0.1 stack_reshape.6
  1.5 0.1 broadcast_add_fusion
  1.6 0.1 stack_reshape.7
  1.7 0.6 concatenate.23.ids_in
  2.3 0.1 concatenate.29
  2.5 0.6 convert_element_type.17.bias_in
  3.1 0.7 multiply_convert_fusion.silu_in
  3.8 0.7 constant_dynamic-slice_fusion.cond_in
  4.5 1.9 copy.28.f2_in
  6.4 250.6 %block.1 = (bf16[128,1152]{1,0:T(8,128)(2,1)}, bf16[128,1152]{1,0:T(8,128)(2,1)}, f32[16,288]{1,0:T(8,128)}, f32[144,1728]{1,0:T(8,128)}, f32[1,1728]{1,0:T(1,12...) custom-call(bf16[128,1152]{1,0:T(8,128)(2,1)} %bitcast.6, ...), custom_call_target="tpu_custom_call" | custom-call | tf_op jit(solution)/shard_map/block/pallas_call | solution.py:1263
  257.1 0.6 copy-done.15
  257.7 0.6 reduce.2
  258.3 0.6 reduce.4
  258.9 0.6 reduce.1
  259.5 0.6 reduce
  260.1 0.1 copy-done.9
  260.2 0.6 reduce.3
  260.8 2.4 copy.29
  263.3 0.7 copy.37
  264.0 0.4 copy-done.3
  264.3 0.7 copy.38
  265.1 0.0 copy-done.6
  265.1 0.6 copy.39
  265.7 1.0 copy.40
  266.7 0.4 copy-done.2
  267.1 0.8 copy.41
  267.9 0.3 copy-done.5
  268.2 0.7 copy.42
  268.9 0.8 copy.43
  (40 shorter events, 0.1 us)
Async XLA Ops:
  0.6 0.7 copy-start.16
  0.7 0.8 copy-start.17
  0.7 1.0 copy-start.18
  0.7 1.0 copy-start.19
  0.7 1.0 copy-start.13
  0.7 1.6 copy-start.10
  0.7 1.6 copy-start.11
  0.7 2.4 copy-start.7
  257.0 0.7 copy-start.15
  257.0 1.3 copy-start.14
  257.1 1.9 copy-start.12
  257.7 1.8 copy-start.8
  259.5 0.7 copy-start.9
  260.8 2.5 copy-start.4
  260.8 4.9 %copy-start = (f32[144,1728]{1,0:T(8,128)S(1)}, f32[144,1728]{1,0:T(8,128)}, u32[]{:S(2)}) copy-start(f32[144,1728]{1,0:T(8,128)} %get-tuple-element.68) | copy-start | bytes 2985988
  263.3 1.1 copy-start.3
  264.3 0.7 copy-start.6
  265.7 1.4 copy-start.2
  267.1 1.1 copy-start.5
  267.1 1.8 copy-start.1

commit v4 on v3

--- a/solution.py
+++ b/solution.py
@@ -470,7 +470,9 @@
         own_tab=pltpu.VMEM((6, n_sub, width), F32),
         q_z=pltpu.VMEM((nf, rows_d, q_w), BF16),
         q_rows=pltpu.VMEM((nf * 3, rows_d, chip_w), BF16),
-        w_q=pltpu.VMEM((3, nc, 2, rows_d, chip_w), BF16),
+        q_got=pltpu.VMEM((3, nc, rows_d, chip_w), BF16),
+        w_q=pltpu.VMEM((nc, 2, rows_d, q_w), BF16),
+        y_got=pltpu.VMEM((nc, rows_d, q_w), BF16),
         f1_z=pltpu.VMEM((nf, rows_d, ff_c), BF16),
         w_1=pltpu.VMEM((nc, 2, rows_d, ff_c), BF16),
         p_got=pltpu.VMEM((2, nf, rows_d, cols_f), BF16),
@@ -484,9 +486,11 @@
         probs=pltpu.VMEM((nc * heads, own, own), F32),
         mixed=pltpu.VMEM((nc, own, chip_w), BF16),
         sum_s=pltpu.VMEM(tokens, BF16),
-        sum_r=pltpu.VMEM(tokens, BF16),
+        sum_r=pltpu.VMEM((2, own, width), BF16),
+        sum_st=pltpu.VMEM((2, own // 2, width), BF16),
         br_s=pltpu.VMEM(tokens, BF16),
-        br_r=pltpu.VMEM(tokens, BF16),
+        br_r=pltpu.VMEM((2, own, width), BF16),
+        br_st=pltpu.VMEM((2, own // 2, width), BF16),
         m_all=pltpu.VMEM(tokens, BF16),
         da_all=pltpu.VMEM(tokens, BF16),
         attn=pltpu.VMEM((own, width), F32),
@@ -497,11 +501,11 @@
         act=pltpu.VMEM((nc, own, ff_c), BF16),
         d_hid=pltpu.VMEM((nc, own, ff_c), BF16),
         dbr=pltpu.VMEM(tokens, BF16),
-        d_qkv=pltpu.VMEM((3, nc, own, chip_w), BF16),
+        d_qkv=pltpu.VMEM((nc, own, q_w), BF16),
         g_2=pltpu.VMEM((nf, 2, rows_d, ff_c), BF16),
         g_2r=pltpu.VMEM((nf, rows_d, ff_c), BF16),
         g_1r=pltpu.VMEM((nc, rows_d, ff_c), BF16),
-        g_qr=pltpu.VMEM((3, nc, rows_d, chip_w), BF16),
+        g_qr=pltpu.VMEM((nc, rows_d, q_w), BF16),
         g_pr=pltpu.VMEM((rows_d, width), BF16),
         got_q=pltpu.VMEM((2, nf - 1, rows_d, q_w), BF16),
         got_1=pltpu.VMEM((2, nf - 1, rows_d, ff_c), BF16),
@@ -509,11 +513,12 @@
         got_2=pltpu.VMEM((2, nf - 1, rows_d, ff_c), BF16),
         all_2=pltpu.VMEM((2, rows_d, ff_c), F32),
         sub=pltpu.VMEM((6, n_sub, width), F32),
-        d_cut=pltpu.VMEM((nf, n_rows, ada_w), F32),
+        d_part=pltpu.VMEM((2, half, 6 * width), F32),
+        d_core=pltpu.VMEM((half, 6 * width), F32),
+        d_cut=pltpu.VMEM((nf, half, ada_w), F32),
         d_bias=pltpu.VMEM((8, width), F32),
-        dz=pltpu.VMEM((nf, n_rows, ada_w), F32),
+        dz=pltpu.VMEM((nf, half, ada_w), F32),
         dzb=pltpu.VMEM((nf, 8, width), F32),
-        d_both=pltpu.VMEM((2, half, ada_w), F32),
         d_tot=pltpu.VMEM((2, half, ada_w), F32),
         d_bsum=pltpu.VMEM((8, width), F32),
         d_coreb=pltpu.VMEM((8, width), F32),
@@ -538,12 +543,15 @@
         chip_peers = [place.peer(CHIP, step) for step in range(1, nc)]
         plane_peers = [place.peer(PLANE, step) for step in range(1, nf)]
 
-        def loop(count, body):
+        def loop(count, body, unroll=1):
             def run(i, carry):
                 body(i)
                 return carry
 
-            lax.fori_loop(0, count, run, 0)
+            lax.fori_loop(0, count, run, 0, unroll=unroll)
+
+        def loop_rows(body):
+            loop(n_sub, body, 2)
 
         def when(condition, body):
             pl.when(condition)(body)
@@ -566,10 +574,93 @@
                 device_id_type=MESH_ID,
             )
 
-        def chip_send(src, dst, base, step):
-            other, device = place.peer(CHIP, step)
-            at = base + step - 1
-            return pair(src(other), dst.at[c], device, at, at)
+        chip_x, dev_x = place.peer(CHIP, 1)
+        chip_y, dev_y = place.peer(CHIP, 2)
+        chip_d, _ = place.peer(CHIP, 3)
+        first_half, second_half = pl.ds(0, own // 2), pl.ds(own // 2, own // 2)
+
+        class Share:
+            def __init__(self, ref, src=None):
+                def copy(chip, rows, device, at, own_src=None):
+                    from_ref = ref.at[chip, rows] if own_src is None else own_src.at[rows]
+                    return pair(from_ref, ref.at[chip, rows], device, at, at)
+
+                at = reserve(6)
+                self.x_a = copy(c, first_half, dev_x, at, src)
+                self.x_b = copy(c, second_half, dev_x, at + 1, src)
+                self.y_b = copy(c, second_half, dev_y, at + 2, src)
+                self.y_a = copy(c, first_half, dev_y, at + 3, src)
+                self.on_y = copy(chip_x, first_half, dev_y, at + 4)
+                self.on_x = copy(chip_y, second_half, dev_x, at + 5)
+
+            def start(self):
+                for item in (self.x_a, self.y_b, self.x_b, self.y_a):
+                    item.start()
+
+            def relay(self):
+                self.x_a.wait_recv()
+                self.on_y.start()
+                self.y_b.wait_recv()
+                self.on_x.start()
+
+            def arrive(self, step):
+                if step == 1:
+                    self.x_b.wait_recv()
+                elif step == 2:
+                    self.y_a.wait_recv()
+                else:
+                    self.on_y.wait_recv()
+                    self.on_x.wait_recv()
+
+            def sent(self):
+                for item in (self.x_a, self.x_b, self.y_b, self.y_a, self.on_y, self.on_x):
+                    item.wait_send()
+
+        class Merge:
+            def __init__(self, terms, got, stage):
+                self.terms, self.got, self.stage = terms, got, stage
+                at = reserve(6)
+                self.d_x = pair(terms.at[chip_d, first_half], stage.at[0], dev_x, at, at)
+                self.d_y = pair(terms.at[chip_d, second_half], stage.at[1], dev_y, at + 1, at + 1)
+
+                def copy(chip, rows, to, device, index):
+                    return pair(
+                        terms.at[chip, rows], got.at[to, rows], device, at + index, at + index
+                    )
+
+                self.x_a = copy(chip_x, first_half, 0, dev_x, 2)
+                self.x_b = copy(chip_x, second_half, 0, dev_x, 3)
+                self.y_b = copy(chip_y, second_half, 1, dev_y, 4)
+                self.y_a = copy(chip_y, first_half, 1, dev_y, 5)
+
+            def put(self, step, blk, part):
+                self.terms[blk] = part
+
+                def far():
+                    self.d_x.start()
+                    self.d_y.start()
+
+                when(step == 3, far)
+                when(step == 2, self.y_b.start)
+                when(step == 1, self.x_a.start)
+
+            def combine(self):
+                self.d_y.wait()
+                ref = self.terms.at[chip_x, second_half]
+                ref[...] = add_low(ref[...], self.stage[1])
+                self.x_b.start()
+                self.d_x.wait()
+                ref = self.terms.at[chip_y, first_half]
+                ref[...] = add_low(ref[...], self.stage[0])
+                self.y_a.start()
+
+            def finish(self):
+                for item in (self.x_a, self.x_b, self.y_b, self.y_a):
+                    item.wait()
+
+            def rows(self, at):
+                value = self.terms[c, at, :].astype(F32) + self.got[0, at, :].astype(F32)
+                return value + self.got[1, at, :].astype(F32)
 
         up, down = (place.dp, f + 1), (place.dp, f - 1)
 
@@ -661,21 +752,19 @@
                     for _, _, condition, _, copy in self.both(step):
                         when(condition, copy.wait_send)
 
-        greet(place, (CORE, CHIP, PLANE))
+        barrier = pltpu.get_barrier_semaphore()
+        peers = [core_dev] + [peer for _, peer in chip_peers + plane_peers]
+        for peer in peers:
+            pl.semaphore_signal(barrier, inc=1, device_id=peer, device_id_type=MESH_ID)
 
         q_line = Gather(lambda g: r.q_z.at[g])
         p_line = Gather(lambda g: r.p_got.at[k, g])
         f1_line = Gather(lambda g: r.f1_z.at[g])
         f2_line = Gather(lambda g: r.w_2.at[g, k])
-        q_line.start(0, q_in)
         ada_near = wires.near(ada_in, r.ada)
         q_near = wires.near(q_in, r.q_z.at[f])
         f2_near = wires.near(f2_in, r.f2_nat)
         first = []
-        for _, peer in chip_peers:
-            first.append(wires.far(ids_in, r.idsg.at[c], peer))
-        for _, peer in plane_peers:
-            first.append(wires.far(bias_in, r.biasg.at[f], peer))
         first.append(wires.near(x_in, r.xg.at[c]))
         first.append(wires.near(c_in, r.cg.at[c]))
         p_near = wires.near(p_in, r.p_got.at[k, f])
@@ -686,7 +775,18 @@
         ada_bias = jnp.where(place.dp == 0, bias_in[:, n_bias - ada_w :], 0.0)
         value = dot(silu_in[...], r.ada[...]) + ada_bias
         r.m_part[...] = value.reshape(2, half, ada_w)
+        f2_near.wait()
+        turned = r.f2_nat[...].T
+        r.f2_half[...] = turned.reshape(2, rows_d, ff_d)
+        q_near.wait()
+        pl.semaphore_wait(barrier, len(peers))
         m_first = wires.far(r.m_part.at[core_o], r.m_core, core_dev)
+        q_line.start(0, q_in)
+        for _, peer in chip_peers:
+            first.append(wires.far(ids_in, r.idsg.at[c], peer))
+        f2_swap = wires.far(r.f2_half.at[core_o], r.f2_got, core_dev)
+        for _, peer in plane_peers:
+            first.append(wires.far(bias_in, r.biasg.at[f], peer))
 
         w_q, q_rows = r.w_q, r.q_rows
         q_base = reserve(3 * nc)
@@ -696,7 +796,7 @@
         def q_copies(plane, i):
             piece = 3 * plane + i
             kind, chip = piece // nc, piece % nc
-            src, dst = q_rows.at[piece], w_q.at[kind, c, k]
+            src, dst = q_rows.at[piece], r.q_got.at[kind, c]
             far = pair(src, dst, (chip * 2 + k, f), q_base + kind * nc + chip, q_base + kind * nc + c)
             return chip, far, pltpu.make_async_copy(src, dst, r.local.at[q_local + kind])
 
@@ -721,14 +821,13 @@
             when(plane != c, far.start)
             when(plane == c, near.start)
 
-        q_near.wait()
-        q_forward(f)
         m_first.wait()
         m_chip = r.m_chip
         m_chip[c] = r.m_part[k] + r.m_core[...]
         m_second = [wires.far(m_chip.at[c], m_chip.at[c], peer) for _, peer in chip_peers]
-        for _, peer in chip_peers:
-            first.append(wires.far(x_in, r.xg.at[c], peer))
+        q_forward(f)
+        x_share = Share(r.xg, x_in)
+        x_share.start()
         q_line.arrive(0, q_forward)
         q_line.start(1)
         wait_all(m_second)
@@ -737,11 +836,8 @@
             total = total + m_chip[other]
         r.m_z[f, k] = total
         m_third = [wires.far(r.m_z.at[f, k], r.m_z.at[f, k], peer) for _, peer in plane_peers]
+        x_share.relay()
         p_line.start(0, p_in)
-        f2_near.wait()
-        turned = r.f2_nat[...].T
-        r.f2_half[...] = turned.reshape(2, rows_d, ff_d)
-        f2_swap = wires.far(r.f2_half.at[core_o], r.f2_got, core_dev)
         q_line.arrive(1, q_forward)
         q_line.start(2)
         p_line.arrive(0)
@@ -757,14 +853,26 @@
 
         when(k == 0, join_even)
         when(k == 1, join_odd)
+        f2_base = reserve(nf)
+
+        def f2_across(plane):
+            ref = r.w_2.at[plane, k]
+            return pair(ref, ref, core_dev, f2_base + plane, f2_base + plane)
+
+        def f2_forward(plane):
+            f2_across(plane).start()
+
         q_line.arrive(2, q_forward)
         p_line.arrive(1)
         p_line.start(2)
         wait_all(m_third)
         m_last = wires.far(r.m_z.at[:, k], r.m_z.at[:, k], core_dev)
         f2_line.start(0)
+        f2_forward(f)
 
         wait_all(first)
+        for step in range(1, nc):
+            x_share.arrive(step)
         m_last.wait()
         m_rows = [r.m_z[plane].reshape(n_rows, ada_w) for plane in range(nf)]
         r.m_tab[...] = jnp.concatenate(m_rows, axis=1)
@@ -798,19 +906,22 @@
                 value = normal * (1.0 + tab_row(1, blk, g)) + tab_row(0, blk, g)
                 r.a_in[blk, rows, :] = value.astype(BF16)
 
-            loop(n_sub, body)
+            loop_rows(body)
 
         loop(nc, make_a)
 
-        q_core = []
         for kind in range(3):
             for other, _ in chip_peers:
-                ref = w_q.at[kind, other, k]
+                ref = r.q_got.at[kind, other]
                 at = q_base + kind * nc + other
                 pair(ref, ref, core_dev, at, at).wait()
-            ref = w_q.at[kind, c, k]
+            ref = r.q_got.at[kind, c]
             pltpu.make_async_copy(ref, ref, r.local.at[q_local + kind]).wait()
-            q_core.append(wires.far(w_q.at[kind, :, k], w_q.at[kind, :, k], core_dev))
+        q_core = []
+        for chip in range(nc):
+            row = [r.q_got[kind, chip] for kind in range(3)]
+            w_q[chip, k] = jnp.concatenate(row, axis=1)
+            q_core.append(wires.far(w_q.at[chip, k], w_q.at[chip, k], core_dev))
         p_line.arrive(2)
         p_near.wait()
         p_core = wires.far(r.p_got.at[k], r.p_got.at[k], core_dev)
@@ -818,7 +929,9 @@
         f1_forward(f)
         f1_line.arrive(0, f1_forward)
         f1_line.start(1)
-        c_far = [wires.far(c_in, r.cg.at[c], peer) for _, peer in chip_peers]
+        c_share = Share(r.cg, c_in)
+        c_share.start()
+        x_share.sent()
         p_core.wait()
         for side in range(2):
             row = [r.p_got[side, plane] for plane in range(nf)]
@@ -831,8 +944,8 @@
             for h in range(heads)
         ]
 
-        def weight_q(kind):
-            return w_q[kind].reshape(width, chip_w)
+        def weight_q():
+            return w_q[...].reshape(width, q_w)
 
         def qv_bias(plane):
             row = r.biasg[plane]
@@ -845,27 +958,16 @@
         bias_p = jnp.concatenate([r.biasg[g][:, at_p : at_p + cols_f] for g in range(nf)], axis=1)
         bias_o = jnp.concatenate([r.biasg[g][:, at_2 : at_2 + cols_f] for g in range(nf)], axis=1)
         bias_1 = r.biasg[c][:, at_1 : at_1 + ff_c]
-        sum_base = reserve(nc - 1)
-        sum_s, sum_r = r.sum_s, r.sum_r
-
-        def hand_on(step, blk, part, s_ref, r_ref, base):
-            def away():
-                s_ref[blk] = part
-                chip_send(lambda other: s_ref.at[other], r_ref, base, step).start()
-
-            def stay():
-                r_ref[c] = part
-
-            when(step != 0, away)
-            when(step == 0, stay)
+        zero = jnp.zeros_like(bias_q)
+        bias_qkv = jnp.concatenate([bias_q, zero, bias_v], axis=1)
+        attn_merge = Merge(r.sum_s, r.sum_r, r.sum_st)
 
         def attend(i):
-            step = (i + 1) % nc
+            step = nc - 1 - i
             blk = xor_of(c, step, nc)
-            a_now = r.a_in[blk]
-            r.qkv[0, blk] = (dot(a_now, weight_q(0)) + bias_q).astype(BF16)
-            r.qkv[1, blk] = dot(a_now, weight_q(1)).astype(BF16)
-            r.qkv[2, blk] = (dot(a_now, weight_q(2)) + bias_v).astype(BF16)
+            value = (dot(r.a_in[blk], weight_q()) + bias_qkv).astype(BF16)
+            for kind in range(3):
+                r.qkv[kind, blk] = value[:, chip_w * kind : chip_w * (kind + 1)]
             q_now, k_now, v_now = r.qkv[0, blk], r.qkv[1, blk], r.qkv[2, blk]
             frames = r.idsg[blk]
             same = frames.T[:, 0:1] == frames[0:1, :]
@@ -879,38 +981,36 @@
                 mixed = mixed + dot(share.astype(BF16), v_now * head_of[h])
             mixed = mixed.astype(BF16)
             r.mixed[blk] = mixed
-            hand_on(step, blk, dot(mixed, r.w_p[...]).astype(BF16), sum_s, sum_r, sum_base)
+            attn_merge.put(step, blk, dot(mixed, r.w_p[...]).astype(BF16))
 
         loop(nc, attend)
+        attn_merge.combine()
+        c_share.relay()
         f1_line.arrive(1, f1_forward)
         f1_line.start(2)
-        f2_line.arrive(0)
+        f2_line.arrive(0, f2_forward)
         f2_line.start(1)
 
-        for step in range(1, nc):
-            chip_send(lambda other: sum_s.at[other], sum_r, sum_base, step).wait()
+        attn_merge.finish()
 
         def after_attention(g):
             rows = sub_rows(g)
-            value = sum_r[0, rows, :].astype(F32)
-            for other in range(1, nc):
-                value = value + sum_r[other, rows, :].astype(F32)
-            value = value + bias_p
+            value = attn_merge.rows(rows) + bias_p
             r.attn[rows, :] = value
             after = r.xg[c, rows, :].astype(F32) + own_row(2, g) * value
             r.after[rows, :] = after
             normal, _ = ln_parts(after)
             r.m_all[c, rows, :] = (normal * (1.0 + own_row(4, g)) + own_row(3, g)).astype(BF16)
 
-        loop(n_sub, after_attention)
+        loop_rows(after_attention)
         m_all = r.m_all
-        m_base = reserve(nc - 1)
+        m_share = Share(m_all)
+        m_share.start()
+        f1_line.arrive(2, f1_forward)
+        f2_line.arrive(1, f2_forward)
+        f2_line.start(2)
         for step in range(1, nc):
-            chip_send(lambda other: m_all.at[c], m_all, m_base, step).start()
-        f1_line.arrive(2, f1_forward)
-        f2_line.arrive(1)
-        f2_line.start(2)
-        wait_all(c_far)
+            c_share.arrive(step)
 
         def make_dbr(blk):
             def body(g):
@@ -918,20 +1018,24 @@
                 value = r.cg[blk, rows, :].astype(F32) * tab_row(5, blk, g)
                 r.dbr[blk, rows, :] = value.astype(BF16)
 
-            loop(n_sub, body)
+            loop_rows(body)
 
         loop(nc, make_dbr)
+        m_share.relay()
+        f1_core = []
+        ref = r.w_1.at[c, k]
+        pltpu.make_async_copy(ref, ref, r.local.at[f1_local]).wait()
+        f1_core.append(wires.far(ref, ref, core_dev))
         for other, _ in chip_peers:
             ref = r.w_1.at[other, k]
             pair(ref, ref, core_dev, f1_base + other, f1_base + other).wait()
-        ref = r.w_1.at[c, k]
-        pltpu.make_async_copy(ref, ref, r.local.at[f1_local]).wait()
+            f1_core.append(wires.far(ref, ref, core_dev))
         f1_line.sent(f1_in)
-        f1_core = wires.far(r.w_1.at[:, k], r.w_1.at[:, k], core_dev)
-        f2_line.arrive(2)
-        f2_core = wires.far(r.w_2.at[:, k], r.w_2.at[:, k], core_dev)
-        f1_core.wait()
-        f2_core.wait()
+        c_share.sent()
+        f2_line.arrive(2, f2_forward)
+        wait_all(f1_core)
+        for plane in range(nf):
+            f2_across(plane).wait()
 
         def weight_1():
             return r.w_1[...].reshape(width, ff_c)
@@ -939,16 +1043,13 @@
         def weight_2():
             return r.w_2[...].reshape(width, ff_c)
 
-        dm_base = reserve(nc - 1)
-        br_base = reserve(nc - 1)
-        br_s, br_r = r.br_s, r.br_r
+        dm_merge = Merge(r.sum_s, r.sum_r, r.sum_st)
+        br_merge = Merge(r.br_s, r.br_r, r.br_st)
 
         def feed(step):
             blk = xor_of(c, step, nc)
-            when(
-                step != 0,
-                lambda: chip_send(lambda other: m_all.at[c], m_all, m_base, step).wait_recv(),
-            )
+            for at in range(1, nc):
+                when(step == at, functools.partial(m_share.arrive, at))
             r.hid[...] = dot(m_all[blk], weight_1()) + bias_1
 
             def gelu_rows(g):
@@ -957,20 +1058,18 @@
                 r.act[blk, rows, :] = value.astype(BF16)
                 r.slope[rows, :] = slope
 
-            loop(n_sub, gelu_rows)
+            loop_rows(gelu_rows)
             r.hid[...] = dot(r.dbr[blk], weight_2())
 
             def back_rows(g):
                 rows = sub_rows(g)
                 r.d_hid[blk, rows, :] = (r.hid[rows, :] * r.slope[rows, :]).astype(BF16)
 
-            loop(n_sub, back_rows)
-            part = dot_rt(r.d_hid[blk], weight_1()).astype(BF16)
-            hand_on(step, blk, part, sum_s, sum_r, dm_base)
+            loop_rows(back_rows)
+            dm_merge.put(step, blk, dot_rt(r.d_hid[blk], weight_1()).astype(BF16))
 
         loop(nc, feed)
-        for step in range(1, nc):
-            chip_send(lambda other: m_all.at[c], m_all, m_base, step).wait_send()
+        m_share.sent()
 
         def column_cuts(count):
             return [(at, min(at + 256, count)) for at in range(0, count, 256)]
@@ -985,11 +1084,11 @@
         g2_core = wires.far(r.g_2.at[:, core_o], r.g_2r, core_dev)
 
         def branch_out(i):
-            step = (i + 1) % nc
+            step = nc - 1 - i
             blk = xor_of(c, step, nc)
-            part = dot_rt(r.act[blk], weight_2()).astype(BF16)
-            hand_on(step, blk, part, br_s, br_r, br_base)
-
+            br_merge.put(step, blk, dot_rt(r.act[blk], weight_2()).astype(BF16))
+
+        dm_merge.combine()
         loop(nc, branch_out)
         g2_core.wait()
         for plane in range(nf):
@@ -997,15 +1096,12 @@
         sum_2 = Sum(lambda t: r.g_2.at[t, k], r.got_2)
         sum_2.start(0)
 
-        for step in range(1, nc):
-            chip_send(lambda other: sum_s.at[other], sum_r, dm_base, step).wait()
+        dm_merge.finish()
         da_all = r.da_all
 
         def back_norm2(g):
             rows = sub_rows(g)
-            d_m = sum_r[0, rows, :].astype(F32)
-            for other in range(1, nc):
-                d_m = d_m + sum_r[other, rows, :].astype(F32)
+            d_m = dm_merge.rows(rows)
             normal, scale = ln_parts(r.after[rows, :])
             cot_now = r.cg[c, rows, :].astype(F32)
             d_after = cot_now + ln_back(normal, scale, d_m * (1.0 + own_row(4, g)))
@@ -1016,10 +1112,10 @@
             r.sub[4, at, :] = jnp.sum(d_m * normal, axis=0, keepdims=True)
             r.sub[2, at, :] = jnp.sum(d_after * r.attn[rows, :], axis=0, keepdims=True)
 
-        loop(n_sub, back_norm2)
-        da_base = reserve(nc - 1)
-        for step in range(1, nc):
-            chip_send(lambda other: da_all.at[c], da_all, da_base, step).start()
+        loop_rows(back_norm2)
+        da_share = Share(da_all)
+        da_share.start()
+        br_merge.combine()
         sum_2.start(1)
 
         g_1 = r.w_1
@@ -1028,21 +1124,18 @@
             value = dot_lt(m_rows_all, r.d_hid[:, :, lo:hi].reshape(group, hi - lo))
             g_1[:, :, :, lo:hi] = value.astype(BF16).reshape(nc, 2, rows_d, hi - lo)
         g1_core = wires.far(g_1.at[:, core_o], r.g_1r, core_dev)
-
-        for step in range(1, nc):
-            chip_send(lambda other: br_s.at[other], br_r, br_base, step).wait()
+        da_share.relay()
+
+        br_merge.finish()
 
         def finish_out(g):
             rows = sub_rows(g)
-            branch = br_r[0, rows, :].astype(F32)
-            for other in range(1, nc):
-                branch = branch + br_r[other, rows, :].astype(F32)
-            branch = branch + bias_o
+            branch = br_merge.rows(rows) + bias_o
             out[rows, :] = (r.after[rows, :] + own_row(5, g) * branch).astype(BF16)
             cot_now = r.cg[c, rows, :].astype(F32)
             r.sub[5, pl.ds(g, 1), :] = jnp.sum(cot_now * branch, axis=0, keepdims=True)
 
-        loop(n_sub, finish_out)
+        loop_rows(finish_out)
         g1_core.wait()
         for chip in range(nc):
             g_1[chip, k] = add_low(g_1[chip, k], r.g_1r[chip])
@@ -1051,14 +1144,12 @@
         y1_far = [wires.far(g_1.at[other, k], y_1.at[c], peer) for other, peer in chip_peers]
         sum_2.start(2)
 
-        back_base = reserve(nc - 1)
+        back_merge = Merge(r.sum_s, r.sum_r, r.sum_st)
 
         def attend_back(step):
             blk = xor_of(c, step, nc)
-            when(
-                step != 0,
-                lambda: chip_send(lambda other: da_all.at[c], da_all, da_base, step).wait_recv(),
-            )
+            for at in range(1, nc):
+                when(step == at, functools.partial(da_share.arrive, at))
             d_mix = dot_rt(da_all[blk], r.w_p[...]).astype(BF16)
             q_now, k_now, v_now = r.qkv[0, blk], r.qkv[1, blk], r.qkv[2, blk]
             d_q = jnp.zeros((own, chip_w), F32)
@@ -1073,44 +1164,34 @@
                 d_q = d_q + dot(d_score, k_now * head_of[h])
                 d_k = d_k + dot_lt(d_score, q_now * head_of[h])
                 d_v = d_v + dot_lt(share.astype(BF16), d_mix_h)
-            d_q = (d_q * head_scale).astype(BF16)
-            d_k = (d_k * head_scale).astype(BF16)
-            d_v = d_v.astype(BF16)
-            r.d_qkv[0, blk] = d_q
-            r.d_qkv[1, blk] = d_k
-            r.d_qkv[2, blk] = d_v
-            part = dot_rt(d_q, weight_q(0)) + dot_rt(d_k, weight_q(1)) + dot_rt(d_v, weight_q(2))
-            hand_on(step, blk, part.astype(BF16), sum_s, sum_r, back_base)
+            all_three = jnp.concatenate([d_q * head_scale, d_k * head_scale, d_v], axis=1).astype(BF16)
+            r.d_qkv[blk] = all_three
+            back_merge.put(step, blk, dot_rt(all_three, weight_q()).astype(BF16))
 
         loop(nc, attend_back)
-        for step in range(1, nc):
-            chip_send(lambda other: da_all.at[c], da_all, da_base, step).wait_send()
+        da_share.sent()
+        back_merge.combine()
+
+        g_q, g_p = w_q, r.w_p
+        a_rows = all_rows(r.a_in)
+        for lo, hi in column_cuts(q_w):
+            value = dot_lt(a_rows, r.d_qkv[:, :, lo:hi].reshape(group, hi - lo))
+            g_q[:, :, :, lo:hi] = value.astype(BF16).reshape(nc, 2, rows_d, hi - lo)
+        q_core_back = wires.far(g_q.at[:, core_o], r.g_qr, core_dev)
+        g_p[...] = dot_lt(all_rows(r.mixed), all_rows(da_all)).astype(BF16)
+
+        def own_side(ref, side):
+            return ref.at[pl.ds(pl.multiple_of(side * rows_d, SUB), rows_d)]
+
+        p_core_back = wires.far(own_side(g_p, core_o), r.g_pr, core_dev)
+        q_core_back.wait()
+        for chip in range(nc):
+            g_q[chip, k] = add_low(g_q[chip, k], r.g_qr[chip])
+        r.y_got[c] = g_q[c, k]
+        yq_far = [wires.far(g_q.at[other, k], r.y_got.at[c], peer) for other, peer in chip_peers]
         wait_all(y1_far)
         sum_1 = Sum(lambda t: y_1.at[t], r.got_1)
         sum_1.start(0)
-
-        g_q, g_p = w_q, r.w_p
-        a_rows = all_rows(r.a_in)
-        q_core_back = []
-        for kind in range(3):
-            for lo, hi in column_cuts(chip_w):
-                value = dot_lt(a_rows, r.d_qkv[kind, :, :, lo:hi].reshape(group, hi - lo))
-                g_q[kind, :, :, :, lo:hi] = value.astype(BF16).reshape(nc, 2, rows_d, hi - lo)
-            q_core_back.append(wires.far(g_q.at[kind, :, core_o], r.g_qr.at[kind], core_dev))
-        g_p[...] = dot_lt(all_rows(r.mixed), all_rows(da_all)).astype(BF16)
-
-        def own_side(ref, side):
-            return ref.at[pl.ds(pl.multiple_of(side * rows_d, SUB), rows_d)]
-
-        p_core_back = wires.far(own_side(g_p, core_o), r.g_pr, core_dev)
-        yq_far = []
-        for kind in range(3):
-            q_core_back[kind].wait()
-            for chip in range(nc):
-                g_q[kind, chip, k] = add_low(g_q[kind, chip, k], r.g_qr[kind, chip])
-            q_rows[kind * nc + c] = g_q[kind, c, k]
-            for other, peer in chip_peers:
-                yq_far.append(wires.far(g_q.at[kind, other, k], q_rows.at[kind * nc + c], peer))
         p_core_back.wait()
         p_line.sent(p_in)
         y_p = r.p_got
@@ -1121,14 +1202,11 @@
         sum_p.start(0)
         sum_1.start(1)
 
-        for step in range(1, nc):
-            chip_send(lambda other: sum_s.at[other], sum_r, back_base, step).wait()
+        back_merge.finish()
 
         def back_norm1(g):
             rows = sub_rows(g)
-            d_a = sum_r[0, rows, :].astype(F32)
-            for other in range(1, nc):
-                d_a = d_a + sum_r[other, rows, :].astype(F32)
+            d_a = back_merge.rows(rows)
             normal, scale = ln_parts(r.xg[c, rows, :].astype(F32))
             value = r.d_after[rows, :] + ln_back(normal, scale, d_a * (1.0 + own_row(1, g)))
             x_grad[rows, :] = value.astype(BF16)
@@ -1136,24 +1214,29 @@
             r.sub[0, at, :] = jnp.sum(d_a, axis=0, keepdims=True)
             r.sub[1, at, :] = jnp.sum(d_a * normal, axis=0, keepdims=True)
 
-        loop(n_sub, back_norm1)
+        loop_rows(back_norm1)
         hot_turned = own_hot.astype(F32).T.astype(BF16)
         for kind in range(6):
-            r.m_tab[:, width * kind : width * (kind + 1)] = dot3(hot_turned, r.sub[kind])
-        for plane in range(nf):
-            r.d_cut[plane] = r.m_tab[:, ada_w * plane : ada_w * (plane + 1)]
+            value = dot3(hot_turned, r.sub[kind])
+            r.d_part[:, :, width * kind : width * (kind + 1)] = value.reshape(2, half, width)
+        d_core = wires.far(r.d_part.at[core_o], r.d_core, core_dev)
         ones_own = jnp.ones((8, own), BF16)
         ones_all = jnp.ones((8, group), BF16)
         r.d_bias[...] = jnp.zeros((8, width), F32)
         r.d_bias[0:1, :] = dot(ones_own, da_all[c])[0:1]
         r.d_bias[1:2, :] = dot(ones_own, r.dbr[c])[0:1]
-        r.d_bias[2:3, 0:chip_w] = dot(ones_all, all_rows(r.d_qkv.at[0]))[0:1]
-        r.d_bias[3:4, 0:chip_w] = dot(ones_all, all_rows(r.d_qkv.at[2]))[0:1]
+        qkv_sums = dot(ones_all, all_rows(r.d_qkv))[0:1]
+        r.d_bias[2:3, 0:chip_w] = qkv_sums[:, :chip_w]
+        r.d_bias[3:4, 0:chip_w] = qkv_sums[:, 2 * chip_w :]
 
         ones_ff = dot(ones_all, all_rows(r.d_hid))[0:1]
         r.d_bias[4:5, :] = ones_ff[:, :width]
         for part in range(1, ff_c // width):
             r.d_bias[4 + part : 5 + part, :] = ones_ff[:, part * width : (part + 1) * width]
+        d_core.wait()
+        r.d_core[...] = r.d_core[...] + r.d_part[k]
+        for plane in range(nf):
+            r.d_cut[plane] = r.d_core[:, ada_w * plane : ada_w * (plane + 1)]
         small = []
         for other, peer in plane_peers:
             small.append(wires.far(r.d_cut.at[other], r.dz.at[f], peer))
@@ -1165,7 +1248,10 @@
         q_line.sent(q_in)
         y_q = r.q_z
         for plane in range(nf):
-            row = [q_rows[3 * plane + i] for i in range(3)]
+            row = []
+            for i in range(3):
+                kind, chip = (3 * plane + i) // nc, (3 * plane + i) % nc
+                row.append(r.y_got[chip, :, chip_w * kind : chip_w * (kind + 1)])
             y_q[plane] = jnp.concatenate(row, axis=1)
         sum_q = Sum(lambda t: y_q.at[t], r.got_q)
         sum_q.start(0)
@@ -1175,20 +1261,15 @@
         for plane in range(1, nf):
             value = value + r.dz[plane]
             value_b = value_b + r.dzb[plane]
-        r.d_both[...] = value.reshape(2, half, ada_w)
+        m_chip[c] = value
         r.d_bsum[...] = value_b
-        small = [
-            wires.far(r.d_both.at[core_o], r.m_core, core_dev),
-            wires.far(r.d_bsum, r.d_coreb, core_dev),
-        ]
+        b_swap = wires.far(r.d_bsum, r.d_coreb, core_dev)
+        small = [wires.far(m_chip.at[c], m_chip.at[c], peer) for _, peer in chip_peers]
         sum_q.start(1)
         sum_p.start(2)
-        wait_all(small)
-        m_chip[c] = r.d_both[k] + r.m_core[...]
+        b_swap.wait()
         r.d_chipb[c] = r.d_bsum[...] + r.d_coreb[...]
-        small = []
         for _, peer in chip_peers:
-            small.append(wires.far(m_chip.at[c], m_chip.at[c], peer))
             small.append(wires.far(r.d_chipb.at[c], r.d_chipb.at[c], peer))
 
         sum_2.finish(r.all_2.at[k])

time: 270 us -> 252 us (0.933)
  Pallas kernels: 251 us -> 233 us
    pallas_call x1, Pallas kernels: 251 us -> 233 us  [block_kernel(): pl.pallas_call(kernel, out_shape=outs, in_specs=[ANYWHERE] * 2 + [ON_CHIP...]
where the time goes in v4:
time: 252 us
  Pallas kernels  233 us (92%)
  local copies, waits for them, and re-layouts  13.8 us (5%)
  other arithmetic  4.51 us (2%)
    pallas_call x1, Pallas kernels, block_kernel(): pl.pallas_call(kernel, out_shape=outs, in_specs=[ANYWHERE] * 2 + [ON_CHIP...  233 us
    unnamed x49, local copies, waits for them, and re-layouts  12.2 us

profile of v4, /device:TPU:0, one launch (start us, length us, event | category | flops | bytes accessed | tf_op | source)
XLA Modules:
  0.0 251.9 jit_solution(9279860945141412100)
XLA Ops:
  0.7 0.6 copy-done.16
  1.3 0.1 broadcast_add_fusion.1
  1.4 0.1 stack_reshape.6
  1.5 0.0 copy-done.17
  1.5 0.1 broadcast_add_fusion
  1.6 0.1 stack_reshape.7
  1.7 0.6 concatenate.23.ids_in
  2.3 0.1 concatenate.29
  2.5 0.6 convert_element_type.17.bias_in
  3.1 0.7 multiply_convert_fusion.silu_in
  3.8 0.7 constant_dynamic-slice_fusion.cond_in
  4.5 1.9 copy.28.f2_in
  6.4 232.8 %block.1 = (bf16[128,1152]{1,0:T(8,128)(2,1)}, bf16[128,1152]{1,0:T(8,128)(2,1)}, f32[16,288]{1,0:T(8,128)}, f32[144,1728]{1,0:T(8,128)}, f32[1,1728]{1,0:T(1,12...) custom-call(bf16[128,1152]{1,0:T(8,128)(2,1)} %bitcast.6, ...), custom_call_target="tpu_custom_call" | custom-call | tf_op jit(solution)/shard_map/block/pallas_call | solution.py:1344
  239.3 0.6 copy-done.15
  239.9 0.6 reduce.2
  240.5 0.6 reduce.4
  241.1 0.6 reduce.1
  241.7 0.6 reduce
  242.3 0.1 copy-done.9
  242.4 0.6 reduce.3
  243.0 2.4 copy.29
  245.5 0.7 copy.37
  246.2 0.4 copy-done.3
  246.5 0.7 copy.38
  247.3 0.0 copy-done.6
  247.3 0.6 copy.39
  247.9 1.0 copy.40
  248.9 0.4 copy-done.2
  249.3 0.8 copy.41
  250.0 0.3 copy-done.5
  250.4 0.7 copy.42
  251.1 0.8 copy.43
  (40 shorter events, 0.1 us)
Async XLA Ops:
  0.6 0.7 copy-start.16
  0.7 0.8 copy-start.17
  0.7 1.0 copy-start.18
  0.7 1.0 copy-start.19
  0.7 1.0 copy-start.13
  0.7 1.6 copy-start.10
  0.7 1.6 copy-start.11
  0.7 2.4 copy-start.7
  239.2 0.7 copy-start.15
  239.2 1.3 copy-start.14
  239.2 1.9 copy-start.12
  239.9 1.8 copy-start.8
  241.7 0.7 copy-start.9
  243.0 2.5 copy-start.4
  243.0 4.9 %copy-start = (f32[144,1728]{1,0:T(8,128)S(1)}, f32[144,1728]{1,0:T(8,128)}, u32[]{:S(2)}) copy-start(f32[144,1728]{1,0:T(8,128)} %get-tuple-element.68) | copy-start | bytes 2985988
  245.5 1.1 copy-start.3
  246.5 0.7 copy-start.6
  247.9 1.4 copy-start.2
  249.3 1.1 copy-start.5
  249.3 1.8 copy-start.1

commit v5 on v4

--- a/solution.py
+++ b/solution.py
@@ -427,7 +427,7 @@
     group = nc * own
     rows_d, q_w = wq.shape
     chip_w = q_w // 3
-    ff_d, cols_f = w2.shape
+    cols_f, ff_d = w2.shape
     ff_c = 2 * ff_d
     ada_w = w_ada.shape[1]
     n_bias = bias.shape[1]
@@ -443,15 +443,15 @@
         jax.ShapeDtypeStruct((own, width), BF16),
         jax.ShapeDtypeStruct((n_rows, cols_f), F32),
         jax.ShapeDtypeStruct((rows_d, ada_w), F32),
-        jax.ShapeDtypeStruct((1, ada_w), F32),
+        jax.ShapeDtypeStruct((ada_w,), F32),
         jax.ShapeDtypeStruct((rows_d, q_w), F32),
-        jax.ShapeDtypeStruct((1, 2 * chip_w), F32),
+        jax.ShapeDtypeStruct((2 * chip_w,), F32),
         jax.ShapeDtypeStruct((rows_d, cols_f), F32),
-        jax.ShapeDtypeStruct((1, cols_f), F32),
+        jax.ShapeDtypeStruct((cols_f,), F32),
         jax.ShapeDtypeStruct((rows_d, ff_c), F32),
-        jax.ShapeDtypeStruct((1, ff_c), F32),
-        jax.ShapeDtypeStruct((ff_d, cols_f), F32),
-        jax.ShapeDtypeStruct((1, cols_f), F32),
+        jax.ShapeDtypeStruct((ff_c,), F32),
+        jax.ShapeDtypeStruct((cols_f, ff_d), F32),
+        jax.ShapeDtypeStruct((cols_f,), F32),
     )
     tokens = (nc, own, width)
     n_sem = 240
@@ -468,7 +468,7 @@
         m_tab=pltpu.VMEM((n_rows, 6 * width), F32),
         tab=pltpu.VMEM((3, nc * n_sub, width), F32),
         own_tab=pltpu.VMEM((6, n_sub, width), F32),
-        q_z=pltpu.VMEM((nf, rows_d, q_w), BF16),
+        q_z=pltpu.VMEM((nf, rows_d, q_w + cols_f), BF16),
         q_rows=pltpu.VMEM((nf * 3, rows_d, chip_w), BF16),
         q_got=pltpu.VMEM((3, nc, rows_d, chip_w), BF16),
         w_q=pltpu.VMEM((nc, 2, rows_d, q_w), BF16),
@@ -477,8 +477,7 @@
         w_1=pltpu.VMEM((nc, 2, rows_d, ff_c), BF16),
         p_got=pltpu.VMEM((2, nf, rows_d, cols_f), BF16),
         w_p=pltpu.VMEM((chip_w, width), BF16),
-        f2_nat=pltpu.VMEM((ff_d, cols_f), BF16),
-        f2_half=pltpu.VMEM((2, rows_d, ff_d), BF16),
+        f2_half=pltpu.VMEM((cols_f, ff_d), BF16),
         f2_got=pltpu.VMEM((rows_d, ff_d), BF16),
         w_2=pltpu.VMEM((nf, 2, rows_d, ff_c), BF16),
         a_in=pltpu.VMEM(tokens, BF16),
@@ -497,7 +496,6 @@
         after=pltpu.VMEM((own, width), F32),
         d_after=pltpu.VMEM((own, width), F32),
         hid=pltpu.VMEM((own, ff_c), F32),
-        slope=pltpu.VMEM((own, ff_c), F32),
         act=pltpu.VMEM((nc, own, ff_c), BF16),
         d_hid=pltpu.VMEM((nc, own, ff_c), BF16),
         dbr=pltpu.VMEM(tokens, BF16),
@@ -507,12 +505,15 @@
         g_1r=pltpu.VMEM((nc, rows_d, ff_c), BF16),
         g_qr=pltpu.VMEM((nc, rows_d, q_w), BF16),
         g_pr=pltpu.VMEM((rows_d, width), BF16),
-        got_q=pltpu.VMEM((2, nf - 1, rows_d, q_w), BF16),
+        got_q=pltpu.VMEM((2, nf - 1, rows_d, q_w + cols_f), BF16),
         got_1=pltpu.VMEM((2, nf - 1, rows_d, ff_c), BF16),
-        got_p=pltpu.VMEM((2, nf - 1, rows_d, cols_f), BF16),
         got_2=pltpu.VMEM((2, nf - 1, rows_d, ff_c), BF16),
         all_2=pltpu.VMEM((2, rows_d, ff_c), F32),
         sub=pltpu.VMEM((6, n_sub, width), F32),
+        q_nat=pltpu.VMEM((rows_d, q_w), BF16),
+        p_nat=pltpu.VMEM((rows_d, cols_f), BF16),
+        all_q=pltpu.VMEM((rows_d, q_w + cols_f), F32),
+        sub_gate=pltpu.VMEM((nc * n_sub, width), F32),
         d_part=pltpu.VMEM((2, half, 6 * width), F32),
         d_core=pltpu.VMEM((half, 6 * width), F32),
         d_cut=pltpu.VMEM((nf, half, ada_w), F32),
@@ -644,6 +645,10 @@
                 when(step == 2, self.y_b.start)
                 when(step == 1, self.x_a.start)
 
+            def launch(self):
+                for item in (self.d_x, self.d_y, self.y_b, self.x_a):
+                    item.start()
+
             def combine(self):
                 self.d_y.wait()
                 ref = self.terms.at[chip_x, second_half]
@@ -687,7 +692,7 @@
                 for condition, copy in self.both(step, src):
                     when(condition, copy.start)
 
-            def arrive(self, step, then=None):
+            def arrive(self, step, then=None, wait=True):
                 for condition, got, base in (
                     (f - 1 - step >= 0, f - 1 - step, self.up),
                     (f + 1 + step <= nf - 1, f + 1 + step, self.down),
@@ -695,7 +700,8 @@
 
                     def body(got=got, base=base):
                         slot = self.slot(got)
-                        pair(slot, slot, core_dev, base + step, base + step).wait_recv()
+                        if wait:
+                            pair(slot, slot, core_dev, base + step, base + step).wait_recv()
                         if then is not None:
                             then(got)
 
@@ -752,22 +758,24 @@
                     for _, _, condition, _, copy in self.both(step):
                         when(condition, copy.wait_send)
 
+        def own_side(ref, side):
+            return ref.at[pl.ds(pl.multiple_of(side * rows_d, SUB), rows_d)]
+
         barrier = pltpu.get_barrier_semaphore()
         peers = [core_dev] + [peer for _, peer in chip_peers + plane_peers]
         for peer in peers:
             pl.semaphore_signal(barrier, inc=1, device_id=peer, device_id_type=MESH_ID)
 
         q_line = Gather(lambda g: r.q_z.at[g])
-        p_line = Gather(lambda g: r.p_got.at[k, g])
         f1_line = Gather(lambda g: r.f1_z.at[g])
         f2_line = Gather(lambda g: r.w_2.at[g, k])
         ada_near = wires.near(ada_in, r.ada)
-        q_near = wires.near(q_in, r.q_z.at[f])
-        f2_near = wires.near(f2_in, r.f2_nat)
+        q_near = wires.near(q_in, r.q_nat)
+        p_near = wires.near(p_in, r.p_nat)
+        f2_near = wires.near(f2_in, r.f2_half)
         first = []
         first.append(wires.near(x_in, r.xg.at[c]))
         first.append(wires.near(c_in, r.cg.at[c]))
-        p_near = wires.near(p_in, r.p_got.at[k, f])
         f1_near = wires.near(f1_in, r.f1_z.at[f])
         r.idsg[c] = ids_in[...]
         r.biasg[f] = bias_in[...]
@@ -775,18 +783,16 @@
         ada_bias = jnp.where(place.dp == 0, bias_in[:, n_bias - ada_w :], 0.0)
         value = dot(silu_in[...], r.ada[...]) + ada_bias
         r.m_part[...] = value.reshape(2, half, ada_w)
+        q_near.wait()
+        p_near.wait()
+        r.q_z[f] = jnp.concatenate([r.q_nat[...], r.p_nat[...]], axis=1)
         f2_near.wait()
-        turned = r.f2_nat[...].T
-        r.f2_half[...] = turned.reshape(2, rows_d, ff_d)
-        q_near.wait()
         pl.semaphore_wait(barrier, len(peers))
         m_first = wires.far(r.m_part.at[core_o], r.m_core, core_dev)
-        q_line.start(0, q_in)
+        q_line.start(0)
         for _, peer in chip_peers:
             first.append(wires.far(ids_in, r.idsg.at[c], peer))
-        f2_swap = wires.far(r.f2_half.at[core_o], r.f2_got, core_dev)
-        for _, peer in plane_peers:
-            first.append(wires.far(bias_in, r.biasg.at[f], peer))
+        f2_swap = wires.far(own_side(r.f2_half, core_o), r.f2_got, core_dev)
 
         w_q, q_rows = r.w_q, r.q_rows
         q_base = reserve(3 * nc)
@@ -801,6 +807,7 @@
             return chip, far, pltpu.make_async_copy(src, dst, r.local.at[q_local + kind])
 
         def q_forward(plane):
+            r.p_got[k, plane] = r.q_z[plane, :, q_w:]
             for i in range(3):
                 q_rows[3 * plane + i] = r.q_z[plane, :, chip_w * i : chip_w * (i + 1)]
                 chip, far, near = q_copies(plane, i)
@@ -828,28 +835,24 @@
         q_forward(f)
         x_share = Share(r.xg, x_in)
         x_share.start()
-        q_line.arrive(0, q_forward)
-        q_line.start(1)
         wait_all(m_second)
         total = m_chip[0]
         for other in range(1, nc):
             total = total + m_chip[other]
         r.m_z[f, k] = total
         m_third = [wires.far(r.m_z.at[f, k], r.m_z.at[f, k], peer) for _, peer in plane_peers]
+        for _, peer in plane_peers:
+            first.append(wires.far(bias_in, r.biasg.at[f], peer))
+        q_line.arrive(0, q_forward)
+        q_line.start(1)
         x_share.relay()
-        p_line.start(0, p_in)
-        q_line.arrive(1, q_forward)
-        q_line.start(2)
-        p_line.arrive(0)
-        p_line.start(1)
-        f1_line.start(0, f1_in)
         f2_swap.wait()
 
         def join_even():
-            r.w_2[f, k] = jnp.concatenate([r.f2_half[0], r.f2_got[...]], axis=1)
+            r.w_2[f, k] = jnp.concatenate([r.f2_half[:rows_d], r.f2_got[...]], axis=1)
 
         def join_odd():
-            r.w_2[f, k] = jnp.concatenate([r.f2_got[...], r.f2_half[1]], axis=1)
+            r.w_2[f, k] = jnp.concatenate([r.f2_got[...], r.f2_half[rows_d:]], axis=1)
 
         when(k == 0, join_even)
         when(k == 1, join_odd)
@@ -862,17 +865,11 @@
         def f2_forward(plane):
             f2_across(plane).start()
 
-        q_line.arrive(2, q_forward)
-        p_line.arrive(1)
-        p_line.start(2)
+        f2_forward(f)
         wait_all(m_third)
         m_last = wires.far(r.m_z.at[:, k], r.m_z.at[:, k], core_dev)
-        f2_line.start(0)
-        f2_forward(f)
 
         wait_all(first)
-        for step in range(1, nc):
-            x_share.arrive(step)
         m_last.wait()
         m_rows = [r.m_z[plane].reshape(n_rows, ada_w) for plane in range(nf)]
         r.m_tab[...] = jnp.concatenate(m_rows, axis=1)
@@ -908,7 +905,16 @@
 
             loop_rows(body)
 
-        loop(nc, make_a)
+        make_a(c)
+        for step in (1, 2):
+            x_share.arrive(step)
+            make_a(xor_of(c, step, nc))
+        q_line.arrive(1, q_forward)
+        q_line.start(2)
+        f1_line.start(0, f1_in)
+        x_share.arrive(3)
+        make_a(chip_d)
+        q_line.arrive(2, q_forward)
 
         for kind in range(3):
             for other, _ in chip_peers:
@@ -922,15 +928,11 @@
             row = [r.q_got[kind, chip] for kind in range(3)]
             w_q[chip, k] = jnp.concatenate(row, axis=1)
             q_core.append(wires.far(w_q.at[chip, k], w_q.at[chip, k], core_dev))
-        p_line.arrive(2)
-        p_near.wait()
         p_core = wires.far(r.p_got.at[k], r.p_got.at[k], core_dev)
         f1_near.wait()
         f1_forward(f)
         f1_line.arrive(0, f1_forward)
         f1_line.start(1)
-        c_share = Share(r.cg, c_in)
-        c_share.start()
         x_share.sent()
         p_core.wait()
         for side in range(2):
@@ -983,13 +985,17 @@
             r.mixed[blk] = mixed
             attn_merge.put(step, blk, dot(mixed, r.w_p[...]).astype(BF16))
 
+            def next_lines():
+                f1_line.arrive(1)
+                f1_line.start(2)
+                f2_line.start(0)
+
+            when(i == 0, next_lines)
+
         loop(nc, attend)
         attn_merge.combine()
-        c_share.relay()
-        f1_line.arrive(1, f1_forward)
-        f1_line.start(2)
-        f2_line.arrive(0, f2_forward)
-        f2_line.start(1)
+        f1_line.arrive(1, f1_forward, False)
+        f1_line.arrive(2, f1_forward)
 
         attn_merge.finish()
 
@@ -1006,21 +1012,10 @@
         m_all = r.m_all
         m_share = Share(m_all)
         m_share.start()
-        f1_line.arrive(2, f1_forward)
-        f2_line.arrive(1, f2_forward)
-        f2_line.start(2)
-        for step in range(1, nc):
-            c_share.arrive(step)
-
-        def make_dbr(blk):
-            def body(g):
-                rows = sub_rows(g)
-                value = r.cg[blk, rows, :].astype(F32) * tab_row(5, blk, g)
-                r.dbr[blk, rows, :] = value.astype(BF16)
-
-            loop_rows(body)
-
-        loop(nc, make_dbr)
+        c_share = Share(r.cg, c_in)
+        c_share.start()
+        f2_line.arrive(0, f2_forward)
+        f2_line.start(1)
         m_share.relay()
         f1_core = []
         ref = r.w_1.at[c, k]
@@ -1031,11 +1026,9 @@
             pair(ref, ref, core_dev, f1_base + other, f1_base + other).wait()
             f1_core.append(wires.far(ref, ref, core_dev))
         f1_line.sent(f1_in)
-        c_share.sent()
-        f2_line.arrive(2, f2_forward)
+        f2_line.arrive(1, f2_forward)
+        f2_line.start(2)
         wait_all(f1_core)
-        for plane in range(nf):
-            f2_across(plane).wait()
 
         def weight_1():
             return r.w_1[...].reshape(width, ff_c)
@@ -1045,6 +1038,9 @@
 
         dm_merge = Merge(r.sum_s, r.sum_r, r.sum_st)
         br_merge = Merge(r.br_s, r.br_r, r.br_st)
+
+        def mixed_order(i):
+            return (1 + 2 * i) * (1 - i // 2) + (6 - 2 * i) * (i // 2)
 
         def feed(step):
             blk = xor_of(c, step, nc)
@@ -1056,20 +1052,40 @@
                 rows = sub_rows(g)
                 value, slope = gelu_both(r.hid[rows, :])
                 r.act[blk, rows, :] = value.astype(BF16)
-                r.slope[rows, :] = slope
+                r.d_hid[blk, rows, :] = slope.astype(BF16)
 
             loop_rows(gelu_rows)
+            when(step == 1, c_share.relay)
+
+        def feed_back(i):
+            step = mixed_order(i)
+            blk = xor_of(c, step, nc)
+            for at in range(1, nc):
+                when(step == at, functools.partial(c_share.arrive, at))
+
+            def dbr_rows(g):
+                rows = sub_rows(g)
+                value = r.cg[blk, rows, :].astype(F32) * tab_row(5, blk, g)
+                r.dbr[blk, rows, :] = value.astype(BF16)
+
+            loop_rows(dbr_rows)
             r.hid[...] = dot(r.dbr[blk], weight_2())
 
             def back_rows(g):
                 rows = sub_rows(g)
-                r.d_hid[blk, rows, :] = (r.hid[rows, :] * r.slope[rows, :]).astype(BF16)
+                value = r.hid[rows, :] * r.d_hid[blk, rows, :].astype(F32)
+                r.d_hid[blk, rows, :] = value.astype(BF16)
 
             loop_rows(back_rows)
             dm_merge.put(step, blk, dot_rt(r.d_hid[blk], weight_1()).astype(BF16))
 
         loop(nc, feed)
-        m_share.sent()
+        f2_line.arrive(2, f2_forward)
+        for plane in range(nf):
+            f2_across(plane).wait()
+        loop(nc, feed_back)
+        dm_merge.combine()
+        c_share.sent()
 
         def column_cuts(count):
             return [(at, min(at + 256, count)) for at in range(0, count, 256)]
@@ -1082,19 +1098,6 @@
             value = dot_lt(dbr_all, r.act[:, :, lo:hi].reshape(group, hi - lo))
             r.g_2[:, :, :, lo:hi] = value.astype(BF16).reshape(nf, 2, rows_d, hi - lo)
         g2_core = wires.far(r.g_2.at[:, core_o], r.g_2r, core_dev)
-
-        def branch_out(i):
-            step = nc - 1 - i
-            blk = xor_of(c, step, nc)
-            br_merge.put(step, blk, dot_rt(r.act[blk], weight_2()).astype(BF16))
-
-        dm_merge.combine()
-        loop(nc, branch_out)
-        g2_core.wait()
-        for plane in range(nf):
-            r.g_2[plane, k] = add_low(r.g_2[plane, k], r.g_2r[plane])
-        sum_2 = Sum(lambda t: r.g_2.at[t, k], r.got_2)
-        sum_2.start(0)
 
         dm_merge.finish()
         da_all = r.da_all
@@ -1115,8 +1118,12 @@
         loop_rows(back_norm2)
         da_share = Share(da_all)
         da_share.start()
-        br_merge.combine()
-        sum_2.start(1)
+        m_share.sent()
+        g2_core.wait()
+        for plane in range(nf):
+            r.g_2[plane, k] = add_low(r.g_2[plane, k], r.g_2r[plane])
+        sum_2 = Sum(lambda t: r.g_2.at[t, k], r.got_2)
+        sum_2.start(0)
 
         g_1 = r.w_1
         m_rows_all = all_rows(m_all)
@@ -1126,27 +1133,20 @@
         g1_core = wires.far(g_1.at[:, core_o], r.g_1r, core_dev)
         da_share.relay()
 
-        br_merge.finish()
-
-        def finish_out(g):
-            rows = sub_rows(g)
-            branch = br_merge.rows(rows) + bias_o
-            out[rows, :] = (r.after[rows, :] + own_row(5, g) * branch).astype(BF16)
-            cot_now = r.cg[c, rows, :].astype(F32)
-            r.sub[5, pl.ds(g, 1), :] = jnp.sum(cot_now * branch, axis=0, keepdims=True)
-
-        loop_rows(finish_out)
         g1_core.wait()
         for chip in range(nc):
             g_1[chip, k] = add_low(g_1[chip, k], r.g_1r[chip])
         y_1 = r.f1_z
         y_1[c] = g_1[c, k]
         y1_far = [wires.far(g_1.at[other, k], y_1.at[c], peer) for other, peer in chip_peers]
-        sum_2.start(2)
+
+        def gray_order(i):
+            return i + i // 2 - 2 * (i // 3)
 
         back_merge = Merge(r.sum_s, r.sum_r, r.sum_st)
 
-        def attend_back(step):
+        def attend_back(i):
+            step = gray_order(i)
             blk = xor_of(c, step, nc)
             for at in range(1, nc):
                 when(step == at, functools.partial(da_share.arrive, at))
@@ -1167,10 +1167,11 @@
             all_three = jnp.concatenate([d_q * head_scale, d_k * head_scale, d_v], axis=1).astype(BF16)
             r.d_qkv[blk] = all_three
             back_merge.put(step, blk, dot_rt(all_three, weight_q()).astype(BF16))
+            when(i == 1, lambda: sum_2.start(1))
+            when(i == 3, lambda: sum_2.start(2))
 
         loop(nc, attend_back)
         da_share.sent()
-        back_merge.combine()
 
         g_q, g_p = w_q, r.w_p
         a_rows = all_rows(r.a_in)
@@ -1178,10 +1179,8 @@
             value = dot_lt(a_rows, r.d_qkv[:, :, lo:hi].reshape(group, hi - lo))
             g_q[:, :, :, lo:hi] = value.astype(BF16).reshape(nc, 2, rows_d, hi - lo)
         q_core_back = wires.far(g_q.at[:, core_o], r.g_qr, core_dev)
+        back_merge.combine()
         g_p[...] = dot_lt(all_rows(r.mixed), all_rows(da_all)).astype(BF16)
-
-        def own_side(ref, side):
-            return ref.at[pl.ds(pl.multiple_of(side * rows_d, SUB), rows_d)]
 
         p_core_back = wires.far(own_side(g_p, core_o), r.g_pr, core_dev)
         q_core_back.wait()
@@ -1193,13 +1192,39 @@
         sum_1 = Sum(lambda t: y_1.at[t], r.got_1)
         sum_1.start(0)
         p_core_back.wait()
-        p_line.sent(p_in)
-        y_p = r.p_got
-        total = add_low(own_side(g_p, k)[...], r.g_pr[...])
-        for plane in range(nf):
-            y_p[k, plane] = total[:, plane * cols_f : (plane + 1) * cols_f]
-        sum_p = Sum(lambda t: y_p.at[k, t], r.got_p)
-        sum_p.start(0)
+        y_p = add_low(own_side(g_p, k)[...], r.g_pr[...])
+        own_side(g_p, k)[...] = y_p
+
+        ones_own = jnp.ones((8, own), BF16)
+        ones_all = jnp.ones((8, group), BF16)
+        r.d_bias[...] = jnp.zeros((8, width), F32)
+        r.d_bias[0:1, :] = dot(ones_own, da_all[c])[0:1]
+        r.d_bias[1:2, :] = dot(ones_own, r.dbr[c])[0:1]
+        qkv_sums = dot(ones_all, all_rows(r.d_qkv))[0:1]
+        r.d_bias[2:3, 0:chip_w] = qkv_sums[:, :chip_w]
+        r.d_bias[3:4, 0:chip_w] = qkv_sums[:, 2 * chip_w :]
+        ones_ff = dot(ones_all, all_rows(r.d_hid))[0:1]
+        r.d_bias[4:5, :] = ones_ff[:, :width]
+        for part in range(1, ff_c // width):
+            r.d_bias[4 + part : 5 + part, :] = ones_ff[:, part * width : (part + 1) * width]
+        bias_far = [wires.far(r.d_bias, r.dzb.at[f], peer) for _, peer in plane_peers]
+        r.dzb[f] = r.d_bias[...]
+
+        def branch_out(i):
+            step = nc - 1 - i
+            blk = xor_of(c, step, nc)
+            r.hid[...] = dot_rt(r.act[blk], weight_2())
+            r.br_s[blk] = r.hid[...].astype(BF16)
+            bias_once = bias_o * jnp.where(step == 0, 1.0, 0.0)
+
+            def gate_rows(g):
+                rows = sub_rows(g)
+                value = (r.hid[rows, :] + bias_once) * r.cg[blk, rows, :].astype(F32)
+                r.sub_gate[pl.ds(blk * n_sub + g, 1), :] = jnp.sum(value, axis=0, keepdims=True)
+
+            loop_rows(gate_rows)
+
+        loop(nc, branch_out)
         sum_1.start(1)
 
         back_merge.finish()
@@ -1217,22 +1242,12 @@
         loop_rows(back_norm1)
         hot_turned = own_hot.astype(F32).T.astype(BF16)
         for kind in range(6):
-            value = dot3(hot_turned, r.sub[kind])
+            if kind == 5:
+                value = dot3(hot_all.astype(F32).T.astype(BF16), r.sub_gate[...])
+            else:
+                value = dot3(hot_turned, r.sub[kind])
             r.d_part[:, :, width * kind : width * (kind + 1)] = value.reshape(2, half, width)
         d_core = wires.far(r.d_part.at[core_o], r.d_core, core_dev)
-        ones_own = jnp.ones((8, own), BF16)
-        ones_all = jnp.ones((8, group), BF16)
-        r.d_bias[...] = jnp.zeros((8, width), F32)
-        r.d_bias[0:1, :] = dot(ones_own, da_all[c])[0:1]
-        r.d_bias[1:2, :] = dot(ones_own, r.dbr[c])[0:1]
-        qkv_sums = dot(ones_all, all_rows(r.d_qkv))[0:1]
-        r.d_bias[2:3, 0:chip_w] = qkv_sums[:, :chip_w]
-        r.d_bias[3:4, 0:chip_w] = qkv_sums[:, 2 * chip_w :]
-
-        ones_ff = dot(ones_all, all_rows(r.d_hid))[0:1]
-        r.d_bias[4:5, :] = ones_ff[:, :width]
-        for part in range(1, ff_c // width):
-            r.d_bias[4 + part : 5 + part, :] = ones_ff[:, part * width : (part + 1) * width]
         d_core.wait()
         r.d_core[...] = r.d_core[...] + r.d_part[k]
         for plane in range(nf):
@@ -1240,22 +1255,20 @@
         small = []
         for other, peer in plane_peers:
             small.append(wires.far(r.d_cut.at[other], r.dz.at[f], peer))
-            small.append(wires.far(r.d_bias, r.dzb.at[f], peer))
         r.dz[f] = r.d_cut[f]
-        r.dzb[f] = r.d_bias[...]
-        sum_1.start(2)
         wait_all(yq_far)
-        q_line.sent(q_in)
+        q_line.sent()
         y_q = r.q_z
         for plane in range(nf):
             row = []
             for i in range(3):
                 kind, chip = (3 * plane + i) // nc, (3 * plane + i) % nc
                 row.append(r.y_got[chip, :, chip_w * kind : chip_w * (kind + 1)])
+            row.append(own_side(g_p, k)[:, plane * cols_f : (plane + 1) * cols_f])
             y_q[plane] = jnp.concatenate(row, axis=1)
         sum_q = Sum(lambda t: y_q.at[t], r.got_q)
         sum_q.start(0)
-        sum_p.start(1)
+        wait_all(bias_far)
         wait_all(small)
         value, value_b = r.dz[0], r.dzb[0]
         for plane in range(1, nf):
@@ -1266,25 +1279,23 @@
         b_swap = wires.far(r.d_bsum, r.d_coreb, core_dev)
         small = [wires.far(m_chip.at[c], m_chip.at[c], peer) for _, peer in chip_peers]
         sum_q.start(1)
-        sum_p.start(2)
         b_swap.wait()
         r.d_chipb[c] = r.d_bsum[...] + r.d_coreb[...]
         for _, peer in chip_peers:
             small.append(wires.far(r.d_chipb.at[c], r.d_chipb.at[c], peer))
-
-        sum_2.finish(r.all_2.at[k])
-        o2_swap = wires.far(r.all_2.at[k], r.all_2.at[k], core_dev)
+        br_merge.launch()
+        sum_1.start(2)
+
         wait_all(small)
         value = m_chip[0]
         for chip in range(1, nc):
             value = value + m_chip[chip]
         r.d_tot[k] = value
         d_swap = wires.far(r.d_tot.at[k], r.d_tot.at[k], core_dev)
-        sum_q.start(2)
         d_swap.wait()
         d_cols = r.d_tot[...].reshape(n_rows, ada_w)
         silu_turned = silu_in[...].astype(F32).T.astype(BF16)
-        o_bada[...] = jnp.sum(d_cols, axis=0, keepdims=True)
+        o_bada[...] = jnp.sum(d_cols, axis=0)
         value, total = d_cols, None
         for _ in range(3):
             term = value.astype(BF16)
@@ -1293,28 +1304,40 @@
             total = part if total is None else total + part
         r.c_part[f] = total
         c_far = [wires.far(r.c_part.at[f], r.c_part.at[f], peer) for _, peer in plane_peers]
+        sum_q.start(2)
         for lo, hi in column_cuts(ada_w):
             o_ada[:, lo:hi] = dot3(silu_turned, d_cols[:, lo:hi])
-        sum_1.finish(o_1)
-        o2_swap.wait()
-
-        def own_columns(lo):
-            def body():
-                both = r.all_2[:, :, lo : lo + ff_d].reshape(cols_f, ff_d)
-                o_2[...] = both.T
-
-            return body
-
-        when(k == 0, own_columns(0))
-        when(k == 1, own_columns(ff_d))
+        sum_2.finish(r.all_2.at[k])
+        o2_swap = wires.far(r.all_2.at[k], r.all_2.at[k], core_dev)
+        br_merge.combine()
         wait_all(c_far)
         value = r.c_part[0]
         for plane in range(1, nf):
             value = value + r.c_part[plane]
         r.c_all[c, k] = value
-        wait_all([wires.far(r.c_all.at[c, k], r.c_all.at[c, k], peer) for _, peer in chip_peers])
+        c_chip = [wires.far(r.c_all.at[c, k], r.c_all.at[c, k], peer) for _, peer in chip_peers]
+
+
+        br_merge.finish()
+
+        def finish_out(g):
+            rows = sub_rows(g)
+            branch = br_merge.rows(rows) + bias_o
+            out[rows, :] = (r.after[rows, :] + own_row(5, g) * branch).astype(BF16)
+
+        loop_rows(finish_out)
+        wait_all(c_chip)
         c_swap = wires.far(r.c_all.at[:, k], r.c_all.at[:, k], core_dev)
-        sum_p.finish(o_p)
+        o2_swap.wait()
+
+        def own_columns(lo):
+            def body():
+                o_2[...] = r.all_2[:, :, lo : lo + ff_d].reshape(cols_f, ff_d)
+
+            return body
+
+        when(k == 0, own_columns(0))
+        when(k == 1, own_columns(ff_d))
         own_sums = r.d_chipb[0]
         for chip in range(1, nc):
             own_sums = own_sums + r.d_chipb[chip]
@@ -1322,14 +1345,12 @@
 
             def bias_columns(plane=plane):
                 at = plane * cols_f
-                o_bp[...] = own_sums[0:1, at : at + cols_f]
-                o_b2[...] = own_sums[1:2, at : at + cols_f]
+                o_bp[...] = own_sums[0, at : at + cols_f]
+                o_b2[...] = own_sums[1, at : at + cols_f]
                 kind, chip = 2 * plane // nc, 2 * plane % nc
-                o_bqv[...] = jnp.concatenate(
-                    [r.d_chipb[chip + i, 2 + kind : 3 + kind, 0:chip_w] for i in range(2)], axis=1
-                )
-                parts = [r.d_chipb[plane, 4 + i : 5 + i, :] for i in range(ff_c // width)]
-                o_b1[...] = parts[0] if len(parts) == 1 else jnp.concatenate(parts, axis=1)
+                pieces = [r.d_chipb[chip + i, 2 + kind : 3 + kind, 0:chip_w] for i in range(2)]
+                o_bqv[...] = jnp.concatenate(pieces, axis=1)[0]
+                o_b1[...] = r.d_chipb[plane, 4, :]
 
             when(f == plane, bias_columns)
         c_swap.wait()
@@ -1337,8 +1358,11 @@
         cond_now = cond_in[...]
         gate = 1.0 / (1.0 + jnp.exp(-cond_now))
         o_cond[...] = d_silu * (gate * (1.0 + cond_now * (1.0 - gate)))
-        sum_q.finish(o_q)
         f2_line.sent()
+        sum_1.finish(o_1)
+        sum_q.finish(r.all_q)
+        o_q[...] = r.all_q[:, :q_w]
+        o_p[...] = r.all_q[:, q_w:]
         assert wires.remote_count <= n_sem and wires.local_count <= 32
 
     return pl.pallas_call(
@@ -1429,22 +1453,22 @@
             grad_proj, grad_b_proj, grad_fc1, grad_b_fc1, grad_fc2, grad_b_fc2,
         ) = block_kernel(
             dims, patches.reshape(own, width), cotangent.reshape(own, width), id_rows, bias_send,
-            silu_part, cond_own, w_ada, w_qkv, w_proj, w_fc1, w_fc2,
+            silu_part, cond_own, w_ada, w_qkv, w_proj, w_fc1, w_fc2.T,
         )
         return (
             output.reshape(patches.shape),
             input_grad.reshape(patches.shape),
             cond_grad.reshape(micro, clips, cols_f),
             grad_ada,
-            grad_b_ada[0],
+            grad_b_ada,
             grad_qkv,
-            grad_b_qv[0],
+            grad_b_qv,
             grad_proj,
-            grad_b_proj[0],
+            grad_b_proj,
             grad_fc1,
-            grad_b_fc1[0],
-            grad_fc2,
-            grad_b_fc2[0],
+            grad_b_fc1,
+            grad_fc2.T,
+            grad_b_fc2,
         )
 
     ids = jnp.stack([frame_of_slot.reshape(own), clip_of_slot.reshape(own)])

time: 252 us -> 224 us (0.89)
  Pallas kernels: 233 us -> 208 us
  other arithmetic: 4.51 us -> 1.47 us
    pallas_call x1, Pallas kernels: 233 us -> 208 us  [block_kernel(): pl.pallas_call(kernel, out_shape=outs, in_specs=[ANYWHERE] * 2 + [ON_CHIP...]
    pallas_call x5 -> x0, other arithmetic: 3.03 us -> none  [block_kernel(): pl.pallas_call(kernel, out_shape=outs, in_specs=[ANYWHERE] * 2 + [ON_CHIP...]
    unnamed x49 -> x51, local copies, waits for them, and re-layouts: 12.2 us -> 11.8 us
where the time goes in v5:
time: 224 us; the launch traced here: 223 us
  Pallas kernels  208 us (93%)
  local copies, waits for them, and re-layouts  13.4 us (6%)
    pallas_call x1, Pallas kernels, block_kernel(): pl.pallas_call(kernel, out_shape=outs, in_specs=[ANYWHERE] * 2 + [ON_CHIP...  208 us
    unnamed x51, local copies, waits for them, and re-layouts  11.8 us

profile of v5, /device:TPU:0, one launch (start us, length us, event | category | flops | bytes accessed | tf_op | source)
XLA Modules:
  0.0 223.2 jit_solution(13610247427188020428)
XLA Ops:
  0.7 0.0 copy-start.6
  0.7 0.6 copy-done.15
  1.3 0.1 broadcast_add_fusion.1
  1.4 0.1 stack_reshape.6
  1.5 0.1 broadcast_add_fusion
  1.6 0.1 stack_reshape.7
  1.7 0.0 copy-done.18
  1.7 0.0 copy-done.12
  1.7 0.6 concatenate.23.ids_in
  2.3 0.1 concatenate.29
  2.5 0.6 convert_element_type.17.bias_in
  3.1 0.7 multiply_convert_fusion.silu_in
  3.8 0.7 constant_dynamic-slice_fusion.cond_in
  4.5 207.5 %block.1 = (bf16[128,1152]{1,0:T(8,128)(2,1)}, bf16[128,1152]{1,0:T(8,128)(2,1)}, f32[16,288]{1,0:T(8,128)}, f32[144,1728]{1,0:T(8,128)}, f32[1728]{0:T(1024)}, ...) custom-call(bf16[128,1152]{1,0:T(8,128)(2,1)} %bitcast.10, ...), custom_call_target="tpu_custom_call" | custom-call | tf_op jit(solution)/shard_map/block/pallas_call | solution.py:1368
  212.0 1.8 copy.41
  213.8 1.7 copy.42
  215.5 0.6 copy.43
  216.1 0.0 copy-done
  216.1 1.0 copy.44
  217.1 0.6 copy.45
  217.7 0.8 copy.46
  218.5 0.0 copy-done.10
  218.5 0.6 copy.47
  219.1 0.0 copy-done.4
  219.1 0.7 copy.48
  219.8 0.6 copy.49
  220.3 0.0 copy-done.2
  220.3 0.8 copy.50
  221.2 0.6 copy.51
  221.8 0.0 copy-done.1
  221.8 0.9 copy.52
  222.7 0.6 copy.53
  (37 shorter events, 0.1 us)
Async XLA Ops:
  0.6 0.7 copy-start.15
  0.7 0.8 copy-start.16
  0.7 1.0 copy-start.17
  0.7 1.0 copy-start.18
  0.7 1.0 copy-start.12
  0.7 1.6 copy-start.9
  0.7 1.6 copy-start.11
  0.7 2.4 %copy-start.6 = (f32[2,8,1152]{2,1,0:T(8,128)S(1)}, f32[2,8,1152]{2,1,0:T(8,128)}, u32[]{:S(2)}) copy-start(f32[2,8,1152]{2,1,0:T(8,128)} %param.17) | copy-start | bytes 221188
  212.0 4.1 %copy-start = (f32[144,1728]{1,0:T(8,128)S(1)}, f32[144,1728]{1,0:T(8,128)}, u32[]{:S(2)}) copy-start(f32[144,1728]{1,0:T(8,128)} %get-tuple-element.55) | copy-start | bytes 2985988
  213.8 1.7 copy-start.5
  216.1 1.0 copy-start.8
  216.1 1.6 copy-start.3
  217.7 0.8 copy-start.10
  217.7 1.4 copy-start.4
  217.7 2.7 %copy-start.2 = (f32[144,1152]{1,0:T(8,128)S(1)}, f32[144,1152]{1,0:T(8,128)}, u32[]{:S(2)}) copy-start(f32[144,1152]{1,0:T(8,128)} %get-tuple-element.61) | copy-start | bytes 1990660
  219.1 0.7 copy-start.14
  219.8 2.0 copy-start.1
  220.3 0.8 copy-start.7
  221.8 0.9 copy-start.13

commit v6 on v5

--- a/solution.py
+++ b/solution.py
@@ -421,7 +421,7 @@
     return (left.astype(F32) + right.astype(F32)).astype(BF16)
 
 
-def block_kernel(dims, x, cot, ids, bias, silu_part, cond_own, w_ada, wq, wp, w1, w2):
+def block_kernel(dims, x, cot, frames, clips, biases, cond, w_ada, wq, wp, w1, w2):
     nc, nf = dims.nc, dims.nf
     own, width = x.shape
     group = nc * own
@@ -430,13 +430,15 @@
     cols_f, ff_d = w2.shape
     ff_c = 2 * ff_d
     ada_w = w_ada.shape[1]
-    n_bias = bias.shape[1]
+    n_bias = sum(item.shape[0] for item in biases)
     heads = chip_w // HEAD_DIM
-    n_rows = silu_part.shape[0]
+    micro, n_clips, _ = cond.shape
+    n_rows = micro * n_clips
     half = n_rows // 2
     n_sub = own // SUB
     head_scale = HEAD_DIM ** (-0.5)
     last = nf - 2
+    third = rows_d // 3
 
     outs = (
         jax.ShapeDtypeStruct((own, width), BF16),
@@ -458,9 +460,11 @@
     scratch = dict(
         xg=pltpu.VMEM(tokens, BF16),
         cg=pltpu.VMEM(tokens, BF16),
-        idsg=pltpu.VMEM((nc, 8, own), F32),
+        idsg=pltpu.VMEM((nc, 2, own), F32),
         biasg=pltpu.VMEM((nf, 1, n_bias), F32),
         ada=pltpu.VMEM(w_ada.shape, BF16),
+        silu=pltpu.VMEM((n_rows, rows_d), BF16),
+        cond_own=pltpu.VMEM((n_rows, cols_f), F32),
         m_part=pltpu.VMEM((2, half, ada_w), F32),
         m_core=pltpu.VMEM((half, ada_w), F32),
         m_chip=pltpu.VMEM((nc, half, ada_w), F32),
@@ -469,8 +473,8 @@
         tab=pltpu.VMEM((3, nc * n_sub, width), F32),
         own_tab=pltpu.VMEM((6, n_sub, width), F32),
         q_z=pltpu.VMEM((nf, rows_d, q_w + cols_f), BF16),
-        q_rows=pltpu.VMEM((nf * 3, rows_d, chip_w), BF16),
-        q_got=pltpu.VMEM((3, nc, rows_d, chip_w), BF16),
+        q_rows=pltpu.VMEM((nf * 3, third, q_w), BF16),
+        q_got=pltpu.VMEM((3, nc, third, q_w), BF16),
         w_q=pltpu.VMEM((nc, 2, rows_d, q_w), BF16),
         y_got=pltpu.VMEM((nc, rows_d, q_w), BF16),
         f1_z=pltpu.VMEM((nf, rows_d, ff_c), BF16),
@@ -513,6 +517,7 @@
         q_nat=pltpu.VMEM((rows_d, q_w), BF16),
         p_nat=pltpu.VMEM((rows_d, cols_f), BF16),
         all_q=pltpu.VMEM((rows_d, q_w + cols_f), F32),
+        sub_lin=pltpu.VMEM((2, nc * n_sub, width), F32),
         sub_gate=pltpu.VMEM((nc * n_sub, width), F32),
         d_part=pltpu.VMEM((2, half, 6 * width), F32),
         d_core=pltpu.VMEM((half, 6 * width), F32),
@@ -533,7 +538,8 @@
     names = list(scratch)
 
     def kernel(
-        x_in, c_in, ids_in, bias_in, silu_in, cond_in, ada_in, q_in, p_in, f1_in, f2_in,
+        x_in, c_in, frames_in, clips_in, bq_in, bp_in, b1_in, b2_in, ba_in, cond_in, ada_in,
+        q_in, p_in, f1_in, f2_in,
         out, x_grad, o_cond, o_ada, o_bada, o_q, o_bqv, o_p, o_bp, o_1, o_b1, o_2, o_b2, *rest,
     ):
         r = types.SimpleNamespace(**dict(zip(names, rest)))
@@ -777,11 +783,28 @@
         first.append(wires.near(x_in, r.xg.at[c]))
         first.append(wires.near(c_in, r.cg.at[c]))
         f1_near = wires.near(f1_in, r.f1_z.at[f])
-        r.idsg[c] = ids_in[...]
-        r.biasg[f] = bias_in[...]
+        order = lax.broadcasted_iota(jnp.int32, frames_in.shape, 0)
+        for at, value in ((0, frames_in[...] + 65536 * order), (1, clips_in[...] + n_clips * order)):
+            row = [value[i : i + 1].astype(F32) for i in range(micro)]
+            r.idsg[c, at : at + 1, :] = jnp.concatenate(row, axis=1)
+        row = [ref[...].astype(F32).reshape(1, ref.shape[0]) for ref in (bq_in, bp_in, b1_in, b2_in, ba_in)]
+        r.biasg[f] = jnp.concatenate(row, axis=1)
+        cond_rows = cond_in[...].reshape(n_rows, width)
+
+        def own_silu(at):
+            part = cond_rows[:, rows_d * at : rows_d * (at + 1)]
+            r.silu[...] = (part / (1.0 + jnp.exp(-part))).astype(BF16)
+
+        def own_cond(at):
+            r.cond_own[...] = cond_rows[:, cols_f * at : cols_f * (at + 1)]
+
+        for at in range(2 * nc):
+            when(place.dp == at, functools.partial(own_silu, at))
+        for at in range(nf):
+            when(f == at, functools.partial(own_cond, at))
         ada_near.wait()
-        ada_bias = jnp.where(place.dp == 0, bias_in[:, n_bias - ada_w :], 0.0)
-        value = dot(silu_in[...], r.ada[...]) + ada_bias
+        ada_bias = jnp.where(place.dp == 0, row[4], 0.0)
+        value = dot(r.silu[...], r.ada[...]) + ada_bias
         r.m_part[...] = value.reshape(2, half, ada_w)
         q_near.wait()
         p_near.wait()
@@ -791,7 +814,7 @@
         m_first = wires.far(r.m_part.at[core_o], r.m_core, core_dev)
         q_line.start(0)
         for _, peer in chip_peers:
-            first.append(wires.far(ids_in, r.idsg.at[c], peer))
+            first.append(wires.far(r.idsg.at[c], r.idsg.at[c], peer))
         f2_swap = wires.far(own_side(r.f2_half, core_o), r.f2_got, core_dev)
 
         w_q, q_rows = r.w_q, r.q_rows
@@ -809,7 +832,9 @@
         def q_forward(plane):
             r.p_got[k, plane] = r.q_z[plane, :, q_w:]
             for i in range(3):
-                q_rows[3 * plane + i] = r.q_z[plane, :, chip_w * i : chip_w * (i + 1)]
+                piece = r.q_z[plane, :, chip_w * i : chip_w * (i + 1)]
+                parts = [piece[third * j : third * (j + 1)] for j in range(3)]
+                q_rows[3 * plane + i] = jnp.concatenate(parts, axis=1)
                 chip, far, near = q_copies(plane, i)
                 when(chip != c, far.start)
                 when(chip == c, near.start)
@@ -842,7 +867,7 @@
         r.m_z[f, k] = total
         m_third = [wires.far(r.m_z.at[f, k], r.m_z.at[f, k], peer) for _, peer in plane_peers]
         for _, peer in plane_peers:
-            first.append(wires.far(bias_in, r.biasg.at[f], peer))
+            first.append(wires.far(r.biasg.at[f], r.biasg.at[f], peer))
         q_line.arrive(0, q_forward)
         q_line.start(1)
         x_share.relay()
@@ -925,8 +950,10 @@
             pltpu.make_async_copy(ref, ref, r.local.at[q_local + kind]).wait()
         q_core = []
         for chip in range(nc):
-            row = [r.q_got[kind, chip] for kind in range(3)]
-            w_q[chip, k] = jnp.concatenate(row, axis=1)
+            for j in range(3):
+                at = chip_w * j
+                row = [r.q_got[kind, chip, :, at : at + chip_w] for kind in range(3)]
+                w_q[chip, k, third * j : third * (j + 1), :] = jnp.concatenate(row, axis=1)
             q_core.append(wires.far(w_q.at[chip, k], w_q.at[chip, k], core_dev))
         p_core = wires.far(r.p_got.at[k], r.p_got.at[k], core_dev)
         f1_near.wait()
@@ -990,7 +1017,7 @@
                 f1_line.start(2)
                 f2_line.start(0)
 
-            when(i == 0, next_lines)
+            when(i == 1, next_lines)
 
         loop(nc, attend)
         attn_merge.combine()
@@ -1016,7 +1043,6 @@
         c_share.start()
         f2_line.arrive(0, f2_forward)
         f2_line.start(1)
-        m_share.relay()
         f1_core = []
         ref = r.w_1.at[c, k]
         pltpu.make_async_copy(ref, ref, r.local.at[f1_local]).wait()
@@ -1025,6 +1051,7 @@
             ref = r.w_1.at[other, k]
             pair(ref, ref, core_dev, f1_base + other, f1_base + other).wait()
             f1_core.append(wires.far(ref, ref, core_dev))
+        m_share.relay()
         f1_line.sent(f1_in)
         f2_line.arrive(1, f2_forward)
         f2_line.start(2)
@@ -1139,6 +1166,23 @@
         y_1 = r.f1_z
         y_1[c] = g_1[c, k]
         y1_far = [wires.far(g_1.at[other, k], y_1.at[c], peer) for other, peer in chip_peers]
+
+        def branch_out(i):
+            step = nc - 1 - i
+            blk = xor_of(c, step, nc)
+            r.hid[...] = dot_rt(r.act[blk], weight_2())
+            r.br_s[blk] = r.hid[...].astype(BF16)
+            bias_once = bias_o * jnp.where(step == 0, 1.0, 0.0)
+
+            def gate_rows(g):
+                rows = sub_rows(g)
+                value = (r.hid[rows, :] + bias_once) * r.cg[blk, rows, :].astype(F32)
+                r.sub_gate[pl.ds(blk * n_sub + g, 1), :] = jnp.sum(value, axis=0, keepdims=True)
+
+            loop_rows(gate_rows)
+
+        loop(nc, branch_out)
+        sum_2.start(1)
 
         def gray_order(i):
             return i + i // 2 - 2 * (i // 3)
@@ -1167,7 +1211,6 @@
             all_three = jnp.concatenate([d_q * head_scale, d_k * head_scale, d_v], axis=1).astype(BF16)
             r.d_qkv[blk] = all_three
             back_merge.put(step, blk, dot_rt(all_three, weight_q()).astype(BF16))
-            when(i == 1, lambda: sum_2.start(1))
             when(i == 3, lambda: sum_2.start(2))
 
         loop(nc, attend_back)
@@ -1179,22 +1222,54 @@
             value = dot_lt(a_rows, r.d_qkv[:, :, lo:hi].reshape(group, hi - lo))
             g_q[:, :, :, lo:hi] = value.astype(BF16).reshape(nc, 2, rows_d, hi - lo)
         q_core_back = wires.far(g_q.at[:, core_o], r.g_qr, core_dev)
-        back_merge.combine()
+        wait_all(y1_far)
+        sum_1 = Sum(lambda t: y_1.at[t], r.got_1)
+        sum_1.start(0)
         g_p[...] = dot_lt(all_rows(r.mixed), all_rows(da_all)).astype(BF16)
-
         p_core_back = wires.far(own_side(g_p, core_o), r.g_pr, core_dev)
         q_core_back.wait()
         for chip in range(nc):
             g_q[chip, k] = add_low(g_q[chip, k], r.g_qr[chip])
         r.y_got[c] = g_q[c, k]
         yq_far = [wires.far(g_q.at[other, k], r.y_got.at[c], peer) for other, peer in chip_peers]
-        wait_all(y1_far)
-        sum_1 = Sum(lambda t: y_1.at[t], r.got_1)
-        sum_1.start(0)
+
+        def own_terms(step):
+            blk = xor_of(c, step, nc)
+
+            def body(g):
+                rows = sub_rows(g)
+                part = r.sum_s[blk, rows, :].astype(F32)
+                normal, _ = ln_parts(r.xg[blk, rows, :].astype(F32))
+                at = pl.ds(blk * n_sub + g, 1)
+                r.sub_lin[0, at, :] = jnp.sum(part, axis=0, keepdims=True)
+                r.sub_lin[1, at, :] = jnp.sum(part * normal, axis=0, keepdims=True)
+
+            loop_rows(body)
+
+        loop(nc, own_terms)
+        back_merge.combine()
+        all_turned = hot_all.astype(F32).T.astype(BF16)
+        hot_turned = own_hot.astype(F32).T.astype(BF16)
+        for kind in range(6):
+            if kind < 2:
+                value = dot3(all_turned, r.sub_lin[kind])
+            elif kind < 5:
+                value = dot3(hot_turned, r.sub[kind])
+            else:
+                value = dot3(all_turned, r.sub_gate[...])
+            r.d_part[:, :, width * kind : width * (kind + 1)] = value.reshape(2, half, width)
+        d_core = wires.far(r.d_part.at[core_o], r.d_core, core_dev)
+        d_core.wait()
+        r.d_core[...] = r.d_core[...] + r.d_part[k]
+        for plane in range(nf):
+            r.d_cut[plane] = r.d_core[:, ada_w * plane : ada_w * (plane + 1)]
+        small = []
+        for other, peer in plane_peers:
+            small.append(wires.far(r.d_cut.at[other], r.dz.at[f], peer))
+        r.dz[f] = r.d_cut[f]
+        sum_1.start(1)
         p_core_back.wait()
-        y_p = add_low(own_side(g_p, k)[...], r.g_pr[...])
-        own_side(g_p, k)[...] = y_p
-
+        own_side(g_p, k)[...] = add_low(own_side(g_p, k)[...], r.g_pr[...])
         ones_own = jnp.ones((8, own), BF16)
         ones_all = jnp.ones((8, group), BF16)
         r.d_bias[...] = jnp.zeros((8, width), F32)
@@ -1209,53 +1284,12 @@
             r.d_bias[4 + part : 5 + part, :] = ones_ff[:, part * width : (part + 1) * width]
         bias_far = [wires.far(r.d_bias, r.dzb.at[f], peer) for _, peer in plane_peers]
         r.dzb[f] = r.d_bias[...]
-
-        def branch_out(i):
-            step = nc - 1 - i
-            blk = xor_of(c, step, nc)
-            r.hid[...] = dot_rt(r.act[blk], weight_2())
-            r.br_s[blk] = r.hid[...].astype(BF16)
-            bias_once = bias_o * jnp.where(step == 0, 1.0, 0.0)
-
-            def gate_rows(g):
-                rows = sub_rows(g)
-                value = (r.hid[rows, :] + bias_once) * r.cg[blk, rows, :].astype(F32)
-                r.sub_gate[pl.ds(blk * n_sub + g, 1), :] = jnp.sum(value, axis=0, keepdims=True)
-
-            loop_rows(gate_rows)
-
-        loop(nc, branch_out)
-        sum_1.start(1)
-
-        back_merge.finish()
-
-        def back_norm1(g):
-            rows = sub_rows(g)
-            d_a = back_merge.rows(rows)
-            normal, scale = ln_parts(r.xg[c, rows, :].astype(F32))
-            value = r.d_after[rows, :] + ln_back(normal, scale, d_a * (1.0 + own_row(1, g)))
-            x_grad[rows, :] = value.astype(BF16)
-            at = pl.ds(g, 1)
-            r.sub[0, at, :] = jnp.sum(d_a, axis=0, keepdims=True)
-            r.sub[1, at, :] = jnp.sum(d_a * normal, axis=0, keepdims=True)
-
-        loop_rows(back_norm1)
-        hot_turned = own_hot.astype(F32).T.astype(BF16)
-        for kind in range(6):
-            if kind == 5:
-                value = dot3(hot_all.astype(F32).T.astype(BF16), r.sub_gate[...])
-            else:
-                value = dot3(hot_turned, r.sub[kind])
-            r.d_part[:, :, width * kind : width * (kind + 1)] = value.reshape(2, half, width)
-        d_core = wires.far(r.d_part.at[core_o], r.d_core, core_dev)
-        d_core.wait()
-        r.d_core[...] = r.d_core[...] + r.d_part[k]
-        for plane in range(nf):
-            r.d_cut[plane] = r.d_core[:, ada_w * plane : ada_w * (plane + 1)]
-        small = []
-        for other, peer in plane_peers:
-            small.append(wires.far(r.d_cut.at[other], r.dz.at[f], peer))
-        r.dz[f] = r.d_cut[f]
+        wait_all(small)
+        value = r.dz[0]
+        for plane in range(1, nf):
+            value = value + r.dz[plane]
+        m_chip[c] = value
+        small = [wires.far(m_chip.at[c], m_chip.at[c], peer) for _, peer in chip_peers]
         wait_all(yq_far)
         q_line.sent()
         y_q = r.q_z
@@ -1268,33 +1302,38 @@
             y_q[plane] = jnp.concatenate(row, axis=1)
         sum_q = Sum(lambda t: y_q.at[t], r.got_q)
         sum_q.start(0)
+        sum_1.start(2)
         wait_all(bias_far)
-        wait_all(small)
-        value, value_b = r.dz[0], r.dzb[0]
+        value = r.dzb[0]
         for plane in range(1, nf):
-            value = value + r.dz[plane]
-            value_b = value_b + r.dzb[plane]
-        m_chip[c] = value
-        r.d_bsum[...] = value_b
+            value = value + r.dzb[plane]
+        r.d_bsum[...] = value
         b_swap = wires.far(r.d_bsum, r.d_coreb, core_dev)
-        small = [wires.far(m_chip.at[c], m_chip.at[c], peer) for _, peer in chip_peers]
-        sum_q.start(1)
-        b_swap.wait()
-        r.d_chipb[c] = r.d_bsum[...] + r.d_coreb[...]
-        for _, peer in chip_peers:
-            small.append(wires.far(r.d_chipb.at[c], r.d_chipb.at[c], peer))
-        br_merge.launch()
-        sum_1.start(2)
-
+
+        back_merge.finish()
+
+        def back_norm1(g):
+            rows = sub_rows(g)
+            d_a = back_merge.rows(rows)
+            normal, scale = ln_parts(r.xg[c, rows, :].astype(F32))
+            value = r.d_after[rows, :] + ln_back(normal, scale, d_a * (1.0 + own_row(1, g)))
+            x_grad[rows, :] = value.astype(BF16)
+
+        loop_rows(back_norm1)
         wait_all(small)
         value = m_chip[0]
         for chip in range(1, nc):
             value = value + m_chip[chip]
         r.d_tot[k] = value
         d_swap = wires.far(r.d_tot.at[k], r.d_tot.at[k], core_dev)
+        b_swap.wait()
+        r.d_chipb[c] = r.d_bsum[...] + r.d_coreb[...]
+        bias_far = [wires.far(r.d_chipb.at[c], r.d_chipb.at[c], peer) for _, peer in chip_peers]
+        br_merge.launch()
+        sum_q.start(1)
         d_swap.wait()
         d_cols = r.d_tot[...].reshape(n_rows, ada_w)
-        silu_turned = silu_in[...].astype(F32).T.astype(BF16)
+        silu_turned = r.silu[...].astype(F32).T.astype(BF16)
         o_bada[...] = jnp.sum(d_cols, axis=0)
         value, total = d_cols, None
         for _ in range(3):
@@ -1338,6 +1377,7 @@
 
         when(k == 0, own_columns(0))
         when(k == 1, own_columns(ff_d))
+        wait_all(bias_far)
         own_sums = r.d_chipb[0]
         for chip in range(1, nc):
             own_sums = own_sums + r.d_chipb[chip]
@@ -1355,7 +1395,7 @@
             when(f == plane, bias_columns)
         c_swap.wait()
         d_silu = jnp.concatenate([r.c_all[f, 0], r.c_all[f, 1]], axis=1)
-        cond_now = cond_in[...]
+        cond_now = r.cond_own[...]
         gate = 1.0 / (1.0 + jnp.exp(-cond_now))
         o_cond[...] = d_silu * (gate * (1.0 + cond_now * (1.0 - gate)))
         f2_line.sent()
@@ -1368,14 +1408,34 @@
     return pl.pallas_call(
         kernel,
         out_shape=outs,
-        in_specs=[ANYWHERE] * 2 + [ON_CHIP] * 4 + [ANYWHERE] * 5,
+        in_specs=[ANYWHERE] * 2 + [ON_CHIP] * 8 + [ANYWHERE] * 5,
         out_specs=tuple([ON_CHIP] * len(outs)),
         scratch_shapes=list(scratch.values()),
         compiler_params=pltpu.CompilerParams(
             collective_id=0, has_side_effects=True, vmem_limit_bytes=63 * 2**20
         ),
         name="block",
-    )(x, cot, ids, bias, silu_part, cond_own, w_ada, wq, wp, w1, w2)
+    )(x, cot, frames, clips, *biases, cond, w_ada, wq, wp, w1, w2)
+
+
+def land_kernel(arrays):
+    count = len(arrays)
+
+    def kernel(*refs):
+        ins, results, sems = refs[:count], refs[count : 2 * count], refs[-1]
+        copies = [pltpu.make_async_copy(a, b, sems.at[i]) for i, (a, b) in enumerate(zip(ins, results))]
+        for copy in copies:
+            copy.start()
+        wait_all(copies)
+
+    return pl.pallas_call(
+        kernel,
+        out_shape=tuple(jax.ShapeDtypeStruct(a.shape, a.dtype) for a in arrays),
+        in_specs=[ON_CHIP] * count,
+        out_specs=tuple([ANYWHERE] * count),
+        scratch_shapes=[pltpu.SemaphoreType.DMA((count,))],
+        name="land",
+    )(*arrays)
 
 
 def fits_block(n_dp, nf, width, ff, own, micro):
@@ -1442,19 +1502,15 @@
         return cond_grad, grad_w_ada, jnp.sum(d_cols, axis=0)
 
     if fits_block(n_dp, nf, width, ff, own, micro):
-        bias_send = jnp.concatenate([b_qv, b_proj, b_fc1, b_fc2, b_ada]).astype(F32)[None]
-        order = jnp.arange(micro, dtype=jnp.int32)[:, None]
-        pair_rows = jnp.stack(
-            [(frame_of_slot + order * 65536).reshape(own), (clip_of_slot + order * clips).reshape(own)]
+        results = block_kernel(
+            dims, patches.reshape(own, width), cotangent.reshape(own, width), frame_of_slot,
+            clip_of_slot, (b_qv, b_proj, b_fc1, b_fc2, b_ada), conditioning, w_ada, w_qkv, w_proj,
+            w_fc1, w_fc2.T,
         )
-        id_rows = jnp.concatenate([pair_rows.astype(F32), jnp.zeros((6, own), F32)])
         (
             output, input_grad, cond_grad, grad_ada, grad_b_ada, grad_qkv, grad_b_qv,
             grad_proj, grad_b_proj, grad_fc1, grad_b_fc1, grad_fc2, grad_b_fc2,
-        ) = block_kernel(
-            dims, patches.reshape(own, width), cotangent.reshape(own, width), id_rows, bias_send,
-            silu_part, cond_own, w_ada, w_qkv, w_proj, w_fc1, w_fc2.T,
-        )
+        ) = land_kernel(results)
         return (
             output.reshape(patches.shape),
             input_grad.reshape(patches.shape),

time: 224 us -> 208 us (0.929)
  local copies, waits for them, and re-layouts: 13.4 us -> 0 us
    unnamed x51 -> x0, local copies, waits for them, and re-layouts: 11.8 us -> none
    pallas_call x1, Pallas kernels: 208 us -> 203 us  [block_kernel(): pl.pallas_call(kernel, out_shape=outs, in_specs=[ANYWHERE] * 2 + [ON_CHIP...]
    pallas_call x0 -> x1, Pallas kernels: none -> 4.03 us  [land_kernel(): pl.pallas_call(kernel, out_shape=tuple((jax.ShapeDtypeStruct(a.shape, a.d...]
where the time goes in v6:
time: 208 us; the launch traced here: 207 us
  Pallas kernels  207 us (100%)
    pallas_call x1, Pallas kernels, block_kernel(): pl.pallas_call(kernel, out_shape=outs, in_specs=[ANYWHERE] * 2 + [ON_CHIP...  203 us

profile of v6, /device:TPU:0, one launch (start us, length us, event | category | flops | bytes accessed | tf_op | source)
XLA Modules:
  0.0 207.4 jit_solution(2487207390225893620)
XLA Ops:
  0.7 202.5 %block.1 = (bf16[128,1152]{1,0:T(8,128)(2,1)}, bf16[128,1152]{1,0:T(8,128)(2,1)}, f32[16,288]{1,0:T(8,128)}, f32[144,1728]{1,0:T(8,128)}, f32[1728]{0:T(1024)}, ...) custom-call(bf16[128,1152]{1,0:T(8,128)(2,1)} %bitcast.8, ...), custom_call_target="tpu_custom_call" | custom-call | tf_op jit(solution)/shard_map/block/pallas_call | solution.py:1408
  203.2 4.0 %land.1 = (bf16[128,1152]{1,0:T(8,128)(2,1)}, bf16[128,1152]{1,0:T(8,128)(2,1)}, f32[16,288]{1,0:T(8,128)}, f32[144,1728]{1,0:T(8,128)}, f32[1728]{0:T(1024)}, /...) custom-call(bf16[128,1152]{1,0:T(8,128)(2,1)} %get-tuple-element.39., ...), custom_call_target="tpu_custom_call" | custom-call | tf_op jit(solution)/shard_map/land/pallas_call | solution.py:1431

commit v7 on v6

--- a/solution.py
+++ b/solution.py
@@ -521,11 +521,12 @@
         sub_gate=pltpu.VMEM((nc * n_sub, width), F32),
         d_part=pltpu.VMEM((2, half, 6 * width), F32),
         d_core=pltpu.VMEM((half, 6 * width), F32),
-        d_cut=pltpu.VMEM((nf, half, ada_w), F32),
+        d_cut=pltpu.VMEM((nf, half, ada_w), BF16),
         d_bias=pltpu.VMEM((8, width), F32),
-        dz=pltpu.VMEM((nf, half, ada_w), F32),
-        dzb=pltpu.VMEM((nf, 8, width), F32),
+        dz=pltpu.VMEM((nf, half, ada_w), BF16),
+        dzb=pltpu.VMEM((nf, 8, width), BF16),
         d_tot=pltpu.VMEM((2, half, ada_w), F32),
+        d_low=pltpu.VMEM((8, width), BF16),
         d_bsum=pltpu.VMEM((8, width), F32),
         d_coreb=pltpu.VMEM((8, width), F32),
         d_chipb=pltpu.VMEM((nc, 8, width), F32),
@@ -533,15 +534,20 @@
         c_all=pltpu.VMEM((nc, 2, n_rows, rows_d), F32),
         send=pltpu.SemaphoreType.DMA((n_sem,)),
         recv=pltpu.SemaphoreType.DMA((n_sem,)),
-        local=pltpu.SemaphoreType.DMA((32,)),
+        local=pltpu.SemaphoreType.DMA((40,)),
     )
     names = list(scratch)
 
     def kernel(
         x_in, c_in, frames_in, clips_in, bq_in, bp_in, b1_in, b2_in, ba_in, cond_in, ada_in,
         q_in, p_in, f1_in, f2_in,
-        out, x_grad, o_cond, o_ada, o_bada, o_q, o_bqv, o_p, o_bp, o_1, o_b1, o_2, o_b2, *rest,
+        *rest,
     ):
+        homes, rest = rest[: len(outs)], rest[len(outs) :]
+        held, rest = rest[: len(outs)], rest[len(outs) :]
+        (out, x_grad, o_cond, o_ada, o_bada, o_q, o_bqv, o_p, o_bp, o_1, o_b1, o_2, o_b2) = held
+        home_of = {id(ref): home for ref, home in zip(held, homes)}
+        landed = []
         r = types.SimpleNamespace(**dict(zip(names, rest)))
         place = Place(nc, nf)
         wires = Wires(r.send, r.recv, r.local)
@@ -672,6 +678,10 @@
             def rows(self, at):
                 value = self.terms[c, at, :].astype(F32) + self.got[0, at, :].astype(F32)
                 return value + self.got[1, at, :].astype(F32)
+
+        def land(*refs):
+            for ref in refs:
+                landed.append(wires.near(ref, home_of[id(ref)]))
 
         up, down = (place.dp, f + 1), (place.dp, f - 1)
 
@@ -1111,8 +1121,6 @@
         for plane in range(nf):
             f2_across(plane).wait()
         loop(nc, feed_back)
-        dm_merge.combine()
-        c_share.sent()
 
         def column_cuts(count):
             return [(at, min(at + 256, count)) for at in range(0, count, 256)]
@@ -1125,6 +1133,21 @@
             value = dot_lt(dbr_all, r.act[:, :, lo:hi].reshape(group, hi - lo))
             r.g_2[:, :, :, lo:hi] = value.astype(BF16).reshape(nf, 2, rows_d, hi - lo)
         g2_core = wires.far(r.g_2.at[:, core_o], r.g_2r, core_dev)
+
+        dm_merge.combine()
+        g_1 = r.w_1
+        m_rows_all = all_rows(m_all)
+        for lo, hi in column_cuts(ff_c):
+            value = dot_lt(m_rows_all, r.d_hid[:, :, lo:hi].reshape(group, hi - lo))
+            g_1[:, :, :, lo:hi] = value.astype(BF16).reshape(nc, 2, rows_d, hi - lo)
+        g1_core = wires.far(g_1.at[:, core_o], r.g_1r, core_dev)
+        c_share.sent()
+        g2_core.wait()
+        for plane in range(nf):
+            r.g_2[plane, k] = add_low(r.g_2[plane, k], r.g_2r[plane])
+        sum_2 = Sum(lambda t: r.g_2.at[t, k], r.got_2)
+        sum_2.start(0)
+
 
         dm_merge.finish()
         da_all = r.da_all
@@ -1146,18 +1169,6 @@
         da_share = Share(da_all)
         da_share.start()
         m_share.sent()
-        g2_core.wait()
-        for plane in range(nf):
-            r.g_2[plane, k] = add_low(r.g_2[plane, k], r.g_2r[plane])
-        sum_2 = Sum(lambda t: r.g_2.at[t, k], r.got_2)
-        sum_2.start(0)
-
-        g_1 = r.w_1
-        m_rows_all = all_rows(m_all)
-        for lo, hi in column_cuts(ff_c):
-            value = dot_lt(m_rows_all, r.d_hid[:, :, lo:hi].reshape(group, hi - lo))
-            g_1[:, :, :, lo:hi] = value.astype(BF16).reshape(nc, 2, rows_d, hi - lo)
-        g1_core = wires.far(g_1.at[:, core_o], r.g_1r, core_dev)
         da_share.relay()
 
         g1_core.wait()
@@ -1262,7 +1273,7 @@
         d_core.wait()
         r.d_core[...] = r.d_core[...] + r.d_part[k]
         for plane in range(nf):
-            r.d_cut[plane] = r.d_core[:, ada_w * plane : ada_w * (plane + 1)]
+            r.d_cut[plane] = r.d_core[:, ada_w * plane : ada_w * (plane + 1)].astype(BF16)
         small = []
         for other, peer in plane_peers:
             small.append(wires.far(r.d_cut.at[other], r.dz.at[f], peer))
@@ -1282,12 +1293,13 @@
         r.d_bias[4:5, :] = ones_ff[:, :width]
         for part in range(1, ff_c // width):
             r.d_bias[4 + part : 5 + part, :] = ones_ff[:, part * width : (part + 1) * width]
-        bias_far = [wires.far(r.d_bias, r.dzb.at[f], peer) for _, peer in plane_peers]
-        r.dzb[f] = r.d_bias[...]
+        r.d_low[...] = r.d_bias[...].astype(BF16)
+        bias_far = [wires.far(r.d_low, r.dzb.at[f], peer) for _, peer in plane_peers]
+        r.dzb[f] = r.d_low[...]
         wait_all(small)
-        value = r.dz[0]
+        value = r.dz[0].astype(F32)
         for plane in range(1, nf):
-            value = value + r.dz[plane]
+            value = value + r.dz[plane].astype(F32)
         m_chip[c] = value
         small = [wires.far(m_chip.at[c], m_chip.at[c], peer) for _, peer in chip_peers]
         wait_all(yq_far)
@@ -1304,9 +1316,9 @@
         sum_q.start(0)
         sum_1.start(2)
         wait_all(bias_far)
-        value = r.dzb[0]
+        value = r.dzb[0].astype(F32)
         for plane in range(1, nf):
-            value = value + r.dzb[plane]
+            value = value + r.dzb[plane].astype(F32)
         r.d_bsum[...] = value
         b_swap = wires.far(r.d_bsum, r.d_coreb, core_dev)
 
@@ -1320,6 +1332,7 @@
             x_grad[rows, :] = value.astype(BF16)
 
         loop_rows(back_norm1)
+        land(x_grad)
         wait_all(small)
         value = m_chip[0]
         for chip in range(1, nc):
@@ -1346,6 +1359,7 @@
         sum_q.start(2)
         for lo, hi in column_cuts(ada_w):
             o_ada[:, lo:hi] = dot3(silu_turned, d_cols[:, lo:hi])
+        land(o_ada, o_bada)
         sum_2.finish(r.all_2.at[k])
         o2_swap = wires.far(r.all_2.at[k], r.all_2.at[k], core_dev)
         br_merge.combine()
@@ -1365,6 +1379,7 @@
             out[rows, :] = (r.after[rows, :] + own_row(5, g) * branch).astype(BF16)
 
         loop_rows(finish_out)
+        land(out)
         wait_all(c_chip)
         c_swap = wires.far(r.c_all.at[:, k], r.c_all.at[:, k], core_dev)
         o2_swap.wait()
@@ -1377,6 +1392,7 @@
 
         when(k == 0, own_columns(0))
         when(k == 1, own_columns(ff_d))
+        land(o_2)
         wait_all(bias_far)
         own_sums = r.d_chipb[0]
         for chip in range(1, nc):
@@ -1393,24 +1409,29 @@
                 o_b1[...] = r.d_chipb[plane, 4, :]
 
             when(f == plane, bias_columns)
+        land(o_bqv, o_bp, o_b1, o_b2)
         c_swap.wait()
         d_silu = jnp.concatenate([r.c_all[f, 0], r.c_all[f, 1]], axis=1)
         cond_now = r.cond_own[...]
         gate = 1.0 / (1.0 + jnp.exp(-cond_now))
         o_cond[...] = d_silu * (gate * (1.0 + cond_now * (1.0 - gate)))
+        land(o_cond)
         f2_line.sent()
         sum_1.finish(o_1)
+        land(o_1)
         sum_q.finish(r.all_q)
         o_q[...] = r.all_q[:, :q_w]
         o_p[...] = r.all_q[:, q_w:]
-        assert wires.remote_count <= n_sem and wires.local_count <= 32
+        land(o_q, o_p)
+        wait_all(landed)
+        assert wires.remote_count <= n_sem and wires.local_count <= 40
 
     return pl.pallas_call(
         kernel,
         out_shape=outs,
         in_specs=[ANYWHERE] * 2 + [ON_CHIP] * 8 + [ANYWHERE] * 5,
-        out_specs=tuple([ON_CHIP] * len(outs)),
-        scratch_shapes=list(scratch.values()),
+        out_specs=tuple([ANYWHERE] * len(outs)),
+        scratch_shapes=[pltpu.VMEM(item.shape, item.dtype) for item in outs] + list(scratch.values()),
         compiler_params=pltpu.CompilerParams(
             collective_id=0, has_side_effects=True, vmem_limit_bytes=63 * 2**20
         ),
@@ -1422,18 +1443,24 @@
     count = len(arrays)
 
     def kernel(*refs):
-        ins, results, sems = refs[:count], refs[count : 2 * count], refs[-1]
-        copies = [pltpu.make_async_copy(a, b, sems.at[i]) for i, (a, b) in enumerate(zip(ins, results))]
-        for copy in copies:
+        ins, results, held = refs[:count], refs[count : 2 * count], refs[2 * count : 3 * count]
+        arrive, leave = refs[3 * count :]
+        steps = [pltpu.make_async_copy(a, b, arrive.at[i]) for i, (a, b) in enumerate(zip(ins, held))]
+        copies = [pltpu.make_async_copy(a, b, leave.at[i]) for i, (a, b) in enumerate(zip(held, results))]
+        for step in steps:
+            step.start()
+        for step, copy in zip(steps, copies):
+            step.wait()
             copy.start()
         wait_all(copies)
 
     return pl.pallas_call(
         kernel,
         out_shape=tuple(jax.ShapeDtypeStruct(a.shape, a.dtype) for a in arrays),
-        in_specs=[ON_CHIP] * count,
+        in_specs=[ANYWHERE] * count,
         out_specs=tuple([ANYWHERE] * count),
-        scratch_shapes=[pltpu.SemaphoreType.DMA((count,))],
+        scratch_shapes=[pltpu.VMEM(a.shape, a.dtype) for a in arrays]
+        + [pltpu.SemaphoreType.DMA((count,))] * 2,
         name="land",
     )(*arrays)
 

time: 208 us -> 203 us (0.976)
  Pallas kernels: 207 us -> 202 us
    pallas_call x1, Pallas kernels: 203 us -> 198 us  [block_kernel(): pl.pallas_call(kernel, out_shape=outs, in_specs=[ANYWHERE] * 2 + [ON_CHIP...]
where the time goes in v7:
time: 203 us; the launch traced here: 202 us
  Pallas kernels  202 us (100%)
    pallas_call x1, Pallas kernels, block_kernel(): pl.pallas_call(kernel, out_shape=outs, in_specs=[ANYWHERE] * 2 + [ON_CHIP...  198 us

profile of v7, /device:TPU:0, one launch (start us, length us, event | category | flops | bytes accessed | tf_op | source)
XLA Modules:
  0.0 202.5 jit_solution(18156726015064456292)
XLA Ops:
  0.7 198.2 %block.1 = (bf16[128,1152]{1,0:T(8,128)(2,1)}, bf16[128,1152]{1,0:T(8,128)(2,1)}, f32[16,288]{1,0:T(8,128)}, f32[144,1728]{1,0:T(8,128)}, f32[1728]{0:T(1024)}, ...) custom-call(bf16[128,1152]{1,0:T(8,128)(2,1)} %bitcast.8, ...), custom_call_target="tpu_custom_call" | custom-call | tf_op jit(solution)/shard_map/block/pallas_call | solution.py:1429
  198.9 3.4 %land.1 = (bf16[128,1152]{1,0:T(8,128)(2,1)}, bf16[128,1152]{1,0:T(8,128)(2,1)}, f32[16,288]{1,0:T(8,128)}, f32[144,1728]{1,0:T(8,128)}, f32[1728]{0:T(1024)}, /...) custom-call(bf16[128,1152]{1,0:T(8,128)(2,1)} %get-tuple-element.39., ...), custom_call_target="tpu_custom_call" | custom-call | tf_op jit(solution)/shard_map/land/pallas_call | solution.py:1457

commit v8 on v7

--- a/solution.py
+++ b/solution.py
@@ -468,7 +468,7 @@
         m_part=pltpu.VMEM((2, half, ada_w), F32),
         m_core=pltpu.VMEM((half, ada_w), F32),
         m_chip=pltpu.VMEM((nc, half, ada_w), F32),
-        m_z=pltpu.VMEM((nf, 2, half, ada_w), F32),
+        m_z=pltpu.VMEM((nf, 2, half, ada_w), BF16),
         m_tab=pltpu.VMEM((n_rows, 6 * width), F32),
         tab=pltpu.VMEM((3, nc * n_sub, width), F32),
         own_tab=pltpu.VMEM((6, n_sub, width), F32),
@@ -874,7 +874,7 @@
         total = m_chip[0]
         for other in range(1, nc):
             total = total + m_chip[other]
-        r.m_z[f, k] = total
+        r.m_z[f, k] = total.astype(BF16)
         m_third = [wires.far(r.m_z.at[f, k], r.m_z.at[f, k], peer) for _, peer in plane_peers]
         for _, peer in plane_peers:
             first.append(wires.far(r.biasg.at[f], r.biasg.at[f], peer))
@@ -906,7 +906,7 @@
 
         wait_all(first)
         m_last.wait()
-        m_rows = [r.m_z[plane].reshape(n_rows, ada_w) for plane in range(nf)]
+        m_rows = [r.m_z[plane].astype(F32).reshape(n_rows, ada_w) for plane in range(nf)]
         r.m_tab[...] = jnp.concatenate(m_rows, axis=1)
         lead = lax.broadcasted_iota(jnp.int32, (n_sub, own), 1)
         lead = lead == SUB * lax.broadcasted_iota(jnp.int32, (n_sub, own), 0)

time: 203 us -> 200 us (0.985)
  Pallas kernels: 202 us -> 199 us
    pallas_call x1, Pallas kernels: 198 us -> 195 us  [block_kernel(): pl.pallas_call(kernel, out_shape=outs, in_specs=[ANYWHERE] * 2 + [ON_CHIP...]
where the time goes in v8:
time: 200 us
  Pallas kernels  199 us (100%)
    pallas_call x1, Pallas kernels, block_kernel(): pl.pallas_call(kernel, out_shape=outs, in_specs=[ANYWHERE] * 2 + [ON_CHIP...  195 us

profile of v8, /device:TPU:0, one launch (start us, length us, event | category | flops | bytes accessed | tf_op | source)
XLA Modules:
  0.0 199.5 jit_solution(9459156713231664876)
XLA Ops:
  0.7 195.3 %block.1 = (bf16[128,1152]{1,0:T(8,128)(2,1)}, bf16[128,1152]{1,0:T(8,128)(2,1)}, f32[16,288]{1,0:T(8,128)}, f32[144,1728]{1,0:T(8,128)}, f32[1728]{0:T(1024)}, ...) custom-call(bf16[128,1152]{1,0:T(8,128)(2,1)} %bitcast.8, ...), custom_call_target="tpu_custom_call" | custom-call | tf_op jit(solution)/shard_map/block/pallas_call | solution.py:1429
  195.9 3.4 %land.1 = (bf16[128,1152]{1,0:T(8,128)(2,1)}, bf16[128,1152]{1,0:T(8,128)(2,1)}, f32[16,288]{1,0:T(8,128)}, f32[144,1728]{1,0:T(8,128)}, f32[1728]{0:T(1024)}, /...) custom-call(bf16[128,1152]{1,0:T(8,128)(2,1)} %get-tuple-element.39., ...), custom_call_target="tpu_custom_call" | custom-call | tf_op jit(solution)/shard_map/land/pallas_call | solution.py:1457

commit v9 on v8

--- a/solution.py
+++ b/solution.py
@@ -876,8 +876,6 @@
             total = total + m_chip[other]
         r.m_z[f, k] = total.astype(BF16)
         m_third = [wires.far(r.m_z.at[f, k], r.m_z.at[f, k], peer) for _, peer in plane_peers]
-        for _, peer in plane_peers:
-            first.append(wires.far(r.biasg.at[f], r.biasg.at[f], peer))
         q_line.arrive(0, q_forward)
         q_line.start(1)
         x_share.relay()
@@ -946,6 +944,7 @@
             make_a(xor_of(c, step, nc))
         q_line.arrive(1, q_forward)
         q_line.start(2)
+        bias_got = [wires.far(r.biasg.at[f], r.biasg.at[f], peer) for _, peer in plane_peers]
         f1_line.start(0, f1_in)
         x_share.arrive(3)
         make_a(chip_d)
@@ -985,6 +984,8 @@
 
         def weight_q():
             return w_q[...].reshape(width, q_w)
+
+        wait_all(bias_got)
 
         def qv_bias(plane):
             row = r.biasg[plane]

time: 200 us -> 199 us (level)
  no operation moved by 1% of the time
where the time goes in v9:
time: 199 us
  Pallas kernels  198 us (99%)
    pallas_call x1, Pallas kernels, block_kernel(): pl.pallas_call(kernel, out_shape=outs, in_specs=[ANYWHERE] * 2 + [ON_CHIP...  195 us

profile of v9, /device:TPU:0, one launch (start us, length us, event | category | flops | bytes accessed | tf_op | source)
XLA Modules:
  0.0 199.1 jit_solution(9961885538138251602)
XLA Ops:
  0.7 194.8 %block.1 = (bf16[128,1152]{1,0:T(8,128)(2,1)}, bf16[128,1152]{1,0:T(8,128)(2,1)}, f32[16,288]{1,0:T(8,128)}, f32[144,1728]{1,0:T(8,128)}, f32[1728]{0:T(1024)}, ...) custom-call(bf16[128,1152]{1,0:T(8,128)(2,1)} %bitcast.8, ...), custom_call_target="tpu_custom_call" | custom-call | tf_op jit(solution)/shard_map/block/pallas_call | solution.py:1430
  195.5 3.4 %land.1 = (bf16[128,1152]{1,0:T(8,128)(2,1)}, bf16[128,1152]{1,0:T(8,128)(2,1)}, f32[16,288]{1,0:T(8,128)}, f32[144,1728]{1,0:T(8,128)}, f32[1728]{0:T(1024)}, /...) custom-call(bf16[128,1152]{1,0:T(8,128)(2,1)} %get-tuple-element.39., ...), custom_call_target="tpu_custom_call" | custom-call | tf_op jit(solution)/shard_map/land/pallas_call | solution.py:1458
